TPU v7x, 256 devices: a whole 4x4x8 slice. The times are simulated.
256 devices in a mesh: seq: 32 (over y, x, core), head: 8 (over z).
Axes of the slice: x: 4, y: 4, z: 8, core: 2. Of those that a mesh axis runs over, the one named last changes fastest.
Arguments:
- queries: bfloat16 [16384, 2048], P('seq', 'head'), may hold values from -60 to 60
- keys: bfloat16 [16384, 2048], P('seq', 'head'), may hold values from -6 to 6
- values: bfloat16 [16384, 2048], P('seq', 'head'), may hold values from -6 to 6
- grad_out: bfloat16 [16384, 2048], P('seq', 'head'), may hold values from -6 to 6
- retrieved: int32 [256, 16], P(('seq', 'head')), may hold values from 0 to 255, as said below
- mem_bias: float32 [16], P('head'), may hold values from -2 to 1
Outputs:
- attended: bfloat16 [16384, 2048], P('seq', 'head')
- grad_queries: bfloat16 [16384, 2048], P('seq', 'head')
- grad_keys: bfloat16 [16384, 2048], P('seq', 'head')
- grad_values: bfloat16 [16384, 2048], P('seq', 'head')
Inputs may be any that keep to these rules, and one draw needn't show every extreme that they name: `retrieved`: each row names 16 different blocks. The 8 rows of one segment name exactly 32 distinct blocks together, at most 2 of them from the blocks of any one segment, and exactly 2 from some segment.
All inputs are finite; a program needn't handle non-finite values.
Results may differ from a plain program's by a relative error of at most 0.0055.
Values may be sent and summed in bfloat16 or wider, within the bound.
No kernel may reach another device: no remote copies, remote signals or barrier semaphores. Data moves between devices by JAX's collectives and lax.ppermute only.
A program may use at most 128 MiB of HBM per device.

v0:
```python
import math

import jax
import jax.numpy as jnp
from jax import lax
from jax.experimental import pallas as pl
from jax.experimental.pallas import tpu as pltpu
from jax.sharding import PartitionSpec as P


BLK = 64
NY, NX, NC = 4, 4, 2
NSEQ = NY * NX * NC
HD = 128
FEAT = 256
SEG = 512
POOL = 32
LOG2E = 1.4426950408889634
SCALE = 1.0 / math.sqrt(HD)
OFFS = (0, 1, -1, 2)
QT = 256
KC = 256
NSPLIT = POOL * BLK // KC
SPC = KC // BLK


def seq_of(y, x, c):
    return (y * NX + x) * NC + c


def shift(value, dy, dx, dc):
    pairs = [
        (seq_of(y, x, c), seq_of((y + dy) % NY, (x + dx) % NX, (c + dc) % NC))
        for y in range(NY)
        for x in range(NX)
        for c in range(NC)
    ]
    return lax.ppermute(value, "seq", pairs)


def dot(a, b, dims):
    return lax.dot_general(a, b, (dims, ((), ())), preferred_element_type=jnp.float32)


NN = ((1,), (0,))
NT = ((1,), (1,))
TN = ((0,), (0,))


def iota(shape, dim):
    return lax.broadcasted_iota(jnp.int32, shape, dim)


def flag(cond):
    return jnp.where(cond, 1.0, 0.0)


def select_kernel(where_ref, tseg_ref, trow_ref, *refs):
    pieces_k, pieces_v = refs[:8], refs[8:16]
    table_ref, mask_ref = refs[16:18]
    outs = refs[18:30]
    prefix_ref, table_smem, table_sem, sems = refs[30:]
    me = where_ref[0]
    nid = NSEQ * 8
    ids = iota((NSEQ, nid), 1)
    flags = ids < 0
    for e in range(128):
        flags = flags | (tseg_ref[:, e : e + 1] == ids)
    wanted = flag(flags)
    row, col = iota((nid, nid), 0), iota((nid, nid), 1)
    upto = flag(row <= col)
    upto8 = flag((row <= col) & ((row >> 3) == (col >> 3)))
    prefix = dot(wanted.astype(jnp.bfloat16), upto.astype(jnp.bfloat16), NN)
    prefix8 = dot(wanted.astype(jnp.bfloat16), upto8.astype(jnp.bfloat16), NN)
    gid, gw = iota((nid, NSEQ), 0), iota((nid, NSEQ), 1)
    same = (gid >> 3) == gw
    ones = flag(same).astype(jnp.bfloat16)
    inner = jnp.where(same, (gid & 7).astype(jnp.float32), 0.0).astype(jnp.bfloat16)
    for r in range(2):
        picked = jnp.where(prefix8 == float(r + 1), wanted, 0.0)
        has = dot(picked.astype(jnp.bfloat16), ones, NN)
        block = dot(picked.astype(jnp.bfloat16), inner, NN)
        place = dot((picked * (prefix - 1.0)).astype(jnp.bfloat16), ones, NN)
        table_ref[r * NSEQ : (r + 1) * NSEQ, :] = jnp.where(has > 0.5, block, -1.0).astype(jnp.int32)
        spare = iota((NSEQ, NSEQ), 1) + POOL + NSEQ * r
        table_ref[(2 + r) * NSEQ : (3 + r) * NSEQ, :] = jnp.where(has > 0.5, place.astype(jnp.int32), spare)
    to_smem = pltpu.make_async_copy(table_ref, table_smem, table_sem)
    to_smem.start()
    prefix_ref[...] = jnp.where(flags, prefix - 1.0, -1.0)
    mine = prefix_ref[pl.ds(me, 1), :]
    compact = flag(iota((POOL, nid), 0).astype(jnp.float32) == mine)
    named = trow_ref[pl.ds(me * 8, 8), :]
    ids8 = iota((8, nid), 1)
    used = ids8 < 0
    for e in range(16):
        used = used | (named[:, e : e + 1] == ids8)
    used = flag(used & (ids8 < me * 8 + iota((8, nid), 0)))
    spread = flag(iota((8, SEG), 0) == (iota((8, SEG), 1) >> 6))
    by_id = dot(used.astype(jnp.bfloat16), spread.astype(jnp.bfloat16), TN)
    mask_ref[...] = dot(compact.astype(jnp.bfloat16), by_id.astype(jnp.bfloat16), NN)
    to_smem.wait()
    y, x, c = me // 8, (me // 2) % 4, me % 2
    for kind, pieces in ((0, pieces_k), (1, pieces_v)):
        for oi, off in enumerate(OFFS[1:]):
            if kind == 0:
                reader = seq_of(y, (x + off + 4) % 4, c)
            else:
                reader = seq_of((y + off + 4) % 4, x, c)
            for j in range(16):
                di, dc, r = j // 4, (j // 2) % 2, j % 2
                d = OFFS[di]
                if kind == 0:
                    writer = seq_of((y + d + 4) % 4, x, (c + dc) % 2)
                else:
                    writer = seq_of(y, (x + d + 4) % 4, (c + dc) % 2)
                block = jnp.maximum(table_smem[r * NSEQ + reader, writer], 0)
                rows = pl.ds(pl.multiple_of(block * BLK, BLK), BLK)
                for h in range(2):
                    i = h * 6 + kind * 3 + oi
                    pltpu.make_async_copy(
                        pieces[di * 2 + dc].at[rows, pl.ds(h * HD, HD)], outs[i].at[j], sems.at[i]
                    ).start()
    for i in range(12):
        pltpu.make_async_copy(outs[i], outs[i], sems.at[i]).wait()


def select(where, tseg, trow, pieces_k, pieces_v):
    spec = lambda space: pl.BlockSpec(memory_space=space)
    return pl.pallas_call(
        select_kernel,
        name="select",
        in_specs=[spec(pltpu.SMEM), spec(pltpu.VMEM), spec(pltpu.VMEM)] + [spec(pl.ANY)] * 16,
        out_specs=[spec(pltpu.VMEM)] * 14,
        out_shape=[
            jax.ShapeDtypeStruct((4 * NSEQ, NSEQ), jnp.int32),
            jax.ShapeDtypeStruct((POOL, SEG), jnp.float32),
        ]
        + [jax.ShapeDtypeStruct((16, BLK, HD), jnp.bfloat16)] * 12,
        scratch_shapes=[
            pltpu.VMEM((NSEQ, NSEQ * 8), jnp.float32),
            pltpu.SMEM((4 * NSEQ, NSEQ), jnp.int32),
            pltpu.SemaphoreType.DMA,
            pltpu.SemaphoreType.DMA((12,)),
        ],
        cost_estimate=pl.CostEstimate(flops=10_000_000, bytes_accessed=8 << 20, transcendentals=0),
    )(where, tseg, trow, *pieces_k, *pieces_v)


def attend_kernel(h, where_ref, table_ref, bias_ref, q_ref, do_ref, k_ref, v_ref, mask_ref, *refs):
    pieces = (refs[:8], refs[8:16])
    srcs = (refs[16:19], refs[19:22])
    refs = refs[22 + 2 * h :]
    att_hbm, gq_hbm, dkl_ref, dvl_ref, back_ref = refs[:5]
    kt, vt, s_ref, dp_ref, add_ref, dka, dva, dkb, dvb, att_ref, gq_ref, sems, out_sem, end_sem = refs[5:]
    me = where_ref[0]
    y, x, c = me // 8, (me // 2) % 4, me % 2
    tiles = (kt, vt)
    hs = slice(h * HD, (h + 1) * HD)
    for kind in range(2):
        for oi, off in enumerate(OFFS):
            for j in range(16):
                di, dc, r = j // 4, (j // 2) % 2, j % 2
                d = OFFS[di]
                if kind == 0:
                    writer = seq_of((y + d + 4) % 4, (x + off + 4) % 4, (c + dc) % 2)
                else:
                    writer = seq_of((y + off + 4) % 4, (x + d + 4) % 4, (c + dc) % 2)
                place = table_ref[(2 + r) * NSEQ + me, writer]
                if oi == 0:
                    block = jnp.maximum(table_ref[r * NSEQ + me, writer], 0)
                    rows = pl.ds(pl.multiple_of(block * BLK, BLK), BLK)
                    src = pieces[kind][di * 2 + dc].at[rows, pl.ds(h * HD, HD)]
                else:
                    src = srcs[kind][oi - 1].at[j]
                pltpu.make_async_copy(
                    src,
                    tiles[kind].at[pl.ds(pl.multiple_of(place * BLK, BLK), BLK), :],
                    sems.at[kind],
                ).start()
    for i in range(NSPLIT):
        add_ref[i] = jnp.where(mask_ref[i * SPC : (i + 1) * SPC, :] > 0.5, bias_ref[h] * LOG2E, -1e30)
    keys = POOL * BLK

    def fold(value, op):
        return op(value.reshape(KC // 8, 8, QT), axis=0)

    for kind in range(2):
        all_slots = tiles[kind].at[pl.ds(0, 2 * NSEQ * BLK), :]
        pltpu.make_async_copy(all_slots, all_slots, sems.at[kind]).wait()

    for t in range(SEG // QT):
        rows = slice(t * QT, (t + 1) * QT)
        qc, doc = q_ref[rows, hs], do_ref[rows, hs]
        local = (t + 1) * QT // KC

        def mem_score(i, top):
            at = pl.ds(pl.multiple_of(i * KC, KC), KC)
            score = dot(kt[at, :], qc, NT) * (SCALE * LOG2E)
            add = add_ref[i, :, rows]
            score = (score.reshape(SPC, BLK, QT) + add[:, None, :]).reshape(KC, QT)
            s_ref[at, :] = score
            return jnp.maximum(top, fold(score, jnp.max))

        top = jnp.full((8, QT), -1e30, jnp.float32)
        for n in range(local):
            score = dot(k_ref[n * KC : (n + 1) * KC, hs], qc, NT) * (SCALE * LOG2E)
            if (n + 1) * KC > t * QT:
                score = jnp.where(iota((KC, QT), 0) + n * KC <= iota((KC, QT), 1) + t * QT, score, -1e30)
            s_ref[keys + n * KC : keys + (n + 1) * KC, :] = score
            top = jnp.maximum(top, fold(score, jnp.max))
        top = lax.fori_loop(0, NSPLIT, mem_score, top)
        top = jnp.max(top, axis=0, keepdims=True)

        def weigh(i, mass):
            at = pl.ds(pl.multiple_of(i * KC, KC), KC)
            e = jnp.exp2(s_ref[at, :] - top)
            s_ref[at, :] = e
            return mass + fold(e, jnp.sum)

        mass = lax.fori_loop(0, NSPLIT + local, weigh, jnp.zeros((8, QT), jnp.float32))
        inv = 1.0 / jnp.sum(mass, axis=0, keepdims=True)

        def forward(at, vc, put, carry):
            out, delta = carry
            p = s_ref[at, :] * inv
            s_ref[at, :] = p
            w = p.astype(jnp.bfloat16)
            out = out + dot(vc, w, TN)
            put(dot(w, doc, NN))
            dp = dot(vc, doc, NT)
            dp_ref[at, :] = dp
            return out, delta + fold(p * dp, jnp.sum)

        def backward(at, kc, put, dq):
            ds = (s_ref[at, :] * (dp_ref[at, :] - delta) * SCALE).astype(jnp.bfloat16)
            put(dot(ds, qc, NN))
            return dq + dot(kc, ds, TN)

        def putter(ref, at):
            def put(value):
                ref[at, :] = value if t == 0 else ref[at, :] + value

            return put

        def local_putter(ref, n):
            at = slice(n * KC, (n + 1) * KC)

            def put(value):
                ref[at, :] = value if n * KC >= t * QT else ref[at, :] + value

            return put

        def mem_forward(i, carry):
            at = pl.ds(pl.multiple_of(i * KC, KC), KC)
            return forward(at, vt[at, :], putter(dva, at), carry)

        def mem_backward(i, dq):
            at = pl.ds(pl.multiple_of(i * KC, KC), KC)
            return backward(at, kt[at, :], putter(dka, at), dq)

        carry = (jnp.zeros((HD, QT), jnp.float32), jnp.zeros((8, QT), jnp.float32))
        carry = lax.fori_loop(0, NSPLIT, mem_forward, carry)
        for n in range(local):
            at = slice(keys + n * KC, keys + (n + 1) * KC)
            carry = forward(at, v_ref[n * KC : (n + 1) * KC, hs], local_putter(dvl_ref, n), carry)
        out, delta = carry
        delta = jnp.sum(delta, axis=0, keepdims=True)
        att_ref[rows, :] = out.T.astype(jnp.bfloat16)
        dq = lax.fori_loop(0, NSPLIT, mem_backward, jnp.zeros((HD, QT), jnp.float32))
        for n in range(local):
            at = slice(keys + n * KC, keys + (n + 1) * KC)
            dq = backward(at, k_ref[n * KC : (n + 1) * KC, hs], local_putter(dkl_ref, n), dq)
        gq_ref[rows, :] = dq.T.astype(jnp.bfloat16)
    ends = [
        pltpu.make_async_copy(src, dst.at[:, pl.ds(h * HD, HD)], end_sem.at[i])
        for i, (src, dst) in enumerate(((att_ref, att_hbm), (gq_ref, gq_hbm)))
    ]
    for copy in ends:
        copy.start()
    dkb[...] = dka[...].astype(jnp.bfloat16)
    dvb[...] = dva[...].astype(jnp.bfloat16)
    for w in range(NSEQ):
        for r in range(2):
            place = jnp.minimum(table_ref[(2 + r) * NSEQ + me, w], POOL - 1)
            for kind, ref in ((0, dkb), (1, dvb)):
                pltpu.make_async_copy(
                    ref.at[pl.ds(pl.multiple_of(place * BLK, BLK), BLK), :],
                    back_ref.at[w, kind * 2 + r],
                    out_sem,
                ).start()
    pltpu.make_async_copy(back_ref, back_ref, out_sem).wait()
    for copy in ends:
        copy.wait()


def attend(h, where, table, bias, q, do, k, v, mask, pieces_k, pieces_v, srcs, done):
    bf, f32, vm, hbm, sm = jnp.bfloat16, jnp.float32, pltpu.VMEM, pl.ANY, pltpu.SMEM
    spec = lambda space: pl.BlockSpec(memory_space=space)
    keys = POOL * BLK
    extra = list(done)
    return pl.pallas_call(
        lambda *refs: attend_kernel(h, *refs),
        in_specs=[spec(sm)] * 3 + [spec(vm)] * 5 + [spec(hbm)] * (22 + len(extra)),
        out_specs=[spec(hbm)] * 2 + [spec(vm)] * 2 + [spec(hbm)],
        out_shape=[
            jax.ShapeDtypeStruct((SEG, FEAT), bf),
            jax.ShapeDtypeStruct((SEG, FEAT), bf),
            jax.ShapeDtypeStruct((SEG, HD), f32),
            jax.ShapeDtypeStruct((SEG, HD), f32),
            jax.ShapeDtypeStruct((NSEQ, 4, BLK, HD), bf),
        ],
        scratch_shapes=[
            pltpu.VMEM((96 * BLK, HD), bf),
            pltpu.VMEM((96 * BLK, HD), bf),
            pltpu.VMEM((keys + SEG, QT), f32),
            pltpu.VMEM((keys + SEG, QT), f32),
            pltpu.VMEM((NSPLIT, SPC, SEG), f32),
            pltpu.VMEM((keys, HD), f32),
            pltpu.VMEM((keys, HD), f32),
            pltpu.VMEM((keys, HD), bf),
            pltpu.VMEM((keys, HD), bf),
            pltpu.VMEM((SEG, HD), bf),
            pltpu.VMEM((SEG, HD), bf),
            pltpu.SemaphoreType.DMA((2,)),
            pltpu.SemaphoreType.DMA,
            pltpu.SemaphoreType.DMA((2,)),
        ],
        input_output_aliases={30: 0, 31: 1} if extra else {},
        cost_estimate=pl.CostEstimate(flops=16_000_000_000, bytes_accessed=8 << 20, transcendentals=1_500_000),
    )(where, table, bias, q, do, k, v, mask, *pieces_k, *pieces_v, *srcs, *extra)


def settle_kernel(h, where_ref, table_ref, dkl_ref, dvl_ref, back_ref, *refs):
    gk_hbm, gv_hbm, dk, dv, dkb, dvb, sems = refs[2 * h :]
    me = where_ref[0]
    dk[...] = dkl_ref[...]
    dv[...] = dvl_ref[...]

    def step(s, _):
        for r in range(2):
            block = table_ref[r * NSEQ + s, me]

            @pl.when(block >= 0)
            def _():
                at = pl.ds(pl.multiple_of(block * BLK, BLK), BLK)
                dk[at, :] += back_ref[s, r].astype(jnp.float32)
                dv[at, :] += back_ref[s, 2 + r].astype(jnp.float32)

        return 0

    lax.fori_loop(0, NSEQ, step, 0)
    dkb[...] = dk[...].astype(jnp.bfloat16)
    dvb[...] = dv[...].astype(jnp.bfloat16)
    ends = [
        pltpu.make_async_copy(src, dst.at[:, pl.ds(h * HD, HD)], sems.at[i])
        for i, (src, dst) in enumerate(((dkb, gk_hbm), (dvb, gv_hbm)))
    ]
    for copy in ends:
        copy.start()
    for copy in ends:
        copy.wait()


def settle(h, where, table, dkl, dvl, back, done):
    spec = lambda space: pl.BlockSpec(memory_space=space)
    extra = list(done)
    return pl.pallas_call(
        lambda *refs: settle_kernel(h, *refs),
        in_specs=[spec(pltpu.SMEM)] * 2 + [spec(pltpu.VMEM)] * 3 + [spec(pl.ANY)] * len(extra),
        out_specs=[spec(pl.ANY)] * 2,
        out_shape=[jax.ShapeDtypeStruct((SEG, FEAT), jnp.bfloat16)] * 2,
        scratch_shapes=[pltpu.VMEM((SEG, HD), jnp.float32)] * 2
        + [pltpu.VMEM((SEG, HD), jnp.bfloat16)] * 2
        + [pltpu.SemaphoreType.DMA((2,))],
        input_output_aliases={5: 0, 6: 1} if extra else {},
        cost_estimate=pl.CostEstimate(flops=2_000_000, bytes_accessed=3 << 20, transcendentals=0),
    )(where, table, dkl, dvl, back, *extra)


def layer(queries, keys, values, grad_out, retrieved, mem_bias):
    where = lax.axis_index("seq").astype(jnp.int32).reshape(1)
    devices = lax.axis_size("seq") * lax.axis_size("head")
    copies = jnp.broadcast_to(retrieved, (devices, *retrieved.shape))
    lists = lax.all_to_all(copies, ("seq", "head"), split_axis=0, concat_axis=0, tiled=True)
    trow = lists.reshape(devices, 16)
    tseg = lists.reshape(NSEQ, 128)
    col_k = [keys] + [shift(keys, -d, 0, 0) for d in OFFS[1:]]
    row_v = [values] + [shift(values, 0, -d, 0) for d in OFFS[1:]]
    pieces_k = [p for piece in col_k for p in (piece, shift(piece, 0, 0, 1))]
    pieces_v = [p for piece in row_v for p in (piece, shift(piece, 0, 0, 1))]
    table, mask, *msgs = select(where, tseg, trow, pieces_k, pieces_v)
    near_k, near_v = shift(msgs[8], 0, -1, 0), shift(msgs[11], -1, 0, 0)
    fetched = []
    for h in range(2):
        kp, km, k2, vp, vm, v2 = msgs[h * 6 : h * 6 + 6]
        if h == 0:
            far_k, far_v = shift(k2, 0, 2, 0), shift(v2, 2, 0, 0)
        else:
            far_k, far_v = shift(near_k, 0, -1, 0), shift(near_v, -1, 0, 0)
        fetched.append(
            [
                shift(km, 0, -1, 0),
                shift(kp, 0, 1, 0),
                far_k,
                shift(vm, -1, 0, 0),
                shift(vp, 1, 0, 0),
                far_v,
            ]
        )
    rows, grads = (), ()
    parts = []
    for h in range(2):
        *rows, dkl, dvl, back = attend(
            h, where, table, mem_bias, queries, grad_out, keys, values, mask, pieces_k, pieces_v, fetched[h], rows
        )
        back = lax.all_to_all(back, "seq", split_axis=0, concat_axis=0, tiled=True)
        parts.append((dkl, dvl, back))
    for h in range(2):
        grads = settle(h, where, table, *parts[h], grads)
    return *rows, *grads


def solution(mesh):
    whole = P("seq", "head")
    return jax.shard_map(
        layer,
        mesh=mesh,
        in_specs=(whole, whole, whole, whole, P(("seq", "head"), None), P("head")),
        out_specs=(whole, whole, whole, whole),
        check_vma=False,
    )
```

profile of v0, /device:TPU:1, one launch (start us, length us, event | category | flops | bytes accessed | tf_op | source)
XLA Modules:
  0.0 210.4 jit_solution(17301462353459766293)
XLA Ops:
  0.6 2.1 %collective-permute-start.10 = (bf16[512,256]{1,0:T(8,128)(2,1)}, bf16[512,256]{1,0:T(8,128)(2,1)S(1)}, u32[]{:S(2)}, u32[]{:S(2)}) collective-permute-start(bf16[512,256]{1,0:T(8,128)(2,1)} %refs_16_.3), channel_id=1, source_target_pairs={{0,16},{8,24},{16,32},{24,40},{32,48},{40,56},{48,0},{56,8},{64,80... | collective-permute-start | bytes 786440 | tf_op jit(solution)/shard_map/ppermute | solution.py:38
  2.7 2.5 %collective-permute-start.12 = (bf16[512,256]{1,0:T(8,128)(2,1)}, bf16[512,256]{1,0:T(8,128)(2,1)S(1)}, u32[]{:S(2)}, u32[]{:S(2)}) collective-permute-start(bf16[512,256]{1,0:T(8,128)(2,1)} %refs_16_.3), channel_id=1, source_target_pairs={{0,32},{8,40},{16,48},{24,56},{32,0},{40,8},{48,16},{56,24},{64,96... | collective-permute-start | bytes 786440 | tf_op jit(solution)/shard_map/ppermute | solution.py:38
  5.2 2.7 %collective-permute-start.1 = (bf16[512,256]{1,0:T(8,128)(2,1)}, bf16[512,256]{1,0:T(8,128)(2,1)S(1)}, u32[]{:S(2)}, u32[]{:S(2)}) collective-permute-start(bf16[512,256]{1,0:T(8,128)(2,1)} %refs_8_.5), channel_id=1, source_target_pairs={{0,192},{8,200},{16,208},{24,216},{32,224},{40,232},{48,240},{56,2... | collective-permute-start | bytes 786440 | tf_op jit(solution)/shard_map/ppermute | solution.py:38
  7.9 1.6 collective-permute-start.5
  9.6 1.8 collective-permute-start.8
  11.4 5.3 %collective-permute-done.12.refs_14_.refs_22_ = bf16[512,256]{1,0:T(8,128)(2,1)S(1)} collective-permute-done((bf16[512,256]{1,0:T(8,128)(2,1)}, bf16[512,256]{1,0:T(8,128)(2,1)S(1)}, u32[]{:S(2)}, u32[]{:S(2)}) %collective-permute-start.12) | collective-permute-done | bytes 262176 | tf_op jit(solution)/shard_map/ppermute | solution.py:38
  16.7 1.5 collective-permute-start
  18.3 2.1 collective-permute-start.7
  20.4 3.3 %collective-permute-start.11 = (bf16[512,256]{1,0:T(8,128)(2,1)S(1)}, bf16[512,256]{1,0:T(8,128)(2,1)S(1)}, u32[]{:S(2)}, u32[]{:S(2)}) collective-permute-start(bf16[512,256]{1,0:T(8,128)(2,1)S(1)} %collective-permute-done.10.refs_12_.refs_20_), channel_id=1, source_target_pairs={{0,8},{8,0},{16,24},{24,16},{32,40},{40,32},{48,56},{56,48},{64,72... | collective-permute-start | bytes 786440 | tf_op jit(solution)/shard_map/ppermute | solution.py:38
  25.2 1.4 broadcast_in_dim.3
  26.6 10.4 %all-to-all-start = ((s32[256,1,16]{2,1,0:T(1,128)}), s32[256,1,16]{2,1,0:T(1,128)S(1)}, u32[]{:S(2)}, u32[]{:S(2)}) async-start(s32[256,1,16]{2,1,0:T(1,128)} %broadcast_in_dim.3), calls=%async_computation | async-start | bytes 262144 | tf_op jit(solution)/shard_map/all_to_all | solution.py:384
  37.0 13.0 %all-to-all-done = s32[256,1,16]{2,1,0:T(1,128)S(1)} async-done(((s32[256,1,16]{2,1,0:T(1,128)}), s32[256,1,16]{2,1,0:T(1,128)S(1)}, u32[]{:S(2)}, u32[]{:S(2)}) %all-to-all-start) | async-done | bytes 16416 | tf_op jit(solution)/shard_map/all_to_all | solution.py:384
  53.1 7.7 %select.1 = (s32[128,32]{1,0:T(8,128)}, f32[32,512]{1,0:T(8,128)}, bf16[16,64,128]{2,1,0:T(8,128)(2,1)}, bf16[16,64,128]{2,1,0:T(8,128)(2,1)}, bf16[16,64,128]{2...) custom-call(s32[1]{0:T(128)} %bitcast.where_ref.refs_0_, ...), custom_call_target="tpu_custom_call" | custom-call | flops 10000000 | bytes 8388608 | tf_op jit(solution)/shard_map/select/pallas_call | solution.py:129
  64.8 3.4 %collective-permute-done.22.refs_24_ = bf16[16,64,128]{2,1,0:T(8,128)(2,1)S(1)} collective-permute-done((bf16[16,64,128]{2,1,0:T(8,128)(2,1)}, bf16[16,64,128]{2,1,0:T(8,128)(2,1)S(1)}, u32[]{:S(2)}, u32[]{:S(2)}) %collective-permute-start.22) | collective-permute-done | bytes 262176 | tf_op jit(solution)/shard_map/ppermute | solution.py:38
  68.2 1.2 collective-permute-start.27
  69.4 6.8 %collective-permute-done.23.refs_25_ = bf16[16,64,128]{2,1,0:T(8,128)(2,1)S(1)} collective-permute-done((bf16[16,64,128]{2,1,0:T(8,128)(2,1)}, bf16[16,64,128]{2,1,0:T(8,128)(2,1)S(1)}, u32[]{:S(2)}, u32[]{:S(2)}) %collective-permute-start.23) | collective-permute-done | bytes 262176 | tf_op jit(solution)/shard_map/ppermute | solution.py:38
  77.3 18.9 %shard_map.96 = (bf16[512,256]{1,0:T(8,128)(2,1)}, bf16[512,256]{1,0:T(8,128)(2,1)}, f32[512,128]{1,0:T(8,128)}, f32[512,128]{1,0:T(8,128)}, bf16[32,4,64,128]{3,2,1,0:T(8,128)(2,1)}) custom-call(s32[1]{0:T(128)} %bitcast.where_ref.refs_0_, s32[128,32]{1,0:T(8,128)} %get-tuple-element.32.refs_1_, f32[2]{0:T(128)} %refs_2_.3, bf16[512,256]{1,0:T(8,128)(2,1)} %refs_3_.3, ...), custom_call_target="tpu_custom_call" | custom-call | flops 16000000000 | bytes 8388608 | tf_op jit(solution)/shard_map/pallas_call | solution.py:301
  96.2 7.8 %all-to-all-start.2 = ((bf16[32,4,64,128]{3,2,1,0:T(8,128)(2,1)}), bf16[32,4,64,128]{3,2,1,0:T(8,128)(2,1)S(1)}, u32[]{:S(2)}, u32[]{:S(2)}) async-start(bf16[32,4,64,128]{3,2,1,0:T(8,128)(2,1)} %get-tuple-element.55), calls=%async_computation.2 | async-start | bytes 4194304 | tf_op jit(solution)/shard_map/all_to_all | solution.py:416
  104.0 2.6 %collective-permute-start.16 = (bf16[16,64,128]{2,1,0:T(8,128)(2,1)}, bf16[16,64,128]{2,1,0:T(8,128)(2,1)S(1)}, u32[]{:S(2)}, u32[]{:S(2)}) collective-permute-start(bf16[16,64,128]{2,1,0:T(8,128)(2,1)} %get-tuple-element.36), channel_id=1, source_target_pairs={{0,48},{8,56},{16,0},{24,8},{32,16},{40,24},{48,32},{56,40},{64,11... | collective-permute-start | bytes 786440 | tf_op jit(solution)/shard_map/ppermute | solution.py:38
  106.7 2.5 %collective-permute-start.20 = (bf16[16,64,128]{2,1,0:T(8,128)(2,1)S(1)}, bf16[16,64,128]{2,1,0:T(8,128)(2,1)S(1)}, u32[]{:S(2)}, u32[]{:S(2)}) collective-permute-start(bf16[16,64,128]{2,1,0:T(8,128)(2,1)S(1)} %copy-done.18), channel_id=1, source_target_pairs={{0,192},{8,200},{16,208},{24,216},{32,224},{40,232},{48,240},{56,2... | collective-permute-start | bytes 786440 | tf_op jit(solution)/shard_map/ppermute | solution.py:38
  111.2 23.5 %collective-permute-done.16 = bf16[16,64,128]{2,1,0:T(8,128)(2,1)S(1)} collective-permute-done((bf16[16,64,128]{2,1,0:T(8,128)(2,1)}, bf16[16,64,128]{2,1,0:T(8,128)(2,1)S(1)}, u32[]{:S(2)}, u32[]{:S(2)}) %collective-permute-start.16) | collective-permute-done | bytes 262176 | tf_op jit(solution)/shard_map/ppermute | solution.py:38
  134.7 2.0 collective-permute-start.19
  137.6 2.6 %collective-permute-done.14.refs_24_ = bf16[16,64,128]{2,1,0:T(8,128)(2,1)S(1)} collective-permute-done((bf16[16,64,128]{2,1,0:T(8,128)(2,1)S(1)}, bf16[16,64,128]{2,1,0:T(8,128)(2,1)S(1)}, u32[]{:S(2)}, u32[]{:S(2)}) %collective-permute-start.14) | collective-permute-done | bytes 262176 | tf_op jit(solution)/shard_map/ppermute | solution.py:38
  140.3 3.2 %collective-permute-start.21 = (bf16[16,64,128]{2,1,0:T(8,128)(2,1)S(1)}, bf16[16,64,128]{2,1,0:T(8,128)(2,1)S(1)}, u32[]{:S(2)}, u32[]{:S(2)}) collective-permute-start(bf16[16,64,128]{2,1,0:T(8,128)(2,1)S(1)} %collective-permute-done.20), channel_id=1, source_target_pairs={{0,192},{8,200},{16,208},{24,216},{32,224},{40,232},{48,240},{56,2... | collective-permute-start | bytes 786440 | tf_op jit(solution)/shard_map/ppermute | solution.py:38
  143.5 2.2 %collective-permute-done.17.refs_26_ = bf16[16,64,128]{2,1,0:T(8,128)(2,1)S(1)} collective-permute-done((bf16[16,64,128]{2,1,0:T(8,128)(2,1)S(1)}, bf16[16,64,128]{2,1,0:T(8,128)(2,1)S(1)}, u32[]{:S(2)}, u32[]{:S(2)}) %collective-permute-start.17) | collective-permute-done | bytes 262176 | tf_op jit(solution)/shard_map/ppermute | solution.py:38
  145.7 1.9 collective-permute-done.21.refs_29_
  148.3 18.9 %shard_map.97 = (bf16[512,256]{1,0:T(8,128)(2,1)}, bf16[512,256]{1,0:T(8,128)(2,1)}, f32[512,128]{1,0:T(8,128)}, f32[512,128]{1,0:T(8,128)}, bf16[32,4,64,128]{3,2,1,0:T(8,128)(2,1)}) custom-call(s32[1]{0:T(128)} %bitcast.where_ref.refs_0_, s32[128,32]{1,0:T(8,128)} %get-tuple-element.32.refs_1_, ...), custom_call_target="tpu_custom_call", output_to_operand_aliasing={{0}: (30, {}), {1}: (31, {})} | custom-call | flops 16000000000 | bytes 8388608 | tf_op jit(solution)/shard_map/pallas_call | solution.py:301
  167.2 1.3 copy-done
  168.6 9.3 %all-to-all-start.1 = ((bf16[32,4,64,128]{3,2,1,0:T(8,128)(2,1)}), bf16[32,4,64,128]{3,2,1,0:T(8,128)(2,1)}, u32[]{:S(2)}, u32[]{:S(2)}) async-start(bf16[32,4,64,128]{3,2,1,0:T(8,128)(2,1)} %get-tuple-element.52), calls=%async_computation.1 | async-start | bytes 4194304 | tf_op jit(solution)/shard_map/all_to_all | solution.py:416
  177.9 3.6 %shard_map.98 = (bf16[512,256]{1,0:T(8,128)(2,1)}, bf16[512,256]{1,0:T(8,128)(2,1)}) custom-call(s32[1]{0:T(128)} %bitcast.where_ref.refs_0_, s32[128,32]{1,0:T(8,128)} %get-tuple-element.32.refs_1_, f32[512,128]{1,0:T(8,128)} %get-tuple-element.53.refs_2_, f32[512,128]{1,0:T(8,128)} %get-tuple-element.54.refs_3_, bf16[32,4,64,128]{3,2,1,0:T(8,128)(2,1)} %copy-done), custom_call_target="tpu_custom_call" | custom-call | flops 2000000 | bytes 3145728 | tf_op jit(solution)/shard_map/pallas_call | solution.py:367
  181.5 25.1 %all-to-all-done.1.refs_4_ = bf16[32,4,64,128]{3,2,1,0:T(8,128)(2,1)} async-done(((bf16[32,4,64,128]{3,2,1,0:T(8,128)(2,1)}), bf16[32,4,64,128]{3,2,1,0:T(8,128)(2,1)}, u32[]{:S(2)}, u32[]{:S(2)}) %all-to-all-start.1) | async-done | bytes 2097184 | tf_op jit(solution)/shard_map/all_to_all | solution.py:416
  206.6 3.6 %shard_map.99 = (bf16[512,256]{1,0:T(8,128)(2,1)}, bf16[512,256]{1,0:T(8,128)(2,1)}) custom-call(s32[1]{0:T(128)} %bitcast.where_ref.refs_0_, s32[128,32]{1,0:T(8,128)} %get-tuple-element.32.refs_1_, f32[512,128]{1,0:T(8,128)} %get-tuple-element.50.refs_2_, f32[512,128]{1,0:T(8,128)} %get-tuple-element.51.refs_3_, ...), custom_call_target="tpu_custom_call", output_to_operand_aliasing={{0}: (5, {}), {1}: (6, {})} | custom-call | flops 2000000 | bytes 3145728 | tf_op jit(solution)/shard_map/pallas_call | solution.py:367
  (101 shorter events, 13.4 us)
Async XLA Ops:
  0.6 8.9 %collective-permute-start.10 = (bf16[512,256]{1,0:T(8,128)(2,1)}, bf16[512,256]{1,0:T(8,128)(2,1)S(1)}, u32[]{:S(2)}, u32[]{:S(2)}) collective-permute-start(bf16[512,256]{1,0:T(8,128)(2,1)} %refs_16_.3), channel_id=1, source_target_pairs={{0,16},{8,24},{16,32},{24,40},{32,48},{40,56},{48,0},{56,8},{64,80... | collective-permute-start | bytes 786440 | tf_op jit(solution)/shard_map/ppermute | solution.py:38
  2.7 14.0 %collective-permute-start.12 = (bf16[512,256]{1,0:T(8,128)(2,1)}, bf16[512,256]{1,0:T(8,128)(2,1)S(1)}, u32[]{:S(2)}, u32[]{:S(2)}) collective-permute-start(bf16[512,256]{1,0:T(8,128)(2,1)} %refs_16_.3), channel_id=1, source_target_pairs={{0,32},{8,40},{16,48},{24,56},{32,0},{40,8},{48,16},{56,24},{64,96... | collective-permute-start | bytes 786440 | tf_op jit(solution)/shard_map/ppermute | solution.py:38
  5.2 13.1 %collective-permute-start.1 = (bf16[512,256]{1,0:T(8,128)(2,1)}, bf16[512,256]{1,0:T(8,128)(2,1)S(1)}, u32[]{:S(2)}, u32[]{:S(2)}) collective-permute-start(bf16[512,256]{1,0:T(8,128)(2,1)} %refs_8_.5), channel_id=1, source_target_pairs={{0,192},{8,200},{16,208},{24,216},{32,224},{40,232},{48,240},{56,2... | collective-permute-start | bytes 786440 | tf_op jit(solution)/shard_map/ppermute | solution.py:38
  7.9 12.5 %collective-permute-start.3 = (bf16[512,256]{1,0:T(8,128)(2,1)}, bf16[512,256]{1,0:T(8,128)(2,1)S(1)}, u32[]{:S(2)}, u32[]{:S(2)}) collective-permute-start(bf16[512,256]{1,0:T(8,128)(2,1)} %refs_8_.5), channel_id=1, source_target_pairs={{0,64},{8,72},{16,80},{24,88},{32,96},{40,104},{48,112},{56,120},{... | collective-permute-start | bytes 786440 | tf_op jit(solution)/shard_map/ppermute | solution.py:38
  7.9 15.8 %collective-permute-start.5 = (bf16[512,256]{1,0:T(8,128)(2,1)}, bf16[512,256]{1,0:T(8,128)(2,1)S(1)}, u32[]{:S(2)}, u32[]{:S(2)}) collective-permute-start(bf16[512,256]{1,0:T(8,128)(2,1)} %refs_8_.5), channel_id=1, source_target_pairs={{0,128},{8,136},{16,144},{24,152},{32,160},{40,168},{48,176},{56,1... | collective-permute-start | bytes 786440 | tf_op jit(solution)/shard_map/ppermute | solution.py:38
  9.6 42.6 %copy-start.2 = (bf16[512,256]{1,0:T(8,128)(2,1)}, bf16[512,256]{1,0:T(8,128)(2,1)S(1)}, u32[]{:S(2)}) copy-start(bf16[512,256]{1,0:T(8,128)(2,1)S(1)} %collective-permute-done.10.refs_12_.refs_20_) | copy-start | bytes 786436
  9.6 14.2 %collective-permute-start.8 = (bf16[512,256]{1,0:T(8,128)(2,1)}, bf16[512,256]{1,0:T(8,128)(2,1)S(1)}, u32[]{:S(2)}, u32[]{:S(2)}) collective-permute-start(bf16[512,256]{1,0:T(8,128)(2,1)} %refs_16_.3), channel_id=1, source_target_pairs={{0,48},{8,56},{16,0},{24,8},{32,16},{40,24},{48,32},{56,40},{64,11... | collective-permute-start | bytes 786440 | tf_op jit(solution)/shard_map/ppermute | solution.py:38
  16.7 7.5 %collective-permute-start = (bf16[512,256]{1,0:T(8,128)(2,1)}, bf16[512,256]{1,0:T(8,128)(2,1)S(1)}, u32[]{:S(2)}, u32[]{:S(2)}) collective-permute-start(bf16[512,256]{1,0:T(8,128)(2,1)} %refs_8_.5), channel_id=1, source_target_pairs={{0,8},{8,0},{16,24},{24,16},{32,40},{40,32},{48,56},{56,48},{64,72... | collective-permute-start | bytes 786440 | tf_op jit(solution)/shard_map/ppermute | solution.py:38
  18.3 6.0 %collective-permute-start.7 = (bf16[512,256]{1,0:T(8,128)(2,1)}, bf16[512,256]{1,0:T(8,128)(2,1)S(1)}, u32[]{:S(2)}, u32[]{:S(2)}) collective-permute-start(bf16[512,256]{1,0:T(8,128)(2,1)} %refs_16_.3), channel_id=1, source_target_pairs={{0,8},{8,0},{16,24},{24,16},{32,40},{40,32},{48,56},{56,48},{64,72... | collective-permute-start | bytes 786440 | tf_op jit(solution)/shard_map/ppermute | solution.py:38
  20.4 4.5 %collective-permute-start.11 = (bf16[512,256]{1,0:T(8,128)(2,1)S(1)}, bf16[512,256]{1,0:T(8,128)(2,1)S(1)}, u32[]{:S(2)}, u32[]{:S(2)}) collective-permute-start(bf16[512,256]{1,0:T(8,128)(2,1)S(1)} %collective-permute-done.10.refs_12_.refs_20_), channel_id=1, source_target_pairs={{0,8},{8,0},{16,24},{24,16},{32,40},{40,32},{48,56},{56,48},{64,72... | collective-permute-start | bytes 786440 | tf_op jit(solution)/shard_map/ppermute | solution.py:38
  23.7 28.5 %collective-permute-start.13 = (bf16[512,256]{1,0:T(8,128)(2,1)S(1)}, bf16[512,256]{1,0:T(8,128)(2,1)S(1)}, u32[]{:S(2)}, u32[]{:S(2)}) collective-permute-start(bf16[512,256]{1,0:T(8,128)(2,1)S(1)} %collective-permute-done.12.refs_14_.refs_22_), channel_id=1, source_target_pairs={{0,8},{8,0},{16,24},{24,16},{32,40},{40,32},{48,56},{56,48},{64,72... | collective-permute-start | bytes 786440 | tf_op jit(solution)/shard_map/ppermute | solution.py:38
  23.8 28.4 %collective-permute-start.2 = (bf16[512,256]{1,0:T(8,128)(2,1)S(1)}, bf16[512,256]{1,0:T(8,128)(2,1)S(1)}, u32[]{:S(2)}, u32[]{:S(2)}) collective-permute-start(bf16[512,256]{1,0:T(8,128)(2,1)S(1)} %collective-permute-done.1.refs_2_.refs_10_), channel_id=1, source_target_pairs={{0,8},{8,0},{16,24},{24,16},{32,40},{40,32},{48,56},{56,48},{64,72... | collective-permute-start | bytes 786440 | tf_op jit(solution)/shard_map/ppermute | solution.py:38
  24.2 28.0 %collective-permute-start.4 = (bf16[512,256]{1,0:T(8,128)(2,1)S(1)}, bf16[512,256]{1,0:T(8,128)(2,1)S(1)}, u32[]{:S(2)}, u32[]{:S(2)}) collective-permute-start(bf16[512,256]{1,0:T(8,128)(2,1)S(1)} %collective-permute-done.3.refs_4_.refs_12_), channel_id=1, source_target_pairs={{0,8},{8,0},{16,24},{24,16},{32,40},{40,32},{48,56},{56,48},{64,72... | collective-permute-start | bytes 786440 | tf_op jit(solution)/shard_map/ppermute | solution.py:38
  24.3 27.9 %collective-permute-start.6 = (bf16[512,256]{1,0:T(8,128)(2,1)S(1)}, bf16[512,256]{1,0:T(8,128)(2,1)}, u32[]{:S(2)}, u32[]{:S(2)}) collective-permute-start(bf16[512,256]{1,0:T(8,128)(2,1)S(1)} %collective-permute-done.5.refs_6_.refs_14_), channel_id=1, source_target_pairs={{0,8},{8,0},{16,24},{24,16},{32,40},{40,32},{48,56},{56,48},{64,72... | collective-permute-start | bytes 786440 | tf_op jit(solution)/shard_map/ppermute | solution.py:38
  24.9 27.4 %collective-permute-start.9 = (bf16[512,256]{1,0:T(8,128)(2,1)S(1)}, bf16[512,256]{1,0:T(8,128)(2,1)}, u32[]{:S(2)}, u32[]{:S(2)}) collective-permute-start(bf16[512,256]{1,0:T(8,128)(2,1)S(1)} %collective-permute-done.8.refs_10_.refs_18_), channel_id=1, source_target_pairs={{0,8},{8,0},{16,24},{24,16},{32,40},{40,32},{48,56},{56,48},{64,72... | collective-permute-start | bytes 786440 | tf_op jit(solution)/shard_map/ppermute | solution.py:38
  26.6 23.3 %all-to-all-start = ((s32[256,1,16]{2,1,0:T(1,128)}), s32[256,1,16]{2,1,0:T(1,128)S(1)}, u32[]{:S(2)}, u32[]{:S(2)}) async-start(s32[256,1,16]{2,1,0:T(1,128)} %broadcast_in_dim.3), calls=%async_computation | async-start | bytes 262144 | tf_op jit(solution)/shard_map/all_to_all | solution.py:384
  60.7 7.4 %collective-permute-start.22 = (bf16[16,64,128]{2,1,0:T(8,128)(2,1)}, bf16[16,64,128]{2,1,0:T(8,128)(2,1)S(1)}, u32[]{:S(2)}, u32[]{:S(2)}) collective-permute-start(bf16[16,64,128]{2,1,0:T(8,128)(2,1)} %get-tuple-element.40), channel_id=1, source_target_pairs={{0,48},{8,56},{16,0},{24,8},{32,16},{40,24},{48,32},{56,40},{64,11... | collective-permute-start | bytes 786440 | tf_op jit(solution)/shard_map/ppermute | solution.py:38
  61.7 14.4 %collective-permute-start.23 = (bf16[16,64,128]{2,1,0:T(8,128)(2,1)}, bf16[16,64,128]{2,1,0:T(8,128)(2,1)S(1)}, u32[]{:S(2)}, u32[]{:S(2)}) collective-permute-start(bf16[16,64,128]{2,1,0:T(8,128)(2,1)} %get-tuple-element.41), channel_id=1, source_target_pairs={{0,16},{8,24},{16,32},{24,40},{32,48},{40,56},{48,0},{56,8},{64,80... | collective-permute-start | bytes 786440 | tf_op jit(solution)/shard_map/ppermute | solution.py:38
  62.3 13.9 %collective-permute-start.24 = (bf16[16,64,128]{2,1,0:T(8,128)(2,1)}, bf16[16,64,128]{2,1,0:T(8,128)(2,1)S(1)}, u32[]{:S(2)}, u32[]{:S(2)}) collective-permute-start(bf16[16,64,128]{2,1,0:T(8,128)(2,1)} %get-tuple-element.42), channel_id=1, source_target_pairs={{0,32},{8,40},{16,48},{24,56},{32,0},{40,8},{48,16},{56,24},{64,96... | collective-permute-start | bytes 786440 | tf_op jit(solution)/shard_map/ppermute | solution.py:38
  63.3 12.8 %collective-permute-start.25 = (bf16[16,64,128]{2,1,0:T(8,128)(2,1)}, bf16[16,64,128]{2,1,0:T(8,128)(2,1)S(1)}, u32[]{:S(2)}, u32[]{:S(2)}) collective-permute-start(bf16[16,64,128]{2,1,0:T(8,128)(2,1)} %get-tuple-element.43), channel_id=1, source_target_pairs={{0,192},{8,200},{16,208},{24,216},{32,224},{40,232},{48,240},{56,2... | collective-permute-start | bytes 786440 | tf_op jit(solution)/shard_map/ppermute | solution.py:38
  64.2 12.0 %collective-permute-start.26 = (bf16[16,64,128]{2,1,0:T(8,128)(2,1)}, bf16[16,64,128]{2,1,0:T(8,128)(2,1)S(1)}, u32[]{:S(2)}, u32[]{:S(2)}) collective-permute-start(bf16[16,64,128]{2,1,0:T(8,128)(2,1)} %get-tuple-element.44), channel_id=1, source_target_pairs={{0,64},{8,72},{16,80},{24,88},{32,96},{40,104},{48,112},{56,120},{... | collective-permute-start | bytes 786440 | tf_op jit(solution)/shard_map/ppermute | solution.py:38
  68.2 8.0 %collective-permute-start.27 = (bf16[16,64,128]{2,1,0:T(8,128)(2,1)}, bf16[16,64,128]{2,1,0:T(8,128)(2,1)S(1)}, u32[]{:S(2)}, u32[]{:S(2)}) collective-permute-start(bf16[16,64,128]{2,1,0:T(8,128)(2,1)} %get-tuple-element.45), channel_id=1, source_target_pairs={{0,128},{8,136},{16,144},{24,152},{32,160},{40,168},{48,176},{56,1... | collective-permute-start | bytes 786440 | tf_op jit(solution)/shard_map/ppermute | solution.py:38
  96.2 71.0 %all-to-all-start.2 = ((bf16[32,4,64,128]{3,2,1,0:T(8,128)(2,1)}), bf16[32,4,64,128]{3,2,1,0:T(8,128)(2,1)S(1)}, u32[]{:S(2)}, u32[]{:S(2)}) async-start(bf16[32,4,64,128]{3,2,1,0:T(8,128)(2,1)} %get-tuple-element.55), calls=%async_computation.2 | async-start | bytes 4194304 | tf_op jit(solution)/shard_map/all_to_all | solution.py:416
  104.0 30.6 %collective-permute-start.16 = (bf16[16,64,128]{2,1,0:T(8,128)(2,1)}, bf16[16,64,128]{2,1,0:T(8,128)(2,1)S(1)}, u32[]{:S(2)}, u32[]{:S(2)}) collective-permute-start(bf16[16,64,128]{2,1,0:T(8,128)(2,1)} %get-tuple-element.36), channel_id=1, source_target_pairs={{0,48},{8,56},{16,0},{24,8},{32,16},{40,24},{48,32},{56,40},{64,11... | collective-permute-start | bytes 786440 | tf_op jit(solution)/shard_map/ppermute | solution.py:38
  106.7 30.0 %collective-permute-start.20 = (bf16[16,64,128]{2,1,0:T(8,128)(2,1)S(1)}, bf16[16,64,128]{2,1,0:T(8,128)(2,1)S(1)}, u32[]{:S(2)}, u32[]{:S(2)}) collective-permute-start(bf16[16,64,128]{2,1,0:T(8,128)(2,1)S(1)} %copy-done.18), channel_id=1, source_target_pairs={{0,192},{8,200},{16,208},{24,216},{32,224},{40,232},{48,240},{56,2... | collective-permute-start | bytes 786440 | tf_op jit(solution)/shard_map/ppermute | solution.py:38
  109.2 31.1 %collective-permute-start.14 = (bf16[16,64,128]{2,1,0:T(8,128)(2,1)S(1)}, bf16[16,64,128]{2,1,0:T(8,128)(2,1)S(1)}, u32[]{:S(2)}, u32[]{:S(2)}) collective-permute-start(bf16[16,64,128]{2,1,0:T(8,128)(2,1)S(1)} %copy-done.17), channel_id=1, source_target_pairs={{0,48},{8,56},{16,0},{24,8},{32,16},{40,24},{48,32},{56,40},{64,11... | collective-permute-start | bytes 786440 | tf_op jit(solution)/shard_map/ppermute | solution.py:38
  109.7 33.7 %collective-permute-start.15 = (bf16[16,64,128]{2,1,0:T(8,128)(2,1)S(1)}, bf16[16,64,128]{2,1,0:T(8,128)(2,1)S(1)}, u32[]{:S(2)}, u32[]{:S(2)}) collective-permute-start(bf16[16,64,128]{2,1,0:T(8,128)(2,1)S(1)} %copy-done.16), channel_id=1, source_target_pairs={{0,16},{8,24},{16,32},{24,40},{32,48},{40,56},{48,0},{56,8},{64,80... | collective-permute-start | bytes 786440 | tf_op jit(solution)/shard_map/ppermute | solution.py:38
  110.6 32.8 %collective-permute-start.18 = (bf16[16,64,128]{2,1,0:T(8,128)(2,1)S(1)}, bf16[16,64,128]{2,1,0:T(8,128)(2,1)S(1)}, u32[]{:S(2)}, u32[]{:S(2)}) collective-permute-start(bf16[16,64,128]{2,1,0:T(8,128)(2,1)S(1)} %copy-done.15), channel_id=1, source_target_pairs={{0,192},{8,200},{16,208},{24,216},{32,224},{40,232},{48,240},{56,2... | collective-permute-start | bytes 786440 | tf_op jit(solution)/shard_map/ppermute | solution.py:38
  134.7 8.8 %collective-permute-start.19 = (bf16[16,64,128]{2,1,0:T(8,128)(2,1)S(1)}, bf16[16,64,128]{2,1,0:T(8,128)(2,1)S(1)}, u32[]{:S(2)}, u32[]{:S(2)}) collective-permute-start(bf16[16,64,128]{2,1,0:T(8,128)(2,1)S(1)} %copy-done.14), channel_id=1, source_target_pairs={{0,64},{8,72},{16,80},{24,88},{32,96},{40,104},{48,112},{56,120},{... | collective-permute-start | bytes 786440 | tf_op jit(solution)/shard_map/ppermute | solution.py:38
  136.7 9.0 %collective-permute-start.17 = (bf16[16,64,128]{2,1,0:T(8,128)(2,1)S(1)}, bf16[16,64,128]{2,1,0:T(8,128)(2,1)S(1)}, u32[]{:S(2)}, u32[]{:S(2)}) collective-permute-start(bf16[16,64,128]{2,1,0:T(8,128)(2,1)S(1)} %collective-permute-done.16), channel_id=1, source_target_pairs={{0,48},{8,56},{16,0},{24,8},{32,16},{40,24},{48,32},{56,40},{64,11... | collective-permute-start | bytes 786440 | tf_op jit(solution)/shard_map/ppermute | solution.py:38
  140.3 7.3 %collective-permute-start.21 = (bf16[16,64,128]{2,1,0:T(8,128)(2,1)S(1)}, bf16[16,64,128]{2,1,0:T(8,128)(2,1)S(1)}, u32[]{:S(2)}, u32[]{:S(2)}) collective-permute-start(bf16[16,64,128]{2,1,0:T(8,128)(2,1)S(1)} %collective-permute-done.20), channel_id=1, source_target_pairs={{0,192},{8,200},{16,208},{24,216},{32,224},{40,232},{48,240},{56,2... | collective-permute-start | bytes 786440 | tf_op jit(solution)/shard_map/ppermute | solution.py:38
  168.6 38.0 %all-to-all-start.1 = ((bf16[32,4,64,128]{3,2,1,0:T(8,128)(2,1)}), bf16[32,4,64,128]{3,2,1,0:T(8,128)(2,1)}, u32[]{:S(2)}, u32[]{:S(2)}) async-start(bf16[32,4,64,128]{3,2,1,0:T(8,128)(2,1)} %get-tuple-element.52), calls=%async_computation.1 | async-start | bytes 4194304 | tf_op jit(solution)/shard_map/all_to_all | solution.py:416
  (30 other events, 366.7 us)
where the time goes:
time: 213 us; the launch traced here: 210 us
  waiting for transfers between devices  83.9 us (39%)
  starting transfers between devices  65.1 us (31%)
  Pallas kernels  52.8 us (25%)
  local copies, waits for them, and re-layouts  6.52 us (3%)
    ppermute x28, waiting for transfers between devices, shift(): return lax.ppermute(value, 'seq', pairs)  45.8 us
    pallas_call x2, Pallas kernels, attend(): pl.pallas_call(lambda *refs: attend_kernel(h, *refs), in_specs=[spec(sm)]...  37.8 us
    ppermute x28, starting transfers between devices, shift(): return lax.ppermute(value, 'seq', pairs)  37.6 us
    all_to_all x2, waiting for transfers between devices, layer(): back = lax.all_to_all(back, 'seq', split_axis=0, concat_axis=0, tiled=True)  25.1 us
    all_to_all x2, starting transfers between devices, layer(): back = lax.all_to_all(back, 'seq', split_axis=0, concat_axis=0, tiled=True)  17.1 us
    all_to_all x1, waiting for transfers between devices, layer(): lax.all_to_all(copies, ('seq', 'head'), split_axis=0, concat_axis=0, tile...  13 us
    all_to_all x1, starting transfers between devices, layer(): lax.all_to_all(copies, ('seq', 'head'), split_axis=0, concat_axis=0, tile...  10.4 us
    pallas_call x1, Pallas kernels, select(): pl.pallas_call(select_kernel, name='select', in_specs=[spec(pltpu.SMEM),...  7.66 us
  transfers between devices with their start and end apart: 31, of which 10 were waited for; matrix products, arithmetic and copies ran while one was open for 2% of the time, Pallas kernels for 11%

commit v1 on v0

--- a/solution.py
+++ b/solution.py
@@ -18,7 +18,7 @@
 LOG2E = 1.4426950408889634
 SCALE = 1.0 / math.sqrt(HD)
 OFFS = (0, 1, -1, 2)
-QT = 256
+QT = 512
 KC = 256
 NSPLIT = POOL * BLK // KC
 SPC = KC // BLK
@@ -55,17 +55,17 @@
     return jnp.where(cond, 1.0, 0.0)
 
 
-def select_kernel(where_ref, tseg_ref, trow_ref, *refs):
-    pieces_k, pieces_v = refs[:8], refs[8:16]
-    table_ref, mask_ref = refs[16:18]
-    outs = refs[18:30]
-    prefix_ref, table_smem, table_sem, sems = refs[30:]
-    me = where_ref[0]
+def order_of(me, y, x, c):
+    return ((c ^ (me % 2)) * NY + (y ^ (me // 8))) * NX + (x ^ ((me // 2) % 4))
+
+
+def prep_kernel(where_ref, lists_ref, table_ref, mask_ref):
+    me, head = where_ref[0], where_ref[1]
     nid = NSEQ * 8
     ids = iota((NSEQ, nid), 1)
     flags = ids < 0
     for e in range(128):
-        flags = flags | (tseg_ref[:, e : e + 1] == ids)
+        flags = flags | (lists_ref[:, e : e + 1] == ids)
     wanted = flag(flags)
     row, col = iota((nid, nid), 0), iota((nid, nid), 1)
     upto = flag(row <= col)
@@ -84,28 +84,47 @@
         table_ref[r * NSEQ : (r + 1) * NSEQ, :] = jnp.where(has > 0.5, block, -1.0).astype(jnp.int32)
         spare = iota((NSEQ, NSEQ), 1) + POOL + NSEQ * r
         table_ref[(2 + r) * NSEQ : (3 + r) * NSEQ, :] = jnp.where(has > 0.5, place.astype(jnp.int32), spare)
-    to_smem = pltpu.make_async_copy(table_ref, table_smem, table_sem)
-    to_smem.start()
-    prefix_ref[...] = jnp.where(flags, prefix - 1.0, -1.0)
-    mine = prefix_ref[pl.ds(me, 1), :]
+    mine = jnp.where(flags, prefix - 1.0, -1.0)[0:1, :]
     compact = flag(iota((POOL, nid), 0).astype(jnp.float32) == mine)
-    named = trow_ref[pl.ds(me * 8, 8), :]
-    ids8 = iota((8, nid), 1)
+    own = lists_ref[0:1, :]
+    ids8, row8 = iota((8, nid), 1), iota((8, nid), 0)
     used = ids8 < 0
     for e in range(16):
-        used = used | (named[:, e : e + 1] == ids8)
-    used = flag(used & (ids8 < me * 8 + iota((8, nid), 0)))
-    spread = flag(iota((8, SEG), 0) == (iota((8, SEG), 1) >> 6))
+        named = jnp.zeros((8, nid), jnp.int32)
+        for j in range(8):
+            named = jnp.where(row8 == j, own[:, j * 16 + e : j * 16 + e + 1], named)
+        used = used | (named == ids8)
+    used = flag(used & (ids8 < me * 8 + (row8 ^ head)))
+    spread = flag((iota((8, SEG), 0) ^ head) == (iota((8, SEG), 1) >> 6))
     by_id = dot(used.astype(jnp.bfloat16), spread.astype(jnp.bfloat16), TN)
     mask_ref[...] = dot(compact.astype(jnp.bfloat16), by_id.astype(jnp.bfloat16), NN)
-    to_smem.wait()
+
+
+def prep(where, lists):
+    return pl.pallas_call(
+        prep_kernel,
+        name="prep",
+        in_specs=[pl.BlockSpec(memory_space=pltpu.SMEM), pl.BlockSpec(memory_space=pltpu.VMEM)],
+        out_specs=[pl.BlockSpec(memory_space=pltpu.VMEM)] * 2,
+        out_shape=[
+            jax.ShapeDtypeStruct((4 * NSEQ, NSEQ), jnp.int32),
+            jax.ShapeDtypeStruct((POOL, SEG), jnp.float32),
+        ],
+        cost_estimate=pl.CostEstimate(flops=10_000_000, bytes_accessed=1 << 20, transcendentals=0),
+    )(where, lists)
+
+
+def select_kernel(where_ref, table_ref, *refs):
+    pieces_k, pieces_v = refs[:8], refs[8:16]
+    outs, sems = refs[16:28], refs[28]
+    me = where_ref[0]
     y, x, c = me // 8, (me // 2) % 4, me % 2
-    for kind, pieces in ((0, pieces_k), (1, pieces_v)):
-        for oi, off in enumerate(OFFS[1:]):
+    for oi, off in enumerate(OFFS[1:]):
+        for kind, pieces in ((0, pieces_k), (1, pieces_v)):
             if kind == 0:
-                reader = seq_of(y, (x + off + 4) % 4, c)
+                reader = order_of(me, y, (x + off + 4) % 4, c)
             else:
-                reader = seq_of((y + off + 4) % 4, x, c)
+                reader = order_of(me, (y + off + 4) % 4, x, c)
             for j in range(16):
                 di, dc, r = j // 4, (j // 2) % 2, j % 2
                 d = OFFS[di]
@@ -113,7 +132,7 @@
                     writer = seq_of((y + d + 4) % 4, x, (c + dc) % 2)
                 else:
                     writer = seq_of(y, (x + d + 4) % 4, (c + dc) % 2)
-                block = jnp.maximum(table_smem[r * NSEQ + reader, writer], 0)
+                block = jnp.maximum(table_ref[r * NSEQ + reader, writer], 0)
                 rows = pl.ds(pl.multiple_of(block * BLK, BLK), BLK)
                 for h in range(2):
                     i = h * 6 + kind * 3 + oi
@@ -124,26 +143,17 @@
         pltpu.make_async_copy(outs[i], outs[i], sems.at[i]).wait()
 
 
-def select(where, tseg, trow, pieces_k, pieces_v):
+def select(where, table, pieces_k, pieces_v):
     spec = lambda space: pl.BlockSpec(memory_space=space)
     return pl.pallas_call(
         select_kernel,
         name="select",
-        in_specs=[spec(pltpu.SMEM), spec(pltpu.VMEM), spec(pltpu.VMEM)] + [spec(pl.ANY)] * 16,
-        out_specs=[spec(pltpu.VMEM)] * 14,
-        out_shape=[
-            jax.ShapeDtypeStruct((4 * NSEQ, NSEQ), jnp.int32),
-            jax.ShapeDtypeStruct((POOL, SEG), jnp.float32),
-        ]
-        + [jax.ShapeDtypeStruct((16, BLK, HD), jnp.bfloat16)] * 12,
-        scratch_shapes=[
-            pltpu.VMEM((NSEQ, NSEQ * 8), jnp.float32),
-            pltpu.SMEM((4 * NSEQ, NSEQ), jnp.int32),
-            pltpu.SemaphoreType.DMA,
-            pltpu.SemaphoreType.DMA((12,)),
-        ],
-        cost_estimate=pl.CostEstimate(flops=10_000_000, bytes_accessed=8 << 20, transcendentals=0),
-    )(where, tseg, trow, *pieces_k, *pieces_v)
+        in_specs=[spec(pltpu.SMEM)] * 2 + [spec(pl.ANY)] * 16,
+        out_specs=[spec(pltpu.VMEM)] * 12,
+        out_shape=[jax.ShapeDtypeStruct((16, BLK, HD), jnp.bfloat16)] * 12,
+        scratch_shapes=[pltpu.SemaphoreType.DMA((12,))],
+        cost_estimate=pl.CostEstimate(flops=1_000_000, bytes_accessed=6 << 20, transcendentals=0),
+    )(where, table, *pieces_k, *pieces_v)
 
 
 def attend_kernel(h, where_ref, table_ref, bias_ref, q_ref, do_ref, k_ref, v_ref, mask_ref, *refs):
@@ -165,9 +175,9 @@
                     writer = seq_of((y + d + 4) % 4, (x + off + 4) % 4, (c + dc) % 2)
                 else:
                     writer = seq_of((y + off + 4) % 4, (x + d + 4) % 4, (c + dc) % 2)
-                place = table_ref[(2 + r) * NSEQ + me, writer]
+                place = table_ref[(2 + r) * NSEQ, writer]
                 if oi == 0:
-                    block = jnp.maximum(table_ref[r * NSEQ + me, writer], 0)
+                    block = jnp.maximum(table_ref[r * NSEQ, writer], 0)
                     rows = pl.ds(pl.multiple_of(block * BLK, BLK), BLK)
                     src = pieces[kind][di * 2 + dc].at[rows, pl.ds(h * HD, HD)]
                 else:
@@ -281,7 +291,7 @@
     dvb[...] = dva[...].astype(jnp.bfloat16)
     for w in range(NSEQ):
         for r in range(2):
-            place = jnp.minimum(table_ref[(2 + r) * NSEQ + me, w], POOL - 1)
+            place = jnp.minimum(table_ref[(2 + r) * NSEQ, w], POOL - 1)
             for kind, ref in ((0, dkb), (1, dvb)):
                 pltpu.make_async_copy(
                     ref.at[pl.ds(pl.multiple_of(place * BLK, BLK), BLK), :],
@@ -338,7 +348,7 @@
 
     def step(s, _):
         for r in range(2):
-            block = table_ref[r * NSEQ + s, me]
+            block = table_ref[r * NSEQ + order_of(me, s // 8, (s // 2) % 4, s % 2), me]
 
             @pl.when(block >= 0)
             def _():
@@ -378,17 +388,20 @@
 
 
 def layer(queries, keys, values, grad_out, retrieved, mem_bias):
-    where = lax.axis_index("seq").astype(jnp.int32).reshape(1)
-    devices = lax.axis_size("seq") * lax.axis_size("head")
-    copies = jnp.broadcast_to(retrieved, (devices, *retrieved.shape))
-    lists = lax.all_to_all(copies, ("seq", "head"), split_axis=0, concat_axis=0, tiled=True)
-    trow = lists.reshape(devices, 16)
-    tseg = lists.reshape(NSEQ, 128)
+    where = jnp.stack([lax.axis_index("seq"), lax.axis_index("head")]).astype(jnp.int32)
+    lists = retrieved
+    for bit in (1, 2, 4):
+        other = lax.ppermute(lists, "head", [(i, i ^ bit) for i in range(8)])
+        lists = jnp.concatenate([lists, other], axis=1)
+    for bit in (2, 4, 8, 16, 1):
+        other = lax.ppermute(lists, "seq", [(i, i ^ bit) for i in range(NSEQ)])
+        lists = jnp.concatenate([lists, other], axis=0)
+    table, mask = prep(where, lists)
     col_k = [keys] + [shift(keys, -d, 0, 0) for d in OFFS[1:]]
     row_v = [values] + [shift(values, 0, -d, 0) for d in OFFS[1:]]
     pieces_k = [p for piece in col_k for p in (piece, shift(piece, 0, 0, 1))]
     pieces_v = [p for piece in row_v for p in (piece, shift(piece, 0, 0, 1))]
-    table, mask, *msgs = select(where, tseg, trow, pieces_k, pieces_v)
+    msgs = select(where, table, pieces_k, pieces_v)
     near_k, near_v = shift(msgs[8], 0, -1, 0), shift(msgs[11], -1, 0, 0)
     fetched = []
     for h in range(2):

time: 213 us -> 220 us (1.033)
  starting transfers between devices: 65.1 us -> 76.7 us
  Pallas kernels: 52.8 us -> 47.2 us
  other arithmetic: 0.97 us -> 5.06 us
    ppermute x0 -> x8, starting transfers between devices: none -> 24.7 us  [the longest x5 13 us: layer(): other = lax.ppermute(lists, 'seq', [(i, i ^ bit) for i in range(NSEQ)])]
    all_to_all x1 -> x0, waiting for transfers between devices: 13 us -> none  [layer(): lax.all_to_all(copies, ('seq', 'head'), split_axis=0, concat_axis=0, tile...]
    ppermute x0 -> x8, waiting for transfers between devices: none -> 11.2 us  [the longest x5 8.19 us: layer(): other = lax.ppermute(lists, 'seq', [(i, i ^ bit) for i in range(NSEQ)])]
    all_to_all x1 -> x0, starting transfers between devices: 10.4 us -> none  [layer(): lax.all_to_all(copies, ('seq', 'head'), split_axis=0, concat_axis=0, tile...]
    pallas_call x2, Pallas kernels: 37.8 us -> 29.7 us  [attend(): pl.pallas_call(lambda *refs: attend_kernel(h, *refs), in_specs=[spec(sm)]...]
    concatenate x0 -> x6, other arithmetic: none -> 4.39 us  [the longest x3 2.2 us: layer(): lists = jnp.concatenate([lists, other], axis=0)]
    ppermute x28, starting transfers between devices: 37.6 us -> 35.1 us  [shift(): return lax.ppermute(value, 'seq', pairs)]
    pallas_call x1 -> x2, Pallas kernels: 7.66 us -> 8.69 us  [the longest x1 5.78 us: select(): pl.pallas_call(select_kernel, name='select', in_specs=[spec(pltpu.SMEM)]...]
  transfers between devices with their start and end apart: 31 -> 38, of which waited for: 10 -> 17; matrix products, arithmetic and copies ran while one was open for 2% -> 2% of each run, Pallas kernels for 11% -> 10%
where the time goes in v1:
time: 220 us; the launch traced here: 219 us
  waiting for transfers between devices  83.2 us (38%)
  starting transfers between devices  76.7 us (35%)
  Pallas kernels  47.2 us (21%)
  local copies, waits for them, and re-layouts  5.52 us (3%)
  other arithmetic  5.06 us (2%)
    ppermute x28, waiting for transfers between devices, shift(): return lax.ppermute(value, 'seq', pairs)  47.7 us
    ppermute x28, starting transfers between devices, shift(): return lax.ppermute(value, 'seq', pairs)  35.1 us
    pallas_call x2, Pallas kernels, attend(): pl.pallas_call(lambda *refs: attend_kernel(h, *refs), in_specs=[spec(sm)]...  29.7 us
    all_to_all x2, waiting for transfers between devices, layer(): back = lax.all_to_all(back, 'seq', split_axis=0, concat_axis=0, tiled=True)  24.4 us
    all_to_all x2, starting transfers between devices, layer(): back = lax.all_to_all(back, 'seq', split_axis=0, concat_axis=0, tiled=True)  17 us
    ppermute x5, starting transfers between devices, layer(): other = lax.ppermute(lists, 'seq', [(i, i ^ bit) for i in range(NSEQ)])  13 us
    ppermute x3, starting transfers between devices, layer(): other = lax.ppermute(lists, 'head', [(i, i ^ bit) for i in range(8)])  11.6 us
    pallas_call x2, Pallas kernels, settle(): pl.pallas_call(lambda *refs: settle_kernel(h, *refs), in_specs=[spec(pltp...  8.73 us
  transfers between devices with their start and end apart: 38, of which 17 were waited for; matrix products, arithmetic and copies ran while one was open for 2% of the time, Pallas kernels for 10%

profile of v1, /device:TPU:1, one launch (start us, length us, event | category | flops | bytes accessed | tf_op | source)
XLA Modules:
  0.0 218.8 jit_solution(17460513283354058032)
XLA Ops:
  0.6 2.5 %collective-permute-start = (s32[1,16]{1,0:T(1,128)}, s32[1,16]{1,0:T(1,128)S(1)}, u32[]{:S(2)}, u32[]{:S(2)}) collective-permute-start(s32[1,16]{1,0:T(1,128)} %param.10), channel_id=1, source_target_pairs={{0,1},{1,0},{2,3},{3,2},{4,5},{5,4},{6,7},{7,6},{8,9},{9,8},{10,11... | collective-permute-start | bytes 200 | tf_op jit(solution)/shard_map/ppermute | solution.py:394
  5.0 3.0 %collective-permute-start.1 = (s32[1,32]{1,0:T(1,128)S(1)}, s32[1,32]{1,0:T(1,128)S(1)}, u32[]{:S(2)}, u32[]{:S(2)}) collective-permute-start(s32[1,32]{1,0:T(1,128)S(1)} %pad_add_fusion.4), channel_id=1, source_target_pairs={{0,2},{1,3},{2,0},{3,1},{4,6},{5,7},{6,4},{7,5},{8,10},{9,11},{10,... | collective-permute-start | bytes 392 | tf_op jit(solution)/shard_map/ppermute | solution.py:394
  9.7 6.1 %collective-permute-start.2 = (s32[1,64]{1,0:T(1,128)S(1)}, s32[1,64]{1,0:T(1,128)S(1)}, u32[]{:S(2)}, u32[]{:S(2)}) collective-permute-start(s32[1,64]{1,0:T(1,128)S(1)} %pad_add_fusion.5), channel_id=1, source_target_pairs={{0,4},{1,5},{2,6},{3,7},{4,0},{5,1},{6,2},{7,3},{8,12},{9,13},{10,... | collective-permute-start | bytes 776 | tf_op jit(solution)/shard_map/ppermute | solution.py:394
  18.7 2.7 %collective-permute-start.9 = (bf16[512,256]{1,0:T(8,128)(2,1)}, bf16[512,256]{1,0:T(8,128)(2,1)S(1)}, u32[]{:S(2)}, u32[]{:S(2)}) collective-permute-start(bf16[512,256]{1,0:T(8,128)(2,1)} %refs_8_.5), channel_id=1, source_target_pairs={{0,192},{8,200},{16,208},{24,216},{32,224},{40,232},{48,240},{56,2... | collective-permute-start | bytes 786440 | tf_op jit(solution)/shard_map/ppermute | solution.py:38
  23.1 1.8 collective-permute-start.16
  26.3 3.3 %collective-permute-done.4 = s32[2,128]{1,0:T(2,128)S(1)} collective-permute-done((s32[2,128]{1,0:T(2,128)S(1)}, s32[2,128]{1,0:T(2,128)S(1)}, u32[]{:S(2)}, u32[]{:S(2)}) %collective-permute-start.4) | collective-permute-done | bytes 1056 | tf_op jit(solution)/shard_map/ppermute | solution.py:397
  35.2 2.8 %collective-permute-done.6 = s32[8,128]{1,0:T(8,128)S(1)} collective-permute-done((s32[8,128]{1,0:T(8,128)S(1)}, s32[8,128]{1,0:T(8,128)S(1)}, u32[]{:S(2)}, u32[]{:S(2)}) %collective-permute-start.6) | collective-permute-done | bytes 4128 | tf_op jit(solution)/shard_map/ppermute | solution.py:397
  38.0 8.3 %collective-permute-start.7 = (s32[16,128]{1,0:T(8,128)S(1)}, s32[16,128]{1,0:T(8,128)S(1)}, u32[]{:S(2)}, u32[]{:S(2)}) collective-permute-start(s32[16,128]{1,0:T(8,128)S(1)} %concatenate.36), channel_id=1, source_target_pairs={{0,8},{8,0},{16,24},{24,16},{32,40},{40,32},{48,56},{56,48},{64,72... | collective-permute-start | bytes 24584 | tf_op jit(solution)/shard_map/ppermute | solution.py:397
  47.6 1.7 collective-permute-start.20
  50.8 5.7 %collective-permute-done.18.refs_12_.refs_20_ = bf16[512,256]{1,0:T(8,128)(2,1)S(1)} collective-permute-done((bf16[512,256]{1,0:T(8,128)(2,1)}, bf16[512,256]{1,0:T(8,128)(2,1)S(1)}, u32[]{:S(2)}, u32[]{:S(2)}) %collective-permute-start.18) | collective-permute-done | bytes 262176 | tf_op jit(solution)/shard_map/ppermute | solution.py:38
  56.5 6.4 %collective-permute-start.12 = (bf16[512,256]{1,0:T(8,128)(2,1)S(1)}, bf16[512,256]{1,0:T(8,128)(2,1)S(1)}, u32[]{:S(2)}, u32[]{:S(2)}) collective-permute-start(bf16[512,256]{1,0:T(8,128)(2,1)S(1)} %collective-permute-done.11.refs_4_.refs_12_), channel_id=1, source_target_pairs={{0,8},{8,0},{16,24},{24,16},{32,40},{40,32},{48,56},{56,48},{64,72... | collective-permute-start | bytes 786440 | tf_op jit(solution)/shard_map/ppermute | solution.py:38
  64.6 1.8 concatenate.37.lists_ref
  66.4 2.9 %prep.1 = (s32[128,32]{1,0:T(8,128)}, f32[32,512]{1,0:T(8,128)}) custom-call(s32[2]{0:T(128)} %pad_add_fusion.3.where_ref.refs_0_, s32[32,128]{1,0:T(8,128)} %concatenate.37.lists_ref), custom_call_target="tpu_custom_call" | custom-call | flops 10000000 | bytes 1048576 | tf_op jit(solution)/shard_map/prep/pallas_call | solution.py:104
  70.3 5.8 %select.1 = (bf16[16,64,128]{2,1,0:T(8,128)(2,1)}, bf16[16,64,128]{2,1,0:T(8,128)(2,1)}, bf16[16,64,128]{2,1,0:T(8,128)(2,1)}, bf16[16,64,128]{2,1,0:T(8,128)(2,...) custom-call(s32[2]{0:T(128)} %pad_add_fusion.3.where_ref.refs_0_, ...), custom_call_target="tpu_custom_call" | custom-call | flops 1000000 | bytes 6291456 | tf_op jit(solution)/shard_map/select/pallas_call | solution.py:148
  79.8 4.4 %collective-permute-done.30.refs_24_ = bf16[16,64,128]{2,1,0:T(8,128)(2,1)S(1)} collective-permute-done((bf16[16,64,128]{2,1,0:T(8,128)(2,1)}, bf16[16,64,128]{2,1,0:T(8,128)(2,1)S(1)}, u32[]{:S(2)}, u32[]{:S(2)}) %collective-permute-start.30) | collective-permute-done | bytes 262176 | tf_op jit(solution)/shard_map/ppermute | solution.py:38
  86.3 4.0 %collective-permute-done.32.refs_26_ = bf16[16,64,128]{2,1,0:T(8,128)(2,1)S(1)} collective-permute-done((bf16[16,64,128]{2,1,0:T(8,128)(2,1)}, bf16[16,64,128]{2,1,0:T(8,128)(2,1)S(1)}, u32[]{:S(2)}, u32[]{:S(2)}) %collective-permute-start.32) | collective-permute-done | bytes 262176 | tf_op jit(solution)/shard_map/ppermute | solution.py:38
  90.3 2.1 collective-permute-done.35.refs_29_
  93.1 14.9 %shard_map.93 = (bf16[512,256]{1,0:T(8,128)(2,1)}, bf16[512,256]{1,0:T(8,128)(2,1)}, f32[512,128]{1,0:T(8,128)}, f32[512,128]{1,0:T(8,128)}, bf16[32,4,64,128]{3,2,1,0:T(8,128)(2,1)}) custom-call(s32[2]{0:T(128)} %pad_add_fusion.3.where_ref.refs_0_, s32[128,32]{1,0:T(8,128)} %get-tuple-element.32.table_ref.refs_1_, f32[2]{0:T(128)} %refs_2_.3, ...), custom_call_target="tpu_custom_call" | custom-call | flops 16000000000 | bytes 8388608 | tf_op jit(solution)/shard_map/pallas_call | solution.py:311
  108.0 7.7 %all-to-all-start.1 = ((bf16[32,4,64,128]{3,2,1,0:T(8,128)(2,1)}), bf16[32,4,64,128]{3,2,1,0:T(8,128)(2,1)S(1)}, u32[]{:S(2)}, u32[]{:S(2)}) async-start(bf16[32,4,64,128]{3,2,1,0:T(8,128)(2,1)} %get-tuple-element.55), calls=%async_computation.1 | async-start | bytes 4194304 | tf_op jit(solution)/shard_map/all_to_all | solution.py:429
  115.7 2.6 %collective-permute-start.24 = (bf16[16,64,128]{2,1,0:T(8,128)(2,1)}, bf16[16,64,128]{2,1,0:T(8,128)(2,1)S(1)}, u32[]{:S(2)}, u32[]{:S(2)}) collective-permute-start(bf16[16,64,128]{2,1,0:T(8,128)(2,1)} %get-tuple-element.36), channel_id=1, source_target_pairs={{0,48},{8,56},{16,0},{24,8},{32,16},{40,24},{48,32},{56,40},{64,11... | collective-permute-start | bytes 786440 | tf_op jit(solution)/shard_map/ppermute | solution.py:38
  118.4 2.5 %collective-permute-start.28 = (bf16[16,64,128]{2,1,0:T(8,128)(2,1)S(1)}, bf16[16,64,128]{2,1,0:T(8,128)(2,1)S(1)}, u32[]{:S(2)}, u32[]{:S(2)}) collective-permute-start(bf16[16,64,128]{2,1,0:T(8,128)(2,1)S(1)} %copy-done.18), channel_id=1, source_target_pairs={{0,192},{8,200},{16,208},{24,216},{32,224},{40,232},{48,240},{56,2... | collective-permute-start | bytes 786440 | tf_op jit(solution)/shard_map/ppermute | solution.py:38
  122.8 23.5 %collective-permute-done.24 = bf16[16,64,128]{2,1,0:T(8,128)(2,1)S(1)} collective-permute-done((bf16[16,64,128]{2,1,0:T(8,128)(2,1)}, bf16[16,64,128]{2,1,0:T(8,128)(2,1)S(1)}, u32[]{:S(2)}, u32[]{:S(2)}) %collective-permute-start.24) | collective-permute-done | bytes 262176 | tf_op jit(solution)/shard_map/ppermute | solution.py:38
  146.3 2.0 collective-permute-start.27
  149.3 2.6 %collective-permute-done.22.refs_24_ = bf16[16,64,128]{2,1,0:T(8,128)(2,1)S(1)} collective-permute-done((bf16[16,64,128]{2,1,0:T(8,128)(2,1)S(1)}, bf16[16,64,128]{2,1,0:T(8,128)(2,1)S(1)}, u32[]{:S(2)}, u32[]{:S(2)}) %collective-permute-start.22) | collective-permute-done | bytes 262176 | tf_op jit(solution)/shard_map/ppermute | solution.py:38
  152.0 3.2 %collective-permute-start.29 = (bf16[16,64,128]{2,1,0:T(8,128)(2,1)S(1)}, bf16[16,64,128]{2,1,0:T(8,128)(2,1)S(1)}, u32[]{:S(2)}, u32[]{:S(2)}) collective-permute-start(bf16[16,64,128]{2,1,0:T(8,128)(2,1)S(1)} %collective-permute-done.28), channel_id=1, source_target_pairs={{0,192},{8,200},{16,208},{24,216},{32,224},{40,232},{48,240},{56,2... | collective-permute-start | bytes 786440 | tf_op jit(solution)/shard_map/ppermute | solution.py:38
  155.2 2.2 collective-permute-done.25.refs_26_
  157.3 1.9 collective-permute-done.29.refs_29_
  160.0 14.9 %shard_map.94 = (bf16[512,256]{1,0:T(8,128)(2,1)}, bf16[512,256]{1,0:T(8,128)(2,1)}, f32[512,128]{1,0:T(8,128)}, f32[512,128]{1,0:T(8,128)}, bf16[32,4,64,128]{3,2,1,0:T(8,128)(2,1)}) custom-call(s32[2]{0:T(128)} %pad_add_fusion.3.where_ref.refs_0_, s32[128,32]{1,0:T(8,128)} %get-tuple-element.32.table_ref.refs_1_, ...), custom_call_target="tpu_custom_call", output_to_operand_aliasing={{0}: (30, {}), {1}: (31, {})} | custom-call | flops 16000000000 | bytes 8388608 | tf_op jit(solution)/shard_map/pallas_call | solution.py:311
  176.2 9.3 %all-to-all-start = ((bf16[32,4,64,128]{3,2,1,0:T(8,128)(2,1)}), bf16[32,4,64,128]{3,2,1,0:T(8,128)(2,1)}, u32[]{:S(2)}, u32[]{:S(2)}) async-start(bf16[32,4,64,128]{3,2,1,0:T(8,128)(2,1)} %get-tuple-element.52), calls=%async_computation | async-start | bytes 4194304 | tf_op jit(solution)/shard_map/all_to_all | solution.py:429
  185.5 4.4 %shard_map.95 = (bf16[512,256]{1,0:T(8,128)(2,1)}, bf16[512,256]{1,0:T(8,128)(2,1)}) custom-call(s32[2]{0:T(128)} %pad_add_fusion.3.where_ref.refs_0_, s32[128,32]{1,0:T(8,128)} %get-tuple-element.32.table_ref.refs_1_, f32[512,128]{1,0:T(8,128)} %get-tuple-element.53.refs_2_, f32[512,128]{1,0:T(8,128)} %get-tuple-element.54.refs_3_, ...), custom_call_target="tpu_custom_call" | custom-call | flops 2000000 | bytes 3145728 | tf_op jit(solution)/shard_map/pallas_call | solution.py:377
  189.9 24.4 %all-to-all-done.refs_4_ = bf16[32,4,64,128]{3,2,1,0:T(8,128)(2,1)} async-done(((bf16[32,4,64,128]{3,2,1,0:T(8,128)(2,1)}), bf16[32,4,64,128]{3,2,1,0:T(8,128)(2,1)}, u32[]{:S(2)}, u32[]{:S(2)}) %all-to-all-start) | async-done | bytes 2097184 | tf_op jit(solution)/shard_map/all_to_all | solution.py:429
  214.3 4.4 %shard_map.96 = (bf16[512,256]{1,0:T(8,128)(2,1)}, bf16[512,256]{1,0:T(8,128)(2,1)}) custom-call(s32[2]{0:T(128)} %pad_add_fusion.3.where_ref.refs_0_, s32[128,32]{1,0:T(8,128)} %get-tuple-element.32.table_ref.refs_1_, f32[512,128]{1,0:T(8,128)} %get-tuple-element.50.refs_2_, ...), custom_call_target="tpu_custom_call", output_to_operand_aliasing={{0}: (5, {}), {1}: (6, {})} | custom-call | flops 2000000 | bytes 3145728 | tf_op jit(solution)/shard_map/pallas_call | solution.py:377
  (121 shorter events, 32.0 us)
Async XLA Ops:
  9.7 7.1 %collective-permute-start.2 = (s32[1,64]{1,0:T(1,128)S(1)}, s32[1,64]{1,0:T(1,128)S(1)}, u32[]{:S(2)}, u32[]{:S(2)}) collective-permute-start(s32[1,64]{1,0:T(1,128)S(1)} %pad_add_fusion.5), channel_id=1, source_target_pairs={{0,4},{1,5},{2,6},{3,7},{4,0},{5,1},{6,2},{7,3},{8,12},{9,13},{10,... | collective-permute-start | bytes 776 | tf_op jit(solution)/shard_map/ppermute | solution.py:394
  17.5 7.4 %collective-permute-start.3 = (s32[1,128]{1,0:T(1,128)S(1)}, s32[1,128]{1,0:T(1,128)S(1)}, u32[]{:S(2)}, u32[]{:S(2)}) collective-permute-start(s32[1,128]{1,0:T(1,128)S(1)} %pad_add_fusion.6), channel_id=1, source_target_pairs={{0,16},{8,24},{16,0},{24,8},{32,48},{40,56},{48,32},{56,40},{64,80... | collective-permute-start | bytes 1544 | tf_op jit(solution)/shard_map/ppermute | solution.py:397
  18.7 28.9 %collective-permute-start.9 = (bf16[512,256]{1,0:T(8,128)(2,1)}, bf16[512,256]{1,0:T(8,128)(2,1)S(1)}, u32[]{:S(2)}, u32[]{:S(2)}) collective-permute-start(bf16[512,256]{1,0:T(8,128)(2,1)} %refs_8_.5), channel_id=1, source_target_pairs={{0,192},{8,200},{16,208},{24,216},{32,224},{40,232},{48,240},{56,2... | collective-permute-start | bytes 786440 | tf_op jit(solution)/shard_map/ppermute | solution.py:38
  21.4 27.9 %collective-permute-start.11 = (bf16[512,256]{1,0:T(8,128)(2,1)}, bf16[512,256]{1,0:T(8,128)(2,1)S(1)}, u32[]{:S(2)}, u32[]{:S(2)}) collective-permute-start(bf16[512,256]{1,0:T(8,128)(2,1)} %refs_8_.5), channel_id=1, source_target_pairs={{0,64},{8,72},{16,80},{24,88},{32,96},{40,104},{48,112},{56,120},{... | collective-permute-start | bytes 786440 | tf_op jit(solution)/shard_map/ppermute | solution.py:38
  21.4 28.8 %collective-permute-start.13 = (bf16[512,256]{1,0:T(8,128)(2,1)}, bf16[512,256]{1,0:T(8,128)(2,1)S(1)}, u32[]{:S(2)}, u32[]{:S(2)}) collective-permute-start(bf16[512,256]{1,0:T(8,128)(2,1)} %refs_8_.5), channel_id=1, source_target_pairs={{0,128},{8,136},{16,144},{24,152},{32,160},{40,168},{48,176},{56,1... | collective-permute-start | bytes 786440 | tf_op jit(solution)/shard_map/ppermute | solution.py:38
  23.1 27.3 %collective-permute-start.16 = (bf16[512,256]{1,0:T(8,128)(2,1)}, bf16[512,256]{1,0:T(8,128)(2,1)S(1)}, u32[]{:S(2)}, u32[]{:S(2)}) collective-permute-start(bf16[512,256]{1,0:T(8,128)(2,1)} %refs_16_.3), channel_id=1, source_target_pairs={{0,48},{8,56},{16,0},{24,8},{32,16},{40,24},{48,32},{56,40},{64,11... | collective-permute-start | bytes 786440 | tf_op jit(solution)/shard_map/ppermute | solution.py:38
  38.0 9.1 %collective-permute-start.7 = (s32[16,128]{1,0:T(8,128)S(1)}, s32[16,128]{1,0:T(8,128)S(1)}, u32[]{:S(2)}, u32[]{:S(2)}) collective-permute-start(s32[16,128]{1,0:T(8,128)S(1)} %concatenate.36), channel_id=1, source_target_pairs={{0,8},{8,0},{16,24},{24,16},{32,40},{40,32},{48,56},{56,48},{64,72... | collective-permute-start | bytes 24584 | tf_op jit(solution)/shard_map/ppermute | solution.py:397
  47.1 9.4 %collective-permute-start.18 = (bf16[512,256]{1,0:T(8,128)(2,1)}, bf16[512,256]{1,0:T(8,128)(2,1)S(1)}, u32[]{:S(2)}, u32[]{:S(2)}) collective-permute-start(bf16[512,256]{1,0:T(8,128)(2,1)} %refs_16_.3), channel_id=1, source_target_pairs={{0,16},{8,24},{16,32},{24,40},{32,48},{40,56},{48,0},{56,8},{64,80... | collective-permute-start | bytes 786440 | tf_op jit(solution)/shard_map/ppermute | solution.py:38
  47.6 15.3 %collective-permute-start.20 = (bf16[512,256]{1,0:T(8,128)(2,1)}, bf16[512,256]{1,0:T(8,128)(2,1)S(1)}, u32[]{:S(2)}, u32[]{:S(2)}) collective-permute-start(bf16[512,256]{1,0:T(8,128)(2,1)} %refs_16_.3), channel_id=1, source_target_pairs={{0,32},{8,40},{16,48},{24,56},{32,0},{40,8},{48,16},{56,24},{64,96... | collective-permute-start | bytes 786440 | tf_op jit(solution)/shard_map/ppermute | solution.py:38
  49.4 13.6 %collective-permute-start.15 = (bf16[512,256]{1,0:T(8,128)(2,1)}, bf16[512,256]{1,0:T(8,128)(2,1)S(1)}, u32[]{:S(2)}, u32[]{:S(2)}) collective-permute-start(bf16[512,256]{1,0:T(8,128)(2,1)} %refs_16_.3), channel_id=1, source_target_pairs={{0,8},{8,0},{16,24},{24,16},{32,40},{40,32},{48,56},{56,48},{64,72... | collective-permute-start | bytes 786440 | tf_op jit(solution)/shard_map/ppermute | solution.py:38
  50.3 13.1 %collective-permute-start.8 = (bf16[512,256]{1,0:T(8,128)(2,1)}, bf16[512,256]{1,0:T(8,128)(2,1)S(1)}, u32[]{:S(2)}, u32[]{:S(2)}) collective-permute-start(bf16[512,256]{1,0:T(8,128)(2,1)} %refs_8_.5), channel_id=1, source_target_pairs={{0,8},{8,0},{16,24},{24,16},{32,40},{40,32},{48,56},{56,48},{64,72... | collective-permute-start | bytes 786440 | tf_op jit(solution)/shard_map/ppermute | solution.py:38
  50.4 13.3 %collective-permute-start.10 = (bf16[512,256]{1,0:T(8,128)(2,1)S(1)}, bf16[512,256]{1,0:T(8,128)(2,1)S(1)}, u32[]{:S(2)}, u32[]{:S(2)}) collective-permute-start(bf16[512,256]{1,0:T(8,128)(2,1)S(1)} %collective-permute-done.9.refs_2_.refs_10_), channel_id=1, source_target_pairs={{0,8},{8,0},{16,24},{24,16},{32,40},{40,32},{48,56},{56,48},{64,72... | collective-permute-start | bytes 786440 | tf_op jit(solution)/shard_map/ppermute | solution.py:38
  56.5 12.8 %collective-permute-start.12 = (bf16[512,256]{1,0:T(8,128)(2,1)S(1)}, bf16[512,256]{1,0:T(8,128)(2,1)S(1)}, u32[]{:S(2)}, u32[]{:S(2)}) collective-permute-start(bf16[512,256]{1,0:T(8,128)(2,1)S(1)} %collective-permute-done.11.refs_4_.refs_12_), channel_id=1, source_target_pairs={{0,8},{8,0},{16,24},{24,16},{32,40},{40,32},{48,56},{56,48},{64,72... | collective-permute-start | bytes 786440 | tf_op jit(solution)/shard_map/ppermute | solution.py:38
  62.9 6.4 %collective-permute-start.14 = (bf16[512,256]{1,0:T(8,128)(2,1)S(1)}, bf16[512,256]{1,0:T(8,128)(2,1)S(1)}, u32[]{:S(2)}, u32[]{:S(2)}) collective-permute-start(bf16[512,256]{1,0:T(8,128)(2,1)S(1)} %collective-permute-done.13.refs_6_.refs_14_), channel_id=1, source_target_pairs={{0,8},{8,0},{16,24},{24,16},{32,40},{40,32},{48,56},{56,48},{64,72... | collective-permute-start | bytes 786440 | tf_op jit(solution)/shard_map/ppermute | solution.py:38
  63.0 6.3 %collective-permute-start.17 = (bf16[512,256]{1,0:T(8,128)(2,1)S(1)}, bf16[512,256]{1,0:T(8,128)(2,1)S(1)}, u32[]{:S(2)}, u32[]{:S(2)}) collective-permute-start(bf16[512,256]{1,0:T(8,128)(2,1)S(1)} %collective-permute-done.16.refs_10_.refs_18_), channel_id=1, source_target_pairs={{0,8},{8,0},{16,24},{24,16},{32,40},{40,32},{48,56},{56,48},{64,72... | collective-permute-start | bytes 786440 | tf_op jit(solution)/shard_map/ppermute | solution.py:38
  63.4 5.9 %collective-permute-start.19 = (bf16[512,256]{1,0:T(8,128)(2,1)S(1)}, bf16[512,256]{1,0:T(8,128)(2,1)S(1)}, u32[]{:S(2)}, u32[]{:S(2)}) collective-permute-start(bf16[512,256]{1,0:T(8,128)(2,1)S(1)} %collective-permute-done.18.refs_12_.refs_20_), channel_id=1, source_target_pairs={{0,8},{8,0},{16,24},{24,16},{32,40},{40,32},{48,56},{56,48},{64,72... | collective-permute-start | bytes 786440 | tf_op jit(solution)/shard_map/ppermute | solution.py:38
  76.1 8.1 %collective-permute-start.30 = (bf16[16,64,128]{2,1,0:T(8,128)(2,1)}, bf16[16,64,128]{2,1,0:T(8,128)(2,1)S(1)}, u32[]{:S(2)}, u32[]{:S(2)}) collective-permute-start(bf16[16,64,128]{2,1,0:T(8,128)(2,1)} %get-tuple-element.40), channel_id=1, source_target_pairs={{0,48},{8,56},{16,0},{24,8},{32,16},{40,24},{48,32},{56,40},{64,11... | collective-permute-start | bytes 786440 | tf_op jit(solution)/shard_map/ppermute | solution.py:38
  76.2 10.0 %collective-permute-start.31 = (bf16[16,64,128]{2,1,0:T(8,128)(2,1)}, bf16[16,64,128]{2,1,0:T(8,128)(2,1)S(1)}, u32[]{:S(2)}, u32[]{:S(2)}) collective-permute-start(bf16[16,64,128]{2,1,0:T(8,128)(2,1)} %get-tuple-element.41), channel_id=1, source_target_pairs={{0,16},{8,24},{16,32},{24,40},{32,48},{40,56},{48,0},{56,8},{64,80... | collective-permute-start | bytes 786440 | tf_op jit(solution)/shard_map/ppermute | solution.py:38
  77.7 12.6 %collective-permute-start.32 = (bf16[16,64,128]{2,1,0:T(8,128)(2,1)}, bf16[16,64,128]{2,1,0:T(8,128)(2,1)S(1)}, u32[]{:S(2)}, u32[]{:S(2)}) collective-permute-start(bf16[16,64,128]{2,1,0:T(8,128)(2,1)} %get-tuple-element.42), channel_id=1, source_target_pairs={{0,32},{8,40},{16,48},{24,56},{32,0},{40,8},{48,16},{56,24},{64,96... | collective-permute-start | bytes 786440 | tf_op jit(solution)/shard_map/ppermute | solution.py:38
  78.3 12.0 %collective-permute-start.33 = (bf16[16,64,128]{2,1,0:T(8,128)(2,1)}, bf16[16,64,128]{2,1,0:T(8,128)(2,1)S(1)}, u32[]{:S(2)}, u32[]{:S(2)}) collective-permute-start(bf16[16,64,128]{2,1,0:T(8,128)(2,1)} %get-tuple-element.43), channel_id=1, source_target_pairs={{0,192},{8,200},{16,208},{24,216},{32,224},{40,232},{48,240},{56,2... | collective-permute-start | bytes 786440 | tf_op jit(solution)/shard_map/ppermute | solution.py:38
  79.0 11.3 %collective-permute-start.34 = (bf16[16,64,128]{2,1,0:T(8,128)(2,1)}, bf16[16,64,128]{2,1,0:T(8,128)(2,1)S(1)}, u32[]{:S(2)}, u32[]{:S(2)}) collective-permute-start(bf16[16,64,128]{2,1,0:T(8,128)(2,1)} %get-tuple-element.44), channel_id=1, source_target_pairs={{0,64},{8,72},{16,80},{24,88},{32,96},{40,104},{48,112},{56,120},{... | collective-permute-start | bytes 786440 | tf_op jit(solution)/shard_map/ppermute | solution.py:38
  84.2 8.2 %collective-permute-start.35 = (bf16[16,64,128]{2,1,0:T(8,128)(2,1)}, bf16[16,64,128]{2,1,0:T(8,128)(2,1)S(1)}, u32[]{:S(2)}, u32[]{:S(2)}) collective-permute-start(bf16[16,64,128]{2,1,0:T(8,128)(2,1)} %get-tuple-element.45), channel_id=1, source_target_pairs={{0,128},{8,136},{16,144},{24,152},{32,160},{40,168},{48,176},{56,1... | collective-permute-start | bytes 786440 | tf_op jit(solution)/shard_map/ppermute | solution.py:38
  108.0 66.8 %all-to-all-start.1 = ((bf16[32,4,64,128]{3,2,1,0:T(8,128)(2,1)}), bf16[32,4,64,128]{3,2,1,0:T(8,128)(2,1)S(1)}, u32[]{:S(2)}, u32[]{:S(2)}) async-start(bf16[32,4,64,128]{3,2,1,0:T(8,128)(2,1)} %get-tuple-element.55), calls=%async_computation.1 | async-start | bytes 4194304 | tf_op jit(solution)/shard_map/all_to_all | solution.py:429
  115.7 30.6 %collective-permute-start.24 = (bf16[16,64,128]{2,1,0:T(8,128)(2,1)}, bf16[16,64,128]{2,1,0:T(8,128)(2,1)S(1)}, u32[]{:S(2)}, u32[]{:S(2)}) collective-permute-start(bf16[16,64,128]{2,1,0:T(8,128)(2,1)} %get-tuple-element.36), channel_id=1, source_target_pairs={{0,48},{8,56},{16,0},{24,8},{32,16},{40,24},{48,32},{56,40},{64,11... | collective-permute-start | bytes 786440 | tf_op jit(solution)/shard_map/ppermute | solution.py:38
  118.4 30.0 %collective-permute-start.28 = (bf16[16,64,128]{2,1,0:T(8,128)(2,1)S(1)}, bf16[16,64,128]{2,1,0:T(8,128)(2,1)S(1)}, u32[]{:S(2)}, u32[]{:S(2)}) collective-permute-start(bf16[16,64,128]{2,1,0:T(8,128)(2,1)S(1)} %copy-done.18), channel_id=1, source_target_pairs={{0,192},{8,200},{16,208},{24,216},{32,224},{40,232},{48,240},{56,2... | collective-permute-start | bytes 786440 | tf_op jit(solution)/shard_map/ppermute | solution.py:38
  120.8 31.1 %collective-permute-start.22 = (bf16[16,64,128]{2,1,0:T(8,128)(2,1)S(1)}, bf16[16,64,128]{2,1,0:T(8,128)(2,1)S(1)}, u32[]{:S(2)}, u32[]{:S(2)}) collective-permute-start(bf16[16,64,128]{2,1,0:T(8,128)(2,1)S(1)} %copy-done.17), channel_id=1, source_target_pairs={{0,48},{8,56},{16,0},{24,8},{32,16},{40,24},{48,32},{56,40},{64,11... | collective-permute-start | bytes 786440 | tf_op jit(solution)/shard_map/ppermute | solution.py:38
  121.4 33.7 %collective-permute-start.23 = (bf16[16,64,128]{2,1,0:T(8,128)(2,1)S(1)}, bf16[16,64,128]{2,1,0:T(8,128)(2,1)S(1)}, u32[]{:S(2)}, u32[]{:S(2)}) collective-permute-start(bf16[16,64,128]{2,1,0:T(8,128)(2,1)S(1)} %copy-done.16), channel_id=1, source_target_pairs={{0,16},{8,24},{16,32},{24,40},{32,48},{40,56},{48,0},{56,8},{64,80... | collective-permute-start | bytes 786440 | tf_op jit(solution)/shard_map/ppermute | solution.py:38
  122.3 32.8 %collective-permute-start.26 = (bf16[16,64,128]{2,1,0:T(8,128)(2,1)S(1)}, bf16[16,64,128]{2,1,0:T(8,128)(2,1)S(1)}, u32[]{:S(2)}, u32[]{:S(2)}) collective-permute-start(bf16[16,64,128]{2,1,0:T(8,128)(2,1)S(1)} %copy-done.15), channel_id=1, source_target_pairs={{0,192},{8,200},{16,208},{24,216},{32,224},{40,232},{48,240},{56,2... | collective-permute-start | bytes 786440 | tf_op jit(solution)/shard_map/ppermute | solution.py:38
  146.3 8.8 %collective-permute-start.27 = (bf16[16,64,128]{2,1,0:T(8,128)(2,1)S(1)}, bf16[16,64,128]{2,1,0:T(8,128)(2,1)S(1)}, u32[]{:S(2)}, u32[]{:S(2)}) collective-permute-start(bf16[16,64,128]{2,1,0:T(8,128)(2,1)S(1)} %copy-done.14), channel_id=1, source_target_pairs={{0,64},{8,72},{16,80},{24,88},{32,96},{40,104},{48,112},{56,120},{... | collective-permute-start | bytes 786440 | tf_op jit(solution)/shard_map/ppermute | solution.py:38
  148.4 9.0 %collective-permute-start.25 = (bf16[16,64,128]{2,1,0:T(8,128)(2,1)S(1)}, bf16[16,64,128]{2,1,0:T(8,128)(2,1)S(1)}, u32[]{:S(2)}, u32[]{:S(2)}) collective-permute-start(bf16[16,64,128]{2,1,0:T(8,128)(2,1)S(1)} %collective-permute-done.24), channel_id=1, source_target_pairs={{0,48},{8,56},{16,0},{24,8},{32,16},{40,24},{48,32},{56,40},{64,11... | collective-permute-start | bytes 786440 | tf_op jit(solution)/shard_map/ppermute | solution.py:38
  152.0 7.3 %collective-permute-start.29 = (bf16[16,64,128]{2,1,0:T(8,128)(2,1)S(1)}, bf16[16,64,128]{2,1,0:T(8,128)(2,1)S(1)}, u32[]{:S(2)}, u32[]{:S(2)}) collective-permute-start(bf16[16,64,128]{2,1,0:T(8,128)(2,1)S(1)} %collective-permute-done.28), channel_id=1, source_target_pairs={{0,192},{8,200},{16,208},{24,216},{32,224},{40,232},{48,240},{56,2... | collective-permute-start | bytes 786440 | tf_op jit(solution)/shard_map/ppermute | solution.py:38
  176.2 38.0 %all-to-all-start = ((bf16[32,4,64,128]{3,2,1,0:T(8,128)(2,1)}), bf16[32,4,64,128]{3,2,1,0:T(8,128)(2,1)}, u32[]{:S(2)}, u32[]{:S(2)}) async-start(bf16[32,4,64,128]{3,2,1,0:T(8,128)(2,1)} %get-tuple-element.52), calls=%async_computation | async-start | bytes 4194304 | tf_op jit(solution)/shard_map/all_to_all | solution.py:429
  (37 other events, 273.3 us)

commit v2 on v1

v2 whole, which is shorter than its diff:
```python
import math

import jax
import jax.numpy as jnp
from jax import lax
from jax.experimental import pallas as pl
from jax.experimental.pallas import tpu as pltpu
from jax.sharding import PartitionSpec as P

BLK = 64
NSEQ = 32
HD = 128
SEG = 512
POOL = 32
LOG2E = 1.4426950408889634
SCALE = 1.0 / math.sqrt(HD)
QT = 512
KC = 256
SPC = KC // BLK
TILES = 96
COUNT_ROW = 128
TABLE_ROWS = 136


def dot(a, b, dims):
    return lax.dot_general(a, b, (dims, ((), ())), preferred_element_type=jnp.float32)


NN = ((1,), (0,))
NT = ((1,), (1,))
TN = ((0,), (0,))


def iota(shape, dim):
    return lax.broadcasted_iota(jnp.int32, shape, dim)


def flag(cond):
    return jnp.where(cond, 1.0, 0.0)


def prep_kernel(where_ref, rows_ref, table_ref, mask_ref, named_ref, prefix_ref, wanted_ref):
    me = where_ref[0]
    nid = NSEQ * 8
    bf = jnp.bfloat16
    row, col = iota((nid, nid), 0), iota((nid, nid), 1)
    named = row < 0
    for e in range(16):
        named = named | (rows_ref[:, e : e + 1] == col)
    named = flag(named)
    named_ref[...] = named
    pick = flag(iota((NSEQ, nid), 0) == (iota((NSEQ, nid), 1) >> 3))
    wanted = flag(dot(pick.astype(bf), named.astype(bf), NN) > 0.5)
    upto = flag(row <= col)
    upto8 = flag((row <= col) & ((row >> 3) == (col >> 3)))
    prefix = dot(wanted.astype(bf), upto.astype(bf), NN)
    prefix8 = dot(wanted.astype(bf), upto8.astype(bf), NN)
    gid, gw = iota((nid, NSEQ), 0), iota((nid, NSEQ), 1)
    same = (gid >> 3) == gw
    ones = flag(same).astype(bf)
    inner = jnp.where(same, (gid & 7).astype(jnp.float32), 0.0).astype(bf)
    for r in range(2):
        picked = jnp.where(prefix8 == float(r + 1), wanted, 0.0)
        has = dot(picked.astype(bf), ones, NN)
        block = dot(picked.astype(bf), inner, NN)
        place = dot((picked * (prefix - 1.0)).astype(bf), ones, NN)
        table_ref[r * NSEQ : (r + 1) * NSEQ, :] = jnp.where(has > 0.5, block, -1.0).astype(jnp.int32)
        spare = iota((NSEQ, NSEQ), 1) + POOL + NSEQ * r
        table_ref[(2 + r) * NSEQ : (3 + r) * NSEQ, :] = jnp.where(has > 0.5, place.astype(jnp.int32), spare)
    prefix_ref[...] = jnp.where(wanted > 0.5, prefix - 1.0, -1.0)
    wanted_ref[...] = wanted
    spread = flag(iota((8, SEG), 0) == (iota((8, SEG), 1) >> 6))
    ids8, row8 = iota((8, nid), 1), iota((8, nid), 0)
    for h in range(2):
        seg = me if h == 0 else NSEQ - 1 - me
        compact = flag(iota((POOL, nid), 0).astype(jnp.float32) == prefix_ref[pl.ds(seg, 1), :])
        used = jnp.where(ids8 < seg * 8 + row8, named_ref[pl.ds(pl.multiple_of(seg * 8, 8), 8), :], 0.0)
        by_id = dot(used.astype(bf), spread.astype(bf), TN)
        mask_ref[h] = dot(compact.astype(bf), by_id.astype(bf), NN)
        held = jnp.where(iota((1, nid), 1) < seg * 8 + 8, wanted_ref[pl.ds(seg, 1), :], 0.0)
        count = jnp.sum(held, axis=1, keepdims=True)
        table_ref[COUNT_ROW + h : COUNT_ROW + h + 1, :] = jnp.broadcast_to(count, (1, NSEQ)).astype(jnp.int32)


def prep(where, rows):
    return pl.pallas_call(
        prep_kernel,
        name="prep",
        in_specs=[pl.BlockSpec(memory_space=pltpu.SMEM), pl.BlockSpec(memory_space=pltpu.VMEM)],
        out_specs=[pl.BlockSpec(memory_space=pltpu.VMEM)] * 2,
        out_shape=[
            jax.ShapeDtypeStruct((TABLE_ROWS, NSEQ), jnp.int32),
            jax.ShapeDtypeStruct((2, POOL, SEG), jnp.float32),
        ],
        scratch_shapes=[
            pltpu.VMEM((NSEQ * 8, NSEQ * 8), jnp.float32),
            pltpu.VMEM((NSEQ, NSEQ * 8), jnp.float32),
            pltpu.VMEM((NSEQ, NSEQ * 8), jnp.float32),
        ],
        cost_estimate=pl.CostEstimate(flops=10_000_000, bytes_accessed=1 << 20, transcendentals=0),
    )(where, rows)


def tile(index):
    return pl.ds(pl.multiple_of(index * BLK, BLK), BLK)


def select_kernel(where_ref, table_ref, k_ref, v_ref, far_ref, send_ref, sem):
    me = where_ref[0]

    def step(u, _):
        first = u >= me
        reader = jnp.where(first, u, NSEQ - 1 - u)
        writer = jnp.where(first, me, NSEQ - 1 - me)
        for r in range(2):
            rows = tile(jnp.maximum(table_ref[r * NSEQ + reader, writer], 0))

            @pl.when(first)
            def _():
                for kind, ref in ((0, k_ref), (1, v_ref)):
                    pltpu.make_async_copy(ref.at[rows, pl.ds(0, HD)], send_ref.at[u, kind * 2 + r], sem).start()

            @pl.when(jnp.logical_not(first))
            def _():
                for kind in range(2):
                    pltpu.make_async_copy(far_ref.at[kind, rows, :], send_ref.at[u, kind * 2 + r], sem).start()

        return 0

    lax.fori_loop(0, NSEQ, step, 0, unroll=4)
    pltpu.make_async_copy(send_ref, send_ref, sem).wait()


def select(where, table, k, v, far):
    spec = lambda space: pl.BlockSpec(memory_space=space)
    return pl.pallas_call(
        select_kernel,
        name="select",
        in_specs=[spec(pltpu.SMEM)] * 2 + [spec(pltpu.VMEM)] * 3,
        out_specs=spec(pl.ANY),
        out_shape=jax.ShapeDtypeStruct((NSEQ, 4, BLK, HD), jnp.bfloat16),
        scratch_shapes=[pltpu.SemaphoreType.DMA],
        cost_estimate=pl.CostEstimate(flops=1_000_000, bytes_accessed=3 << 20, transcendentals=0),
    )(where, table, k, v, far)


def attend_kernel(where_ref, table_ref, bias_ref, *refs):
    q_ref, do_ref, k_ref, v_ref, far_kv_ref, far_q_ref, mask_ref, got_ref = refs[:8]
    outs, back_ref = refs[8:16], refs[16]
    kt, vt, s_ref, dp_ref, add_ref, dka, dva, dkb, dvb, sems, out_sem = refs[17:]
    me = where_ref[0]
    keys = POOL * BLK
    tiles = (kt, vt)
    segs = (me, NSEQ - 1 - me)

    def fetch(u, _):
        first = u < me
        h = jnp.where(first, 0, 1)
        seg = jnp.where(first, segs[0], segs[1])
        writer = jnp.where(first, u, NSEQ - 1 - u)

        @pl.when(u != me)
        def _():
            for r in range(2):
                at = tile(h * TILES + table_ref[(2 + r) * NSEQ + seg, writer])
                for kind in range(2):
                    pltpu.make_async_copy(
                        got_ref.at[u, kind * 2 + r], tiles[kind].at[at, :], sems.at[kind]
                    ).start()

        return 0

    lax.fori_loop(0, NSEQ, fetch, 0, unroll=4)
    heads = []
    for h in range(2):
        if h == 0:
            lanes = slice(0, HD)
            q, do, k, v = (r.at[:, lanes] for r in (q_ref, do_ref, k_ref, v_ref))
        else:
            q, do, k, v = far_q_ref.at[0], far_q_ref.at[1], far_kv_ref.at[0], far_kv_ref.at[1]
        heads.append((q, do, k, v))
        held = table_ref[COUNT_ROW + h, 0]
        for r in range(2):
            rows = tile(jnp.maximum(table_ref[r * NSEQ + segs[h], segs[h]], 0))
            at = tile(h * TILES + table_ref[(2 + r) * NSEQ + segs[h], segs[h]])
            kt[at, :] = k[rows, :]
            vt[at, :] = v[rows, :]

        def clear(i, _):
            at = tile(h * TILES + i)
            kt[at, :] = jnp.zeros((BLK, HD), jnp.bfloat16)
            vt[at, :] = jnp.zeros((BLK, HD), jnp.bfloat16)
            return 0

        lax.fori_loop(held, (held + SPC - 1) // SPC * SPC, clear, 0)
        for i in range(POOL // SPC):
            add_ref[h, i] = jnp.where(mask_ref[h, i * SPC : (i + 1) * SPC, :] > 0.5, bias_ref[h] * LOG2E, -1e30)
    for kind in range(2):
        most = tiles[kind].at[pl.ds(0, 2 * (NSEQ - 1) * BLK), :]
        pltpu.make_async_copy(most, most, sems.at[kind]).wait()

    def fold(value, op):
        return op(value.reshape(KC // 8, 8, QT), axis=0)

    for h in range(2):
        q, do, k, v = heads[h]
        att_ref, gq_ref, dkl_ref, dvl_ref = outs[h * 4 : h * 4 + 4]
        steps = (table_ref[COUNT_ROW + h, 0] + SPC - 1) // SPC
        qc, doc = q[...], do[...]

        def chunk(i):
            return pl.ds(pl.multiple_of(i * KC, KC), KC)

        def held_chunk(i):
            return pl.ds(pl.multiple_of(h * TILES * BLK + i * KC, KC), KC)

        def mem_score(i, top):
            score = dot(kt[held_chunk(i), :], qc, NT) * (SCALE * LOG2E)
            add = add_ref[h, i]
            score = (score.reshape(SPC, BLK, QT) + add[:, None, :]).reshape(KC, QT)
            s_ref[chunk(i), :] = score
            return jnp.maximum(top, fold(score, jnp.max))

        top = jnp.full((8, QT), -1e30, jnp.float32)
        for n in range(SEG // KC):
            score = dot(k[n * KC : (n + 1) * KC, :], qc, NT) * (SCALE * LOG2E)
            score = jnp.where(iota((KC, QT), 0) + n * KC <= iota((KC, QT), 1), score, -1e30)
            s_ref[keys + n * KC : keys + (n + 1) * KC, :] = score
            top = jnp.maximum(top, fold(score, jnp.max))
        top = lax.fori_loop(0, steps, mem_score, top)
        top = jnp.max(top, axis=0, keepdims=True)

        def weigh(i, mass):
            e = jnp.exp2(s_ref[chunk(i), :] - top)
            s_ref[chunk(i), :] = e
            return mass + fold(e, jnp.sum)

        mass = lax.fori_loop(0, steps, weigh, jnp.zeros((8, QT), jnp.float32))
        mass = lax.fori_loop(POOL // SPC, POOL // SPC + SEG // KC, weigh, mass)
        inv = 1.0 / jnp.sum(mass, axis=0, keepdims=True)

        def forward(at, vc, carry):
            out, delta = carry
            p = s_ref[at, :] * inv
            s_ref[at, :] = p
            w = p.astype(jnp.bfloat16)
            out = out + dot(vc, w, TN)
            dp = dot(vc, doc, NT)
            dp_ref[at, :] = dp
            return dot(w, doc, NN), (out, delta + fold(p * dp, jnp.sum))

        def backward(at, kc, dq):
            ds = (s_ref[at, :] * (dp_ref[at, :] - delta) * SCALE).astype(jnp.bfloat16)
            return dot(ds, qc, NN), dq + dot(kc, ds, TN)

        def mem_forward(i, carry):
            dva[chunk(i), :], carry = forward(chunk(i), vt[held_chunk(i), :], carry)
            return carry

        def mem_backward(i, dq):
            dka[chunk(i), :], dq = backward(chunk(i), kt[held_chunk(i), :], dq)
            return dq

        carry = (jnp.zeros((HD, QT), jnp.float32), jnp.zeros((8, QT), jnp.float32))
        carry = lax.fori_loop(0, steps, mem_forward, carry)
        for n in range(SEG // KC):
            rows = slice(n * KC, (n + 1) * KC)
            at = slice(keys + n * KC, keys + (n + 1) * KC)
            dvl_ref[rows, :], carry = forward(at, v[rows, :], carry)
        out, delta = carry
        delta = jnp.sum(delta, axis=0, keepdims=True)
        att_ref[...] = out.T.astype(jnp.bfloat16)
        dq = lax.fori_loop(0, steps, mem_backward, jnp.zeros((HD, QT), jnp.float32))
        for n in range(SEG // KC):
            rows = slice(n * KC, (n + 1) * KC)
            at = slice(keys + n * KC, keys + (n + 1) * KC)
            dkl_ref[rows, :], dq = backward(at, k[rows, :], dq)
        gq_ref[...] = dq.T.astype(jnp.bfloat16)

        def pack(i, _):
            dkb[h, chunk(i), :] = dka[chunk(i), :].astype(jnp.bfloat16)
            dvb[h, chunk(i), :] = dva[chunk(i), :].astype(jnp.bfloat16)
            return 0

        lax.fori_loop(0, steps, pack, 0)
        for r in range(2):
            block = table_ref[r * NSEQ + segs[h], segs[h]]

            @pl.when(block >= 0)
            def _():
                rows, at = tile(block), tile(table_ref[(2 + r) * NSEQ + segs[h], segs[h]])
                dkl_ref[rows, :] += dkb[h, at, :].astype(jnp.float32)
                dvl_ref[rows, :] += dvb[h, at, :].astype(jnp.float32)

        def put(u, _):
            writer = u if h == 0 else NSEQ - 1 - u
            for r in range(2):
                at = tile(jnp.minimum(table_ref[(2 + r) * NSEQ + segs[h], writer], POOL - 1))
                for kind, ref in ((0, dkb), (1, dvb)):
                    pltpu.make_async_copy(ref.at[h, at, :], back_ref.at[u, kind * 2 + r], out_sem).start()
            return 0

        lax.fori_loop(*((0, me + 1) if h == 0 else (me + 1, NSEQ)), put, 0)
    pltpu.make_async_copy(back_ref, back_ref, out_sem).wait()


def attend(where, table, bias, q, do, k, v, far_kv, far_q, mask, got):
    bf, f32, vm, hbm, sm = jnp.bfloat16, jnp.float32, pltpu.VMEM, pl.ANY, pltpu.SMEM
    spec = lambda space: pl.BlockSpec(memory_space=space)
    keys = POOL * BLK
    each = [jax.ShapeDtypeStruct((SEG, HD), d) for d in (bf, bf, f32, f32)]
    return pl.pallas_call(
        attend_kernel,
        name="attend",
        in_specs=[spec(sm)] * 3 + [spec(vm)] * 7 + [spec(hbm)],
        out_specs=[spec(vm)] * 8 + [spec(hbm)],
        out_shape=each * 2 + [jax.ShapeDtypeStruct((NSEQ, 4, BLK, HD), bf)],
        scratch_shapes=[
            pltpu.VMEM((2 * TILES * BLK, HD), bf),
            pltpu.VMEM((2 * TILES * BLK, HD), bf),
            pltpu.VMEM((keys + SEG, QT), f32),
            pltpu.VMEM((keys + SEG, QT), f32),
            pltpu.VMEM((2, POOL // SPC, SPC, SEG), f32),
            pltpu.VMEM((keys, HD), f32),
            pltpu.VMEM((keys, HD), f32),
            pltpu.VMEM((2, keys, HD), bf),
            pltpu.VMEM((2, keys, HD), bf),
            pltpu.SemaphoreType.DMA((2,)),
            pltpu.SemaphoreType.DMA,
        ],
        cost_estimate=pl.CostEstimate(flops=16_000_000_000, bytes_accessed=8 << 20, transcendentals=1_500_000),
    )(where, table, bias, q, do, k, v, far_kv, far_q, mask, got)


def settle_kernel(where_ref, table_ref, *refs):
    locals_, back_ref = refs[:4], refs[4]
    gk_ref, gv_ref, far_ref, acc = refs[5:]
    me = where_ref[0]
    for i in range(4):
        acc[i] = locals_[i][...]

    def step(u, _):
        first = u > me
        h = jnp.where(first, 0, 1)
        reader = jnp.where(first, u, NSEQ - 1 - u)
        writer = jnp.where(first, me, NSEQ - 1 - me)
        for r in range(2):
            block = table_ref[r * NSEQ + reader, writer]

            @pl.when((block >= 0) & (u != me))
            def _():
                for kind in range(2):
                    acc[h * 2 + kind, tile(block), :] += back_ref[u, kind * 2 + r].astype(jnp.float32)

        return 0

    lax.fori_loop(0, NSEQ, step, 0)
    gk_ref[...] = acc[0].astype(jnp.bfloat16)
    gv_ref[...] = acc[1].astype(jnp.bfloat16)
    far_ref[...] = acc[2:4].astype(jnp.bfloat16)


def settle(where, table, parts, back):
    spec = lambda space: pl.BlockSpec(memory_space=space)
    return pl.pallas_call(
        settle_kernel,
        name="settle",
        in_specs=[spec(pltpu.SMEM)] * 2 + [spec(pltpu.VMEM)] * 5,
        out_specs=[spec(pltpu.VMEM)] * 3,
        out_shape=[jax.ShapeDtypeStruct((SEG, HD), jnp.bfloat16)] * 2
        + [jax.ShapeDtypeStruct((2, SEG, HD), jnp.bfloat16)],
        scratch_shapes=[pltpu.VMEM((4, SEG, HD), jnp.float32)],
        cost_estimate=pl.CostEstimate(flops=2_000_000, bytes_accessed=3 << 20, transcendentals=0),
    )(where, table, *parts, back)


def mirror(first, second):
    pairs = [(i, NSEQ - 1 - i) for i in range(NSEQ)]
    return lax.ppermute(jnp.stack([first, second]), "seq", pairs)


def exchange(value):
    return lax.all_to_all(value, "seq", split_axis=0, concat_axis=0, tiled=True)


def layer(queries, keys, values, grad_out, retrieved, mem_bias):
    where = lax.axis_index("seq").astype(jnp.int32).reshape(1)
    devices = lax.axis_size("seq") * lax.axis_size("head")
    far_kv = mirror(keys[:, HD:], values[:, HD:])
    copies = jnp.broadcast_to(retrieved, (devices, *retrieved.shape))
    lists = lax.all_to_all(copies, ("seq", "head"), split_axis=0, concat_axis=0, tiled=True)
    far_q = mirror(queries[:, HD:], grad_out[:, HD:])
    table, mask = prep(where, lists.reshape(devices, 16))
    send = select(where, table, keys, values, far_kv)
    got = exchange(send)
    att, gq, dkl, dvl, far_att, far_gq, far_dkl, far_dvl, back = attend(
        where, table, mem_bias, queries, grad_out, keys, values, far_kv, far_q, mask, got
    )
    home = mirror(far_att, far_gq)
    attended = jnp.concatenate([att, home[0]], axis=1)
    grad_queries = jnp.concatenate([gq, home[1]], axis=1)
    back = exchange(back)
    gk, gv, far = settle(where, table, (dkl, dvl, far_dkl, far_dvl), back)
    far = lax.ppermute(far, "seq", [(i, NSEQ - 1 - i) for i in range(NSEQ)])
    grad_keys = jnp.concatenate([gk, far[0]], axis=1)
    grad_values = jnp.concatenate([gv, far[1]], axis=1)
    return attended, grad_queries, grad_keys, grad_values


def solution(mesh):
    whole = P("seq", "head")
    return jax.shard_map(
        layer,
        mesh=mesh,
        in_specs=(whole, whole, whole, whole, P(("seq", "head"), None), P("head")),
        out_specs=(whole, whole, whole, whole),
        check_vma=False,
    )
```

time: 220 us -> 149 us (0.68)
  starting transfers between devices: 76.7 us -> 37.1 us
  Pallas kernels: 47.2 us -> 28.3 us
  waiting for transfers between devices: 83.2 us -> 72.9 us
    ppermute x36 -> x4, starting transfers between devices: 59.7 us -> 19 us  [the longest x3 16.8 us: mirror(): return lax.ppermute(jnp.stack([first, second]), 'seq', pairs)]
    ppermute x36 -> x4, waiting for transfers between devices: 58.9 us -> 36.5 us  [the longest x3 28.7 us: mirror(): return lax.ppermute(jnp.stack([first, second]), 'seq', pairs)]
    pallas_call x4 -> x2, Pallas kernels: 38.5 us -> 21.8 us  [the longest x1 17.8 us: attend(): pl.pallas_call(attend_kernel, name='attend', in_specs=[spec(sm)] * 3 + [s...]
    all_to_all x2 -> x3, waiting for transfers between devices: 24.4 us -> 36.3 us  [the longest x2 23.4 us: exchange(): return lax.all_to_all(value, 'seq', split_axis=0, concat_axis=0, tiled=True)]
    pallas_call x1, Pallas kernels: 5.78 us -> 3.29 us  [select(): pl.pallas_call(select_kernel, name='select', in_specs=[spec(pltpu.SMEM)]...]
    all_to_all x2 -> x3, starting transfers between devices: 17 us -> 18.1 us  [the longest x1 9.48 us: layer(): lax.all_to_all(copies, ('seq', 'head'), split_axis=0, concat_axis=0, tile...]
  transfers between devices with their start and end apart: 38 -> 7, of which waited for: 17 -> 4; matrix products, arithmetic and copies ran while one was open for 2% -> 2% of each run, Pallas kernels for 10% -> 5%
where the time goes in v2:
time: 149 us
  waiting for transfers between devices  72.9 us (49%)
  starting transfers between devices  37.1 us (25%)
  Pallas kernels  28.3 us (19%)
  local copies, waits for them, and re-layouts  6.58 us (4%)
  other arithmetic  3.03 us (2%)
    ppermute x3, waiting for transfers between devices, mirror(): return lax.ppermute(jnp.stack([first, second]), 'seq', pairs)  28.7 us
    all_to_all x2, waiting for transfers between devices, exchange(): return lax.all_to_all(value, 'seq', split_axis=0, concat_axis=0, tiled=True)  23.4 us
    pallas_call x1, Pallas kernels, attend(): pl.pallas_call(attend_kernel, name='attend', in_specs=[spec(sm)] * 3 + [s...  17.8 us
    ppermute x3, starting transfers between devices, mirror(): return lax.ppermute(jnp.stack([first, second]), 'seq', pairs)  16.8 us
    all_to_all x1, waiting for transfers between devices, layer(): lax.all_to_all(copies, ('seq', 'head'), split_axis=0, concat_axis=0, tile...  13 us
    all_to_all x1, starting transfers between devices, layer(): lax.all_to_all(copies, ('seq', 'head'), split_axis=0, concat_axis=0, tile...  9.48 us
    all_to_all x2, starting transfers between devices, exchange(): return lax.all_to_all(value, 'seq', split_axis=0, concat_axis=0, tiled=True)  8.57 us
    ppermute x1, waiting for transfers between devices, layer(): far = lax.ppermute(far, 'seq', [(i, NSEQ - 1 - i) for i in range(NSEQ)])  7.83 us
  transfers between devices with their start and end apart: 7, of which 4 were waited for; matrix products, arithmetic and copies ran while one was open for 2% of the time, Pallas kernels for 5%

profile of v2, /device:TPU:1, one launch (start us, length us, event | category | flops | bytes accessed | tf_op | source)
XLA Modules:
  0.0 148.7 jit_solution(15867675205288369850)
XLA Ops:
  0.6 1.0 slice_bitcast_fusion.6
  1.7 6.4 %collective-permute-start = (bf16[2,512,128]{2,1,0:T(8,128)(2,1)S(1)}, bf16[2,512,128]{2,1,0:T(8,128)(2,1)S(1)}, u32[]{:S(2)}, u32[]{:S(2)}) collective-permute-start(bf16[2,512,128]{2,1,0:T(8,128)(2,1)S(1)} %pad_maximum_fusion), channel_id=1, source_target_pairs={{0,248},{8,240},{16,232},{24,224},{32,216},{40,208},{48,200},{56,1... | collective-permute-start | bytes 786440 | tf_op jit(solution)/shard_map/ppermute | solution.py:379
  8.1 1.4 broadcast_in_dim.3
  9.4 9.5 %all-to-all-start = ((s32[256,1,16]{2,1,0:T(1,128)}), s32[256,1,16]{2,1,0:T(1,128)S(1)}, u32[]{:S(2)}, u32[]{:S(2)}) async-start(s32[256,1,16]{2,1,0:T(1,128)} %broadcast_in_dim.3), calls=%async_computation | async-start | bytes 262144 | tf_op jit(solution)/shard_map/all_to_all | solution.py:391
  18.9 13.0 %all-to-all-done = s32[256,1,16]{2,1,0:T(1,128)S(1)} async-done(((s32[256,1,16]{2,1,0:T(1,128)}), s32[256,1,16]{2,1,0:T(1,128)S(1)}, u32[]{:S(2)}, u32[]{:S(2)}) %all-to-all-start) | async-done | bytes 16416 | tf_op jit(solution)/shard_map/all_to_all | solution.py:391
  31.9 0.7 copy-done.2
  32.5 3.3 %prep.1 = (s32[136,32]{1,0:T(8,128)}, f32[2,32,512]{2,1,0:T(8,128)}) custom-call(s32[1]{0:T(128)} %bitcast.where_ref, s32[256,16]{1,0:T(8,128)} %bitcast.21), custom_call_target="tpu_custom_call" | custom-call | flops 10000000 | bytes 1048576 | tf_op jit(solution)/shard_map/prep/pallas_call | solution.py:86
  35.8 0.0 collective-permute-done.far_ref.refs_4_
  35.9 0.7 copy-done.3
  36.6 3.3 %select.1 = bf16[32,4,64,128]{3,2,1,0:T(8,128)(2,1)} custom-call(s32[1]{0:T(128)} %bitcast.where_ref, s32[136,32]{1,0:T(8,128)} %get-tuple-element.18.table_ref, bf16[512,256]{1,0:T(8,128)(2,1)} %refs_2_.1, bf16[512,256]{1,0:T(8,128)(2,1)} %refs_3_.1, bf16[2,512,128]{2,1,0:T(8,128)(2,1)} %copy-done.3), custom_call_target="tpu_custom_call" | custom-call | flops 1000000 | bytes 3145728 | tf_op jit(solution)/shard_map/select/pallas_call | solution.py:136
  39.8 0.0 copy-start.10
  39.9 0.0 copy-start.11
  39.9 4.3 %all-to-all-start.1 = ((bf16[32,4,64,128]{3,2,1,0:T(8,128)(2,1)}), bf16[32,4,64,128]{3,2,1,0:T(8,128)(2,1)S(1)}, u32[]{:S(2)}, u32[]{:S(2)}) async-start(bf16[32,4,64,128]{3,2,1,0:T(8,128)(2,1)} %select.1), calls=%async_computation.1 | async-start | bytes 4194304 | tf_op jit(solution)/shard_map/all_to_all | solution.py:383
  44.2 0.0 copy-done.10
  44.3 5.2 %collective-permute-start.1 = (bf16[2,512,128]{2,1,0:T(8,128)(2,1)S(1)}, bf16[2,512,128]{2,1,0:T(8,128)(2,1)S(1)}, u32[]{:S(2)}, u32[]{:S(2)}) collective-permute-start(bf16[2,512,128]{2,1,0:T(8,128)(2,1)S(1)} %pad_maximum_fusion.1), channel_id=1, source_target_pairs={{0,248},{8,240},{16,232},{24,224},{32,216},{40,208},{48,200},{56,1... | collective-permute-start | bytes 786440 | tf_op jit(solution)/shard_map/ppermute | solution.py:379
  49.5 28.7 %collective-permute-done.1.refs_5_ = bf16[2,512,128]{2,1,0:T(8,128)(2,1)S(1)} collective-permute-done((bf16[2,512,128]{2,1,0:T(8,128)(2,1)S(1)}, bf16[2,512,128]{2,1,0:T(8,128)(2,1)S(1)}, u32[]{:S(2)}, u32[]{:S(2)}) %collective-permute-start.1) | collective-permute-done | bytes 262176 | tf_op jit(solution)/shard_map/ppermute | solution.py:379
  78.2 0.0 all-to-all-done.1.refs_7_
  78.2 0.7 copy-done.12
  78.9 0.7 copy-done.1
  79.7 17.8 %attend.1 = (bf16[512,128]{1,0:T(8,128)(2,1)}, bf16[512,128]{1,0:T(8,128)(2,1)}, f32[512,128]{1,0:T(8,128)}, f32[512,128]{1,0:T(8,128)}, bf16[512,128]{1,0:T(8,1...) custom-call(s32[1]{0:T(128)} %bitcast.where_ref, ...), custom_call_target="tpu_custom_call" | custom-call | flops 16000000000 | bytes 8388608 | tf_op jit(solution)/shard_map/attend/pallas_call | solution.py:312
  97.5 4.2 %all-to-all-start.2 = ((bf16[32,4,64,128]{3,2,1,0:T(8,128)(2,1)}), bf16[32,4,64,128]{3,2,1,0:T(8,128)(2,1)S(1)}, u32[]{:S(2)}, u32[]{:S(2)}) async-start(bf16[32,4,64,128]{3,2,1,0:T(8,128)(2,1)} %get-tuple-element.28), calls=%async_computation.2 | async-start | bytes 4194304 | tf_op jit(solution)/shard_map/all_to_all | solution.py:383
  101.8 5.1 %collective-permute-start.2 = (bf16[2,512,128]{2,1,0:T(8,128)(2,1)S(1)}, bf16[2,512,128]{2,1,0:T(8,128)(2,1)S(1)}, u32[]{:S(2)}, u32[]{:S(2)}) collective-permute-start(bf16[2,512,128]{2,1,0:T(8,128)(2,1)S(1)} %pad_maximum_fusion.2), channel_id=1, source_target_pairs={{0,248},{8,240},{16,232},{24,224},{32,216},{40,208},{48,200},{56,1... | collective-permute-start | bytes 786440 | tf_op jit(solution)/shard_map/ppermute | solution.py:379
  106.9 23.4 %all-to-all-done.2.refs_4_ = bf16[32,4,64,128]{3,2,1,0:T(8,128)(2,1)S(1)} async-done(((bf16[32,4,64,128]{3,2,1,0:T(8,128)(2,1)}), bf16[32,4,64,128]{3,2,1,0:T(8,128)(2,1)S(1)}, u32[]{:S(2)}, u32[]{:S(2)}) %all-to-all-start.2) | async-done | bytes 2097184 | tf_op jit(solution)/shard_map/all_to_all | solution.py:383
  130.3 1.3 copy-done
  131.6 4.0 %settle.1 = (bf16[512,128]{1,0:T(8,128)(2,1)}, bf16[512,128]{1,0:T(8,128)(2,1)}, bf16[2,512,128]{2,1,0:T(8,128)(2,1)}) custom-call(s32[1]{0:T(128)} %bitcast.where_ref, s32[136,32]{1,0:T(8,128)} %get-tuple-element.18.table_ref, f32[512,128]{1,0:T(8,128)} %get-tuple-element.24.refs_0_, f32[512,128]{1,0:T(8,128)} %get-tuple-element.25.refs_1_, ...), custom_call_target="tpu_custom_call" | custom-call | flops 2000000 | bytes 3145728 | tf_op jit(solution)/shard_map/settle/pallas_call | solution.py:365
  135.6 2.3 %collective-permute-start.3 = (bf16[2,512,128]{2,1,0:T(8,128)(2,1)}, bf16[2,512,128]{2,1,0:T(8,128)(2,1)S(1)}, u32[]{:S(2)}, u32[]{:S(2)}) collective-permute-start(bf16[2,512,128]{2,1,0:T(8,128)(2,1)} %get-tuple-element.30), channel_id=1, source_target_pairs={{0,248},{8,240},{16,232},{24,224},{32,216},{40,208},{48,200},{56,1... | collective-permute-start | bytes 786440 | tf_op jit(solution)/shard_map/ppermute | solution.py:404
  137.9 0.0 collective-permute-done.2
  137.9 0.7 pad_maximum_fusion.4
  138.7 0.7 pad_maximum_fusion.3
  139.4 7.8 %collective-permute-done.3 = bf16[2,512,128]{2,1,0:T(8,128)(2,1)S(1)} collective-permute-done((bf16[2,512,128]{2,1,0:T(8,128)(2,1)}, bf16[2,512,128]{2,1,0:T(8,128)(2,1)S(1)}, u32[]{:S(2)}, u32[]{:S(2)}) %collective-permute-start.3) | collective-permute-done | bytes 262176 | tf_op jit(solution)/shard_map/ppermute | solution.py:404
  147.3 0.7 pad_maximum_fusion.6
  148.0 0.7 pad_maximum_fusion.5
  (24 shorter events, 0.2 us)
Async XLA Ops:
  1.7 34.2 %collective-permute-start = (bf16[2,512,128]{2,1,0:T(8,128)(2,1)S(1)}, bf16[2,512,128]{2,1,0:T(8,128)(2,1)S(1)}, u32[]{:S(2)}, u32[]{:S(2)}) collective-permute-start(bf16[2,512,128]{2,1,0:T(8,128)(2,1)S(1)} %pad_maximum_fusion), channel_id=1, source_target_pairs={{0,248},{8,240},{16,232},{24,224},{32,216},{40,208},{48,200},{56,1... | collective-permute-start | bytes 786440 | tf_op jit(solution)/shard_map/ppermute | solution.py:379
  9.4 22.5 %all-to-all-start = ((s32[256,1,16]{2,1,0:T(1,128)}), s32[256,1,16]{2,1,0:T(1,128)S(1)}, u32[]{:S(2)}, u32[]{:S(2)}) async-start(s32[256,1,16]{2,1,0:T(1,128)} %broadcast_in_dim.3), calls=%async_computation | async-start | bytes 262144 | tf_op jit(solution)/shard_map/all_to_all | solution.py:391
  31.9 0.7 copy-start.2
  35.8 0.7 copy-start.3
  39.8 4.4 %copy-start.10 = (bf16[512,256]{1,0:T(8,128)(2,1)S(1)}, bf16[512,256]{1,0:T(8,128)(2,1)}, u32[]{:S(2)}) copy-start(bf16[512,256]{1,0:T(8,128)(2,1)} %refs_0_.1) | copy-start | bytes 786436
  39.9 4.4 %copy-start.11 = (bf16[512,256]{1,0:T(8,128)(2,1)S(1)}, bf16[512,256]{1,0:T(8,128)(2,1)}, u32[]{:S(2)}) copy-start(bf16[512,256]{1,0:T(8,128)(2,1)} %refs_1_.1) | copy-start | bytes 786436
  39.9 38.4 %all-to-all-start.1 = ((bf16[32,4,64,128]{3,2,1,0:T(8,128)(2,1)}), bf16[32,4,64,128]{3,2,1,0:T(8,128)(2,1)S(1)}, u32[]{:S(2)}, u32[]{:S(2)}) async-start(bf16[32,4,64,128]{3,2,1,0:T(8,128)(2,1)} %select.1), calls=%async_computation.1 | async-start | bytes 4194304 | tf_op jit(solution)/shard_map/all_to_all | solution.py:383
  44.3 33.9 %collective-permute-start.1 = (bf16[2,512,128]{2,1,0:T(8,128)(2,1)S(1)}, bf16[2,512,128]{2,1,0:T(8,128)(2,1)S(1)}, u32[]{:S(2)}, u32[]{:S(2)}) collective-permute-start(bf16[2,512,128]{2,1,0:T(8,128)(2,1)S(1)} %pad_maximum_fusion.1), channel_id=1, source_target_pairs={{0,248},{8,240},{16,232},{24,224},{32,216},{40,208},{48,200},{56,1... | collective-permute-start | bytes 786440 | tf_op jit(solution)/shard_map/ppermute | solution.py:379
  78.2 0.7 copy-start.12
  78.2 1.4 copy-start.1
  97.5 4.3 %copy-start.8 = (bf16[512,128]{1,0:T(8,128)(2,1)S(1)}, bf16[512,128]{1,0:T(8,128)(2,1)}, u32[]{:S(2)}) copy-start(bf16[512,128]{1,0:T(8,128)(2,1)} %get-tuple-element.21) | copy-start | bytes 393220
  97.5 4.3 %copy-start.9 = (bf16[512,128]{1,0:T(8,128)(2,1)S(1)}, bf16[512,128]{1,0:T(8,128)(2,1)}, u32[]{:S(2)}) copy-start(bf16[512,128]{1,0:T(8,128)(2,1)} %get-tuple-element.22) | copy-start | bytes 393220
  97.5 32.8 %all-to-all-start.2 = ((bf16[32,4,64,128]{3,2,1,0:T(8,128)(2,1)}), bf16[32,4,64,128]{3,2,1,0:T(8,128)(2,1)S(1)}, u32[]{:S(2)}, u32[]{:S(2)}) async-start(bf16[32,4,64,128]{3,2,1,0:T(8,128)(2,1)} %get-tuple-element.28), calls=%async_computation.2 | async-start | bytes 4194304 | tf_op jit(solution)/shard_map/all_to_all | solution.py:383
  101.7 36.2 %copy-start.5 = (bf16[512,128]{1,0:T(8,128)(2,1)S(1)}, bf16[512,128]{1,0:T(8,128)(2,1)}, u32[]{:S(2)}) copy-start(bf16[512,128]{1,0:T(8,128)(2,1)} %get-tuple-element.23) | copy-start | bytes 393220
  101.8 36.1 %collective-permute-start.2 = (bf16[2,512,128]{2,1,0:T(8,128)(2,1)S(1)}, bf16[2,512,128]{2,1,0:T(8,128)(2,1)S(1)}, u32[]{:S(2)}, u32[]{:S(2)}) collective-permute-start(bf16[2,512,128]{2,1,0:T(8,128)(2,1)S(1)} %pad_maximum_fusion.2), channel_id=1, source_target_pairs={{0,248},{8,240},{16,232},{24,224},{32,216},{40,208},{48,200},{56,1... | collective-permute-start | bytes 786440 | tf_op jit(solution)/shard_map/ppermute | solution.py:379
  130.3 1.3 copy-start
  131.6 7.1 %copy-start.4 = (bf16[512,128]{1,0:T(8,128)(2,1)S(1)}, bf16[512,128]{1,0:T(8,128)(2,1)}, u32[]{:S(2)}) copy-start(bf16[512,128]{1,0:T(8,128)(2,1)} %get-tuple-element.20) | copy-start | bytes 393220
  135.6 11.7 %copy-start.7 = (bf16[512,128]{1,0:T(8,128)(2,1)S(1)}, bf16[512,128]{1,0:T(8,128)(2,1)}, u32[]{:S(2)}) copy-start(bf16[512,128]{1,0:T(8,128)(2,1)} %get-tuple-element.31) | copy-start | bytes 393220
  135.6 12.4 %copy-start.6 = (bf16[512,128]{1,0:T(8,128)(2,1)S(1)}, bf16[512,128]{1,0:T(8,128)(2,1)}, u32[]{:S(2)}) copy-start(bf16[512,128]{1,0:T(8,128)(2,1)} %get-tuple-element.29) | copy-start | bytes 393220
  135.6 11.6 %collective-permute-start.3 = (bf16[2,512,128]{2,1,0:T(8,128)(2,1)}, bf16[2,512,128]{2,1,0:T(8,128)(2,1)S(1)}, u32[]{:S(2)}, u32[]{:S(2)}) collective-permute-start(bf16[2,512,128]{2,1,0:T(8,128)(2,1)} %get-tuple-element.30), channel_id=1, source_target_pairs={{0,248},{8,240},{16,232},{24,224},{32,216},{40,208},{48,200},{56,1... | collective-permute-start | bytes 786440 | tf_op jit(solution)/shard_map/ppermute | solution.py:404

commit v3 on v2

--- a/solution.py
+++ b/solution.py
@@ -6,6 +6,7 @@
 from jax.experimental import pallas as pl
 from jax.experimental.pallas import tpu as pltpu
 from jax.sharding import PartitionSpec as P
+
 
 BLK = 64
 NSEQ = 32
@@ -18,6 +19,8 @@
 KC = 256
 SPC = KC // BLK
 TILES = 96
+PARTS = 8
+VMEM_SETTLE = 16 << 20
 COUNT_ROW = 128
 TABLE_ROWS = 136
 
@@ -39,36 +42,66 @@
     return jnp.where(cond, 1.0, 0.0)
 
 
-def prep_kernel(where_ref, rows_ref, table_ref, mask_ref, named_ref, prefix_ref, wanted_ref):
+def tile(index):
+    return pl.ds(pl.multiple_of(index * BLK, BLK), BLK)
+
+
+def select_kernel(where_ref, rows_ref, upto_ref, upto8_ref, k_ref, v_ref, far_ref, *refs):
+    table_ref, mask_ref, send_ref, table, named_ref, prefix_ref, wanted_ref, table_sem, sem = refs
     me = where_ref[0]
     nid = NSEQ * 8
     bf = jnp.bfloat16
-    row, col = iota((nid, nid), 0), iota((nid, nid), 1)
-    named = row < 0
+    col = iota((nid, nid), 1)
+    named = col < 0
     for e in range(16):
         named = named | (rows_ref[:, e : e + 1] == col)
     named = flag(named)
     named_ref[...] = named
     pick = flag(iota((NSEQ, nid), 0) == (iota((NSEQ, nid), 1) >> 3))
     wanted = flag(dot(pick.astype(bf), named.astype(bf), NN) > 0.5)
-    upto = flag(row <= col)
-    upto8 = flag((row <= col) & ((row >> 3) == (col >> 3)))
-    prefix = dot(wanted.astype(bf), upto.astype(bf), NN)
-    prefix8 = dot(wanted.astype(bf), upto8.astype(bf), NN)
+    prefix = dot(wanted.astype(bf), upto_ref[...], NN)
+    prefix8 = dot(wanted.astype(bf), upto8_ref[...], NN)
     gid, gw = iota((nid, NSEQ), 0), iota((nid, NSEQ), 1)
     same = (gid >> 3) == gw
     ones = flag(same).astype(bf)
     inner = jnp.where(same, (gid & 7).astype(jnp.float32), 0.0).astype(bf)
+    places = []
     for r in range(2):
         picked = jnp.where(prefix8 == float(r + 1), wanted, 0.0)
         has = dot(picked.astype(bf), ones, NN)
         block = dot(picked.astype(bf), inner, NN)
+        table_ref[r * NSEQ : (r + 1) * NSEQ, :] = jnp.where(has > 0.5, block, -1.0).astype(jnp.int32)
+        places.append((picked, has))
+    to_smem = pltpu.make_async_copy(table_ref.at[pl.ds(0, 2 * NSEQ), :], table, table_sem)
+    to_smem.start()
+    for r, (picked, has) in enumerate(places):
         place = dot((picked * (prefix - 1.0)).astype(bf), ones, NN)
-        table_ref[r * NSEQ : (r + 1) * NSEQ, :] = jnp.where(has > 0.5, block, -1.0).astype(jnp.int32)
         spare = iota((NSEQ, NSEQ), 1) + POOL + NSEQ * r
         table_ref[(2 + r) * NSEQ : (3 + r) * NSEQ, :] = jnp.where(has > 0.5, place.astype(jnp.int32), spare)
     prefix_ref[...] = jnp.where(wanted > 0.5, prefix - 1.0, -1.0)
     wanted_ref[...] = wanted
+    to_smem.wait()
+
+    def step(u, _):
+        first = u >= me
+        reader = jnp.where(first, u, NSEQ - 1 - u)
+        writer = jnp.where(first, me, NSEQ - 1 - me)
+        for r in range(2):
+            rows = tile(jnp.maximum(table[r * NSEQ + reader, writer], 0))
+
+            @pl.when(first)
+            def _():
+                for kind, ref in ((0, k_ref), (1, v_ref)):
+                    pltpu.make_async_copy(ref.at[rows, pl.ds(0, HD)], send_ref.at[u, kind * 2 + r], sem).start()
+
+            @pl.when(jnp.logical_not(first))
+            def _():
+                for kind in range(2):
+                    pltpu.make_async_copy(far_ref.at[kind, rows, :], send_ref.at[u, kind * 2 + r], sem).start()
+
+        return 0
+
+    lax.fori_loop(0, NSEQ, step, 0, unroll=4)
     spread = flag(iota((8, SEG), 0) == (iota((8, SEG), 1) >> 6))
     ids8, row8 = iota((8, nid), 1), iota((8, nid), 0)
     for h in range(2):
@@ -80,68 +113,35 @@
         held = jnp.where(iota((1, nid), 1) < seg * 8 + 8, wanted_ref[pl.ds(seg, 1), :], 0.0)
         count = jnp.sum(held, axis=1, keepdims=True)
         table_ref[COUNT_ROW + h : COUNT_ROW + h + 1, :] = jnp.broadcast_to(count, (1, NSEQ)).astype(jnp.int32)
-
-
-def prep(where, rows):
+    pltpu.make_async_copy(send_ref, send_ref, sem).wait()
+
+
+def select(where, rows, k, v, far):
+    spec = lambda space: pl.BlockSpec(memory_space=space)
+    nid = NSEQ * 8
+    row, col = iota((nid, nid), 0), iota((nid, nid), 1)
+    upto = (row <= col).astype(jnp.bfloat16)
+    upto8 = ((row <= col) & ((row >> 3) == (col >> 3))).astype(jnp.bfloat16)
     return pl.pallas_call(
-        prep_kernel,
-        name="prep",
-        in_specs=[pl.BlockSpec(memory_space=pltpu.SMEM), pl.BlockSpec(memory_space=pltpu.VMEM)],
-        out_specs=[pl.BlockSpec(memory_space=pltpu.VMEM)] * 2,
+        select_kernel,
+        name="select",
+        in_specs=[spec(pltpu.SMEM)] + [spec(pltpu.VMEM)] * 6,
+        out_specs=[spec(pltpu.VMEM)] * 2 + [spec(pl.ANY)],
         out_shape=[
             jax.ShapeDtypeStruct((TABLE_ROWS, NSEQ), jnp.int32),
             jax.ShapeDtypeStruct((2, POOL, SEG), jnp.float32),
+            jax.ShapeDtypeStruct((NSEQ, 4, BLK, HD), jnp.bfloat16),
         ],
         scratch_shapes=[
-            pltpu.VMEM((NSEQ * 8, NSEQ * 8), jnp.float32),
-            pltpu.VMEM((NSEQ, NSEQ * 8), jnp.float32),
-            pltpu.VMEM((NSEQ, NSEQ * 8), jnp.float32),
+            pltpu.SMEM((2 * NSEQ, NSEQ), jnp.int32),
+            pltpu.VMEM((nid, nid), jnp.float32),
+            pltpu.VMEM((NSEQ, nid), jnp.float32),
+            pltpu.VMEM((NSEQ, nid), jnp.float32),
+            pltpu.SemaphoreType.DMA,
+            pltpu.SemaphoreType.DMA,
         ],
-        cost_estimate=pl.CostEstimate(flops=10_000_000, bytes_accessed=1 << 20, transcendentals=0),
-    )(where, rows)
-
-
-def tile(index):
-    return pl.ds(pl.multiple_of(index * BLK, BLK), BLK)
-
-
-def select_kernel(where_ref, table_ref, k_ref, v_ref, far_ref, send_ref, sem):
-    me = where_ref[0]
-
-    def step(u, _):
-        first = u >= me
-        reader = jnp.where(first, u, NSEQ - 1 - u)
-        writer = jnp.where(first, me, NSEQ - 1 - me)
-        for r in range(2):
-            rows = tile(jnp.maximum(table_ref[r * NSEQ + reader, writer], 0))
-
-            @pl.when(first)
-            def _():
-                for kind, ref in ((0, k_ref), (1, v_ref)):
-                    pltpu.make_async_copy(ref.at[rows, pl.ds(0, HD)], send_ref.at[u, kind * 2 + r], sem).start()
-
-            @pl.when(jnp.logical_not(first))
-            def _():
-                for kind in range(2):
-                    pltpu.make_async_copy(far_ref.at[kind, rows, :], send_ref.at[u, kind * 2 + r], sem).start()
-
-        return 0
-
-    lax.fori_loop(0, NSEQ, step, 0, unroll=4)
-    pltpu.make_async_copy(send_ref, send_ref, sem).wait()
-
-
-def select(where, table, k, v, far):
-    spec = lambda space: pl.BlockSpec(memory_space=space)
-    return pl.pallas_call(
-        select_kernel,
-        name="select",
-        in_specs=[spec(pltpu.SMEM)] * 2 + [spec(pltpu.VMEM)] * 3,
-        out_specs=spec(pl.ANY),
-        out_shape=jax.ShapeDtypeStruct((NSEQ, 4, BLK, HD), jnp.bfloat16),
-        scratch_shapes=[pltpu.SemaphoreType.DMA],
-        cost_estimate=pl.CostEstimate(flops=1_000_000, bytes_accessed=3 << 20, transcendentals=0),
-    )(where, table, k, v, far)
+        cost_estimate=pl.CostEstimate(flops=10_000_000, bytes_accessed=4 << 20, transcendentals=0),
+    )(where, rows, upto, upto8, k, v, far)
 
 
 def attend_kernel(where_ref, table_ref, bias_ref, *refs):
@@ -195,12 +195,14 @@
         lax.fori_loop(held, (held + SPC - 1) // SPC * SPC, clear, 0)
         for i in range(POOL // SPC):
             add_ref[h, i] = jnp.where(mask_ref[h, i * SPC : (i + 1) * SPC, :] > 0.5, bias_ref[h] * LOG2E, -1e30)
-    for kind in range(2):
-        most = tiles[kind].at[pl.ds(0, 2 * (NSEQ - 1) * BLK), :]
-        pltpu.make_async_copy(most, most, sems.at[kind]).wait()
 
     def fold(value, op):
-        return op(value.reshape(KC // 8, 8, QT), axis=0)
+        return op(value.reshape(KC // 8, 8, value.shape[1]), axis=0)
+
+    def merge(total, value, op):
+        lo = total.shape[1] - value.shape[1]
+        late = op(total[:, lo:], value)
+        return late if lo == 0 else jnp.concatenate([total[:, :lo], late], axis=1)
 
     for h in range(2):
         q, do, k, v = heads[h]
@@ -223,10 +225,15 @@
 
         top = jnp.full((8, QT), -1e30, jnp.float32)
         for n in range(SEG // KC):
-            score = dot(k[n * KC : (n + 1) * KC, :], qc, NT) * (SCALE * LOG2E)
-            score = jnp.where(iota((KC, QT), 0) + n * KC <= iota((KC, QT), 1), score, -1e30)
-            s_ref[keys + n * KC : keys + (n + 1) * KC, :] = score
-            top = jnp.maximum(top, fold(score, jnp.max))
+            lo = n * KC
+            score = dot(k[lo : lo + KC, :], qc[lo:], NT) * (SCALE * LOG2E)
+            score = jnp.where(iota(score.shape, 0) <= iota(score.shape, 1), score, -1e30)
+            s_ref[keys + lo : keys + lo + KC, lo:] = score
+            top = merge(top, fold(score, jnp.max), jnp.maximum)
+        if h == 0:
+            for kind in range(2):
+                most = tiles[kind].at[pl.ds(0, 2 * (NSEQ - 1) * BLK), :]
+                pltpu.make_async_copy(most, most, sems.at[kind]).wait()
         top = lax.fori_loop(0, steps, mem_score, top)
         top = jnp.max(top, axis=0, keepdims=True)
 
@@ -236,22 +243,26 @@
             return mass + fold(e, jnp.sum)
 
         mass = lax.fori_loop(0, steps, weigh, jnp.zeros((8, QT), jnp.float32))
-        mass = lax.fori_loop(POOL // SPC, POOL // SPC + SEG // KC, weigh, mass)
+        for lo in range(0, SEG, KC):
+            at = slice(keys + lo, keys + lo + KC)
+            e = jnp.exp2(s_ref[at, lo:] - top[:, lo:])
+            s_ref[at, lo:] = e
+            mass = merge(mass, fold(e, jnp.sum), jnp.add)
         inv = 1.0 / jnp.sum(mass, axis=0, keepdims=True)
 
-        def forward(at, vc, carry):
+        def forward(at, vc, carry, lo=0):
             out, delta = carry
-            p = s_ref[at, :] * inv
-            s_ref[at, :] = p
+            p = s_ref[at, lo:] * inv[:, lo:]
+            s_ref[at, lo:] = p
             w = p.astype(jnp.bfloat16)
-            out = out + dot(vc, w, TN)
-            dp = dot(vc, doc, NT)
-            dp_ref[at, :] = dp
-            return dot(w, doc, NN), (out, delta + fold(p * dp, jnp.sum))
-
-        def backward(at, kc, dq):
-            ds = (s_ref[at, :] * (dp_ref[at, :] - delta) * SCALE).astype(jnp.bfloat16)
-            return dot(ds, qc, NN), dq + dot(kc, ds, TN)
+            out = merge(out, dot(vc, w, TN), jnp.add)
+            dp = dot(vc, doc[lo:], NT)
+            dp_ref[at, lo:] = dp
+            return dot(w, doc[lo:], NN), (out, merge(delta, fold(p * dp, jnp.sum), jnp.add))
+
+        def backward(at, kc, dq, lo=0):
+            ds = (s_ref[at, lo:] * (dp_ref[at, lo:] - delta[:, lo:]) * SCALE).astype(jnp.bfloat16)
+            return dot(ds, qc[lo:], NN), merge(dq, dot(kc, ds, TN), jnp.add)
 
         def mem_forward(i, carry):
             dva[chunk(i), :], carry = forward(chunk(i), vt[held_chunk(i), :], carry)
@@ -266,7 +277,7 @@
         for n in range(SEG // KC):
             rows = slice(n * KC, (n + 1) * KC)
             at = slice(keys + n * KC, keys + (n + 1) * KC)
-            dvl_ref[rows, :], carry = forward(at, v[rows, :], carry)
+            dvl_ref[rows, :], carry = forward(at, v[rows, :], carry, n * KC)
         out, delta = carry
         delta = jnp.sum(delta, axis=0, keepdims=True)
         att_ref[...] = out.T.astype(jnp.bfloat16)
@@ -274,7 +285,7 @@
         for n in range(SEG // KC):
             rows = slice(n * KC, (n + 1) * KC)
             at = slice(keys + n * KC, keys + (n + 1) * KC)
-            dkl_ref[rows, :], dq = backward(at, k[rows, :], dq)
+            dkl_ref[rows, :], dq = backward(at, k[rows, :], dq, n * KC)
         gq_ref[...] = dq.T.astype(jnp.bfloat16)
 
         def pack(i, _):
@@ -336,10 +347,16 @@
     locals_, back_ref = refs[:4], refs[4]
     gk_ref, gv_ref, far_ref, acc = refs[5:]
     me = where_ref[0]
-    for i in range(4):
-        acc[i] = locals_[i][...]
-
-    def step(u, _):
+    part = pl.program_id(0)
+    count = NSEQ // PARTS
+
+    @pl.when(part == 0)
+    def _():
+        for i in range(4):
+            acc[i] = locals_[i][...]
+
+    def step(i, _):
+        u = part * count + i
         first = u > me
         h = jnp.where(first, 0, 1)
         reader = jnp.where(first, u, NSEQ - 1 - u)
@@ -350,26 +367,35 @@
             @pl.when((block >= 0) & (u != me))
             def _():
                 for kind in range(2):
-                    acc[h * 2 + kind, tile(block), :] += back_ref[u, kind * 2 + r].astype(jnp.float32)
+                    acc[h * 2 + kind, tile(block), :] += back_ref[i, kind * 2 + r].astype(jnp.float32)
 
         return 0
 
-    lax.fori_loop(0, NSEQ, step, 0)
-    gk_ref[...] = acc[0].astype(jnp.bfloat16)
-    gv_ref[...] = acc[1].astype(jnp.bfloat16)
-    far_ref[...] = acc[2:4].astype(jnp.bfloat16)
+    lax.fori_loop(0, count, step, 0)
+
+    @pl.when(part == PARTS - 1)
+    def _():
+        gk_ref[...] = acc[0].astype(jnp.bfloat16)
+        gv_ref[...] = acc[1].astype(jnp.bfloat16)
+        far_ref[...] = acc[2:4].astype(jnp.bfloat16)
 
 
 def settle(where, table, parts, back):
-    spec = lambda space: pl.BlockSpec(memory_space=space)
+    f32, bf = jnp.float32, jnp.bfloat16
+    whole = lambda *shape: pl.BlockSpec(shape, lambda i, *_: (0,) * len(shape))
     return pl.pallas_call(
         settle_kernel,
         name="settle",
-        in_specs=[spec(pltpu.SMEM)] * 2 + [spec(pltpu.VMEM)] * 5,
-        out_specs=[spec(pltpu.VMEM)] * 3,
-        out_shape=[jax.ShapeDtypeStruct((SEG, HD), jnp.bfloat16)] * 2
-        + [jax.ShapeDtypeStruct((2, SEG, HD), jnp.bfloat16)],
-        scratch_shapes=[pltpu.VMEM((4, SEG, HD), jnp.float32)],
+        grid_spec=pltpu.PrefetchScalarGridSpec(
+            num_scalar_prefetch=2,
+            grid=(PARTS,),
+            in_specs=[whole(SEG, HD)] * 4
+            + [pl.BlockSpec((NSEQ // PARTS, 4, BLK, HD), lambda i, *_: (i, 0, 0, 0))],
+            out_specs=[whole(SEG, HD)] * 2 + [whole(2, SEG, HD)],
+            scratch_shapes=[pltpu.VMEM((4, SEG, HD), f32)],
+        ),
+        out_shape=[jax.ShapeDtypeStruct((SEG, HD), bf)] * 2 + [jax.ShapeDtypeStruct((2, SEG, HD), bf)],
+        compiler_params=pltpu.CompilerParams(vmem_limit_bytes=VMEM_SETTLE),
         cost_estimate=pl.CostEstimate(flops=2_000_000, bytes_accessed=3 << 20, transcendentals=0),
     )(where, table, *parts, back)
 
@@ -390,8 +416,7 @@
     copies = jnp.broadcast_to(retrieved, (devices, *retrieved.shape))
     lists = lax.all_to_all(copies, ("seq", "head"), split_axis=0, concat_axis=0, tiled=True)
     far_q = mirror(queries[:, HD:], grad_out[:, HD:])
-    table, mask = prep(where, lists.reshape(devices, 16))
-    send = select(where, table, keys, values, far_kv)
+    table, mask, send = select(where, lists.reshape(devices, 16), keys, values, far_kv)
     got = exchange(send)
     att, gq, dkl, dvl, far_att, far_gq, far_dkl, far_dvl, back = attend(
         where, table, mem_bias, queries, grad_out, keys, values, far_kv, far_q, mask, got

time: 149 us -> 146 us (0.980)
  waiting for transfers between devices: 72.9 us -> 65.4 us
  starting transfers between devices: 37.1 us -> 44.3 us
  Pallas kernels: 28.3 us -> 26 us
  local copies, waits for them, and re-layouts: 6.58 us -> 4.62 us
    all_to_all x1, waiting for transfers between devices: 13 us -> 6.04 us  [layer(): lax.all_to_all(copies, ('seq', 'head'), split_axis=0, concat_axis=0, tile...]
    all_to_all x1, starting transfers between devices: 9.48 us -> 15.6 us  [layer(): lax.all_to_all(copies, ('seq', 'head'), split_axis=0, concat_axis=0, tile...]
    pallas_call x2 -> x1, Pallas kernels: 7.27 us -> 3.08 us  [settle(): pl.pallas_call(settle_kernel, name='settle', grid_spec=pltpu.PrefetchScal...]
    pallas_call x1, Pallas kernels: 3.29 us -> 5.76 us  [select(): pl.pallas_call(select_kernel, name='select', in_specs=[spec(pltpu.SMEM)]...]
    all_to_all x2, starting transfers between devices: 8.57 us -> 11 us  [exchange(): return lax.all_to_all(value, 'seq', split_axis=0, concat_axis=0, tiled=True)]
    unnamed x26 -> x30, local copies, waits for them, and re-layouts: 4.15 us -> 2.2 us
  transfers between devices with their start and end apart: 7 -> 7, of which waited for: 4 -> 5; matrix products, arithmetic and copies ran while one was open for 2% -> 3% of each run, Pallas kernels for 5% -> 2%
where the time goes in v3:
time: 146 us
  waiting for transfers between devices  65.4 us (45%)
  starting transfers between devices  44.3 us (30%)
  Pallas kernels  26 us (18%)
  local copies, waits for them, and re-layouts  4.62 us (3%)
  other arithmetic  4.5 us (3%)
    ppermute x3, waiting for transfers between devices, mirror(): return lax.ppermute(jnp.stack([first, second]), 'seq', pairs)  28.9 us
    all_to_all x2, waiting for transfers between devices, exchange(): return lax.all_to_all(value, 'seq', split_axis=0, concat_axis=0, tiled=True)  22.8 us
    pallas_call x1, Pallas kernels, attend(): pl.pallas_call(attend_kernel, name='attend', in_specs=[spec(sm)] * 3 + [s...  17.1 us
    all_to_all x1, starting transfers between devices, layer(): lax.all_to_all(copies, ('seq', 'head'), split_axis=0, concat_axis=0, tile...  15.6 us
    ppermute x3, starting transfers between devices, mirror(): return lax.ppermute(jnp.stack([first, second]), 'seq', pairs)  15.3 us
    all_to_all x2, starting transfers between devices, exchange(): return lax.all_to_all(value, 'seq', split_axis=0, concat_axis=0, tiled=True)  11 us
    ppermute x1, waiting for transfers between devices, layer(): far = lax.ppermute(far, 'seq', [(i, NSEQ - 1 - i) for i in range(NSEQ)])  7.64 us
    all_to_all x1, waiting for transfers between devices, layer(): lax.all_to_all(copies, ('seq', 'head'), split_axis=0, concat_axis=0, tile...  6.04 us
  transfers between devices with their start and end apart: 7, of which 5 were waited for; matrix products, arithmetic and copies ran while one was open for 3% of the time, Pallas kernels for 2%

profile of v3, /device:TPU:1, one launch (start us, length us, event | category | flops | bytes accessed | tf_op | source)
XLA Modules:
  0.0 145.6 jit_solution(4834900859942620025)
XLA Ops:
  0.6 1.4 broadcast_in_dim.3
  2.0 15.6 %all-to-all-start = ((s32[256,1,16]{2,1,0:T(1,128)}), s32[256,1,16]{2,1,0:T(1,128)S(1)}, u32[]{:S(2)}, u32[]{:S(2)}) async-start(s32[256,1,16]{2,1,0:T(1,128)} %broadcast_in_dim.3), calls=%async_computation | async-start | bytes 262144 | tf_op jit(solution)/shard_map/all_to_all | solution.py:417
  17.7 1.0 slice_bitcast_fusion.6
  18.7 5.1 %collective-permute-start = (bf16[2,512,128]{2,1,0:T(8,128)(2,1)S(1)}, bf16[2,512,128]{2,1,0:T(8,128)(2,1)S(1)}, u32[]{:S(2)}, u32[]{:S(2)}) collective-permute-start(bf16[2,512,128]{2,1,0:T(8,128)(2,1)S(1)} %pad_maximum_fusion), channel_id=1, source_target_pairs={{0,248},{8,240},{16,232},{24,224},{32,216},{40,208},{48,200},{56,1... | collective-permute-start | bytes 786440 | tf_op jit(solution)/shard_map/ppermute | solution.py:405
  23.8 0.8 fusion.1
  24.6 6.0 %all-to-all-done = s32[256,1,16]{2,1,0:T(1,128)S(1)} async-done(((s32[256,1,16]{2,1,0:T(1,128)}), s32[256,1,16]{2,1,0:T(1,128)S(1)}, u32[]{:S(2)}, u32[]{:S(2)}) %all-to-all-start) | async-done | bytes 16416 | tf_op jit(solution)/shard_map/all_to_all | solution.py:417
  30.6 0.2 collective-permute-done.far_ref.refs_4_
  30.9 0.4 copy-done.6
  31.3 0.3 copy-done.7
  31.6 5.8 %select.1 = (s32[136,32]{1,0:T(8,128)}, f32[2,32,512]{2,1,0:T(8,128)}, bf16[32,4,64,128]{3,2,1,0:T(8,128)(2,1)}) custom-call(s32[1]{0:T(128)} %bitcast.where_ref, s32[256,16]{1,0:T(8,128)} %bitcast.21, bf16[256,256]{1,0:T(8,128)(2,1)} %get-tuple-element.40.upto_ref, bf16[256,256]{1,0:T(8,128)(2,1)} %get-tuple-element.41.upto8_ref, bf16[512,256]{1,0:T(8,128)(2,1)} %refs_2_.1, ...), custom_call_target="tpu_custom_call" | custom-call | flops 10000000 | bytes 4194304 | tf_op jit(solution)/shard_map/select/pallas_call | solution.py:125
  37.3 0.0 copy-start.12
  37.3 0.0 copy-start.13
  37.4 6.8 %all-to-all-start.1 = ((bf16[32,4,64,128]{3,2,1,0:T(8,128)(2,1)}), bf16[32,4,64,128]{3,2,1,0:T(8,128)(2,1)S(1)}, u32[]{:S(2)}, u32[]{:S(2)}) async-start(bf16[32,4,64,128]{3,2,1,0:T(8,128)(2,1)} %get-tuple-element.21), calls=%async_computation.1 | async-start | bytes 4194304 | tf_op jit(solution)/shard_map/all_to_all | solution.py:409
  44.2 5.1 %collective-permute-start.1 = (bf16[2,512,128]{2,1,0:T(8,128)(2,1)S(1)}, bf16[2,512,128]{2,1,0:T(8,128)(2,1)S(1)}, u32[]{:S(2)}, u32[]{:S(2)}) collective-permute-start(bf16[2,512,128]{2,1,0:T(8,128)(2,1)S(1)} %pad_maximum_fusion.1), channel_id=1, source_target_pairs={{0,248},{8,240},{16,232},{24,224},{32,216},{40,208},{48,200},{56,1... | collective-permute-start | bytes 786440 | tf_op jit(solution)/shard_map/ppermute | solution.py:405
  49.4 28.7 %collective-permute-done.1.refs_5_ = bf16[2,512,128]{2,1,0:T(8,128)(2,1)S(1)} collective-permute-done((bf16[2,512,128]{2,1,0:T(8,128)(2,1)S(1)}, bf16[2,512,128]{2,1,0:T(8,128)(2,1)S(1)}, u32[]{:S(2)}, u32[]{:S(2)}) %collective-permute-start.1) | collective-permute-done | bytes 262176 | tf_op jit(solution)/shard_map/ppermute | solution.py:405
  78.1 0.7 copy-done.14
  78.8 0.7 copy-done.5
  79.5 17.1 %attend.1 = (bf16[512,128]{1,0:T(8,128)(2,1)}, bf16[512,128]{1,0:T(8,128)(2,1)}, f32[512,128]{1,0:T(8,128)}, f32[512,128]{1,0:T(8,128)}, bf16[512,128]{1,0:T(8,1...) custom-call(s32[1]{0:T(128)} %bitcast.where_ref, ...), custom_call_target="tpu_custom_call" | custom-call | flops 16000000000 | bytes 8388608 | tf_op jit(solution)/shard_map/attend/pallas_call | solution.py:323
  96.7 0.0 copy-start
  96.7 0.0 copy-start.1
  96.7 4.2 %all-to-all-start.2 = ((bf16[32,4,64,128]{3,2,1,0:T(8,128)(2,1)}), bf16[32,4,64,128]{3,2,1,0:T(8,128)(2,1)S(1)}, u32[]{:S(2)}, u32[]{:S(2)}) async-start(bf16[32,4,64,128]{3,2,1,0:T(8,128)(2,1)} %get-tuple-element.30), calls=%async_computation.2 | async-start | bytes 4194304 | tf_op jit(solution)/shard_map/all_to_all | solution.py:409
  101.0 0.7 pad_maximum_fusion.2
  101.7 5.0 %collective-permute-start.2 = (bf16[2,512,128]{2,1,0:T(8,128)(2,1)}, bf16[2,512,128]{2,1,0:T(8,128)(2,1)S(1)}, u32[]{:S(2)}, u32[]{:S(2)}) collective-permute-start(bf16[2,512,128]{2,1,0:T(8,128)(2,1)} %pad_maximum_fusion.2), channel_id=1, source_target_pairs={{0,248},{8,240},{16,232},{24,224},{32,216},{40,208},{48,200},{56,1... | collective-permute-start | bytes 786440 | tf_op jit(solution)/shard_map/ppermute | solution.py:405
  106.7 22.8 %all-to-all-done.2.refs_4_ = bf16[32,4,64,128]{3,2,1,0:T(8,128)(2,1)S(1)} async-done(((bf16[32,4,64,128]{3,2,1,0:T(8,128)(2,1)}), bf16[32,4,64,128]{3,2,1,0:T(8,128)(2,1)S(1)}, u32[]{:S(2)}, u32[]{:S(2)}) %all-to-all-start.2) | async-done | bytes 2097184 | tf_op jit(solution)/shard_map/all_to_all | solution.py:409
  129.5 3.1 %settle.1 = (bf16[512,128]{1,0:T(8,128)(2,1)S(1)}, bf16[512,128]{1,0:T(8,128)(2,1)S(1)}, bf16[2,512,128]{2,1,0:T(8,128)(2,1)S(1)}) custom-call(s32[1]{0:T(128)} %bitcast.where_ref, s32[136,32]{1,0:T(8,128)S(1)} %copy-done.4, f32[512,128]{1,0:T(8,128)S(1)} %copy-done, f32[512,128]{1,0:T(8,128)S(1)} %copy-done.1, f32[512,128]{1,0:T(8,128)S(1)} %copy-done.2, ...), custom_call_target="tpu_custom_call" | custom-call | flops 2000000 | bytes 3145728 | tf_op jit(solution)/shard_map/settle/pallas_call | solution.py:386
  132.6 2.3 %collective-permute-start.3 = (bf16[2,512,128]{2,1,0:T(8,128)(2,1)S(1)}, bf16[2,512,128]{2,1,0:T(8,128)(2,1)S(1)}, u32[]{:S(2)}, u32[]{:S(2)}) collective-permute-start(bf16[2,512,128]{2,1,0:T(8,128)(2,1)S(1)} %get-tuple-element.32), channel_id=1, source_target_pairs={{0,248},{8,240},{16,232},{24,224},{32,216},{40,208},{48,200},{56,1... | collective-permute-start | bytes 786440 | tf_op jit(solution)/shard_map/ppermute | solution.py:429
  135.0 0.0 collective-permute-done.2
  135.0 0.7 pad_maximum_fusion.4
  135.7 0.7 pad_maximum_fusion.3
  136.5 7.6 %collective-permute-done.3 = bf16[2,512,128]{2,1,0:T(8,128)(2,1)S(1)} collective-permute-done((bf16[2,512,128]{2,1,0:T(8,128)(2,1)S(1)}, bf16[2,512,128]{2,1,0:T(8,128)(2,1)S(1)}, u32[]{:S(2)}, u32[]{:S(2)}) %collective-permute-start.3) | collective-permute-done | bytes 262176 | tf_op jit(solution)/shard_map/ppermute | solution.py:429
  144.1 0.7 pad_maximum_fusion.6
  144.9 0.7 pad_maximum_fusion.5
  (29 shorter events, 0.2 us)
Async XLA Ops:
  2.0 28.6 %all-to-all-start = ((s32[256,1,16]{2,1,0:T(1,128)}), s32[256,1,16]{2,1,0:T(1,128)S(1)}, u32[]{:S(2)}, u32[]{:S(2)}) async-start(s32[256,1,16]{2,1,0:T(1,128)} %broadcast_in_dim.3), calls=%async_computation | async-start | bytes 262144 | tf_op jit(solution)/shard_map/all_to_all | solution.py:417
  18.7 12.2 %collective-permute-start = (bf16[2,512,128]{2,1,0:T(8,128)(2,1)S(1)}, bf16[2,512,128]{2,1,0:T(8,128)(2,1)S(1)}, u32[]{:S(2)}, u32[]{:S(2)}) collective-permute-start(bf16[2,512,128]{2,1,0:T(8,128)(2,1)S(1)} %pad_maximum_fusion), channel_id=1, source_target_pairs={{0,248},{8,240},{16,232},{24,224},{32,216},{40,208},{48,200},{56,1... | collective-permute-start | bytes 786440 | tf_op jit(solution)/shard_map/ppermute | solution.py:405
  30.6 0.7 copy-start.6
  30.9 0.7 copy-start.7
  37.3 6.8 %copy-start.12 = (bf16[512,256]{1,0:T(8,128)(2,1)S(1)}, bf16[512,256]{1,0:T(8,128)(2,1)}, u32[]{:S(2)}) copy-start(bf16[512,256]{1,0:T(8,128)(2,1)} %refs_0_.1) | copy-start | bytes 786436
  37.3 6.8 %copy-start.13 = (bf16[512,256]{1,0:T(8,128)(2,1)S(1)}, bf16[512,256]{1,0:T(8,128)(2,1)}, u32[]{:S(2)}) copy-start(bf16[512,256]{1,0:T(8,128)(2,1)} %refs_1_.1) | copy-start | bytes 786436
  37.4 40.7 %all-to-all-start.1 = ((bf16[32,4,64,128]{3,2,1,0:T(8,128)(2,1)}), bf16[32,4,64,128]{3,2,1,0:T(8,128)(2,1)S(1)}, u32[]{:S(2)}, u32[]{:S(2)}) async-start(bf16[32,4,64,128]{3,2,1,0:T(8,128)(2,1)} %get-tuple-element.21), calls=%async_computation.1 | async-start | bytes 4194304 | tf_op jit(solution)/shard_map/all_to_all | solution.py:409
  44.2 33.8 %collective-permute-start.1 = (bf16[2,512,128]{2,1,0:T(8,128)(2,1)S(1)}, bf16[2,512,128]{2,1,0:T(8,128)(2,1)S(1)}, u32[]{:S(2)}, u32[]{:S(2)}) collective-permute-start(bf16[2,512,128]{2,1,0:T(8,128)(2,1)S(1)} %pad_maximum_fusion.1), channel_id=1, source_target_pairs={{0,248},{8,240},{16,232},{24,224},{32,216},{40,208},{48,200},{56,1... | collective-permute-start | bytes 786440 | tf_op jit(solution)/shard_map/ppermute | solution.py:405
  78.1 0.7 copy-start.14
  78.1 1.4 copy-start.5
  96.6 4.3 %copy-start.10 = (bf16[512,128]{1,0:T(8,128)(2,1)S(1)}, bf16[512,128]{1,0:T(8,128)(2,1)}, u32[]{:S(2)}) copy-start(bf16[512,128]{1,0:T(8,128)(2,1)} %get-tuple-element.23) | copy-start | bytes 393220
  96.7 4.3 %copy-start.11 = (bf16[512,128]{1,0:T(8,128)(2,1)S(1)}, bf16[512,128]{1,0:T(8,128)(2,1)}, u32[]{:S(2)}) copy-start(bf16[512,128]{1,0:T(8,128)(2,1)} %get-tuple-element.24) | copy-start | bytes 393220
  96.7 32.8 %copy-start = (f32[512,128]{1,0:T(8,128)S(1)}, f32[512,128]{1,0:T(8,128)}, u32[]{:S(2)}) copy-start(f32[512,128]{1,0:T(8,128)} %get-tuple-element.26.refs_0_) | copy-start | bytes 786436
  96.7 32.8 %copy-start.1 = (f32[512,128]{1,0:T(8,128)S(1)}, f32[512,128]{1,0:T(8,128)}, u32[]{:S(2)}) copy-start(f32[512,128]{1,0:T(8,128)} %get-tuple-element.27.refs_1_) | copy-start | bytes 786436
  96.7 32.8 %copy-start.2 = (f32[512,128]{1,0:T(8,128)S(1)}, f32[512,128]{1,0:T(8,128)}, u32[]{:S(2)}) copy-start(f32[512,128]{1,0:T(8,128)} %get-tuple-element.28.refs_2_) | copy-start | bytes 786436
  96.7 32.8 %copy-start.3 = (f32[512,128]{1,0:T(8,128)S(1)}, f32[512,128]{1,0:T(8,128)}, u32[]{:S(2)}) copy-start(f32[512,128]{1,0:T(8,128)} %get-tuple-element.29.refs_3_) | copy-start | bytes 786436
  96.7 32.8 %copy-start.4 = (s32[136,32]{1,0:T(8,128)S(1)}, s32[136,32]{1,0:T(8,128)}, u32[]{:S(2)}) copy-start(s32[136,32]{1,0:T(8,128)} %get-tuple-element.19.table_ref) | copy-start | bytes 52228
  96.7 32.8 %all-to-all-start.2 = ((bf16[32,4,64,128]{3,2,1,0:T(8,128)(2,1)}), bf16[32,4,64,128]{3,2,1,0:T(8,128)(2,1)S(1)}, u32[]{:S(2)}, u32[]{:S(2)}) async-start(bf16[32,4,64,128]{3,2,1,0:T(8,128)(2,1)} %get-tuple-element.30), calls=%async_computation.2 | async-start | bytes 4194304 | tf_op jit(solution)/shard_map/all_to_all | solution.py:409
  101.7 33.3 %collective-permute-start.2 = (bf16[2,512,128]{2,1,0:T(8,128)(2,1)}, bf16[2,512,128]{2,1,0:T(8,128)(2,1)S(1)}, u32[]{:S(2)}, u32[]{:S(2)}) collective-permute-start(bf16[2,512,128]{2,1,0:T(8,128)(2,1)} %pad_maximum_fusion.2), channel_id=1, source_target_pairs={{0,248},{8,240},{16,232},{24,224},{32,216},{40,208},{48,200},{56,1... | collective-permute-start | bytes 786440 | tf_op jit(solution)/shard_map/ppermute | solution.py:405
  129.5 5.5 %copy-start.9 = (bf16[512,128]{1,0:T(8,128)(2,1)S(1)}, bf16[512,128]{1,0:T(8,128)(2,1)}, u32[]{:S(2)}) copy-start(bf16[512,128]{1,0:T(8,128)(2,1)} %get-tuple-element.25) | copy-start | bytes 393220
  129.5 6.2 %copy-start.8 = (bf16[512,128]{1,0:T(8,128)(2,1)S(1)}, bf16[512,128]{1,0:T(8,128)(2,1)}, u32[]{:S(2)}) copy-start(bf16[512,128]{1,0:T(8,128)(2,1)} %get-tuple-element.22) | copy-start | bytes 393220
  132.6 11.5 %collective-permute-start.3 = (bf16[2,512,128]{2,1,0:T(8,128)(2,1)S(1)}, bf16[2,512,128]{2,1,0:T(8,128)(2,1)S(1)}, u32[]{:S(2)}, u32[]{:S(2)}) collective-permute-start(bf16[2,512,128]{2,1,0:T(8,128)(2,1)S(1)} %get-tuple-element.32), channel_id=1, source_target_pairs={{0,248},{8,240},{16,232},{24,224},{32,216},{40,208},{48,200},{56,1... | collective-permute-start | bytes 786440 | tf_op jit(solution)/shard_map/ppermute | solution.py:429

commit v4 on v3

--- a/solution.py
+++ b/solution.py
@@ -46,62 +46,95 @@
     return pl.ds(pl.multiple_of(index * BLK, BLK), BLK)
 
 
-def select_kernel(where_ref, rows_ref, upto_ref, upto8_ref, k_ref, v_ref, far_ref, *refs):
-    table_ref, mask_ref, send_ref, table, named_ref, prefix_ref, wanted_ref, table_sem, sem = refs
-    me = where_ref[0]
+def names(rows_ref):
     nid = NSEQ * 8
-    bf = jnp.bfloat16
     col = iota((nid, nid), 1)
     named = col < 0
     for e in range(16):
         named = named | (rows_ref[:, e : e + 1] == col)
     named = flag(named)
+    pick = flag(iota((NSEQ, nid), 0) == (iota((NSEQ, nid), 1) >> 3)).astype(jnp.bfloat16)
+    return named, flag(dot(pick, named.astype(jnp.bfloat16), NN) > 0.5)
+
+
+def owners():
+    gid, gw = iota((NSEQ * 8, NSEQ), 0), iota((NSEQ * 8, NSEQ), 1)
+    return (gid >> 3) == gw, (gid & 7).astype(jnp.float32)
+
+
+def select_kernel(where_ref, rows_ref, upto8_ref, k_ref, v_ref, far_ref, *refs):
+    table_ref, send_ref, table, table_sem, sem = refs
+    me = where_ref[0]
+    bf = jnp.bfloat16
+    _, wanted = names(rows_ref)
+    prefix8 = dot(wanted.astype(bf), upto8_ref[...], NN)
+    same, inner = owners()
+    inner = jnp.where(same, inner + 1.0, 0.0).astype(bf)
+    for r in range(2):
+        picked = jnp.where(prefix8 == float(r + 1), wanted, 0.0)
+        table_ref[r * NSEQ : (r + 1) * NSEQ, :] = dot(picked.astype(bf), inner, NN).astype(jnp.int32) - 1
+    to_smem = pltpu.make_async_copy(table_ref, table, table_sem)
+    to_smem.start()
+    to_smem.wait()
+
+    def near(u, _):
+        for r in range(2):
+            rows = tile(jnp.maximum(table[r * NSEQ + u, me], 0))
+            for kind, ref in ((0, k_ref), (1, v_ref)):
+                pltpu.make_async_copy(ref.at[rows, pl.ds(0, HD)], send_ref.at[u, kind * 2 + r], sem).start()
+        return 0
+
+    def far(u, _):
+        for r in range(2):
+            rows = tile(jnp.maximum(table[r * NSEQ + NSEQ - 1 - u, NSEQ - 1 - me], 0))
+            for kind in range(2):
+                pltpu.make_async_copy(far_ref.at[kind, rows, :], send_ref.at[u, kind * 2 + r], sem).start()
+        return 0
+
+    lax.fori_loop(me, NSEQ, near, 0)
+    lax.fori_loop(0, me, far, 0)
+    pltpu.make_async_copy(send_ref, send_ref, sem).wait()
+
+
+def select(where, rows, upto8, k, v, far):
+    spec = lambda space: pl.BlockSpec(memory_space=space)
+    return pl.pallas_call(
+        select_kernel,
+        name="select",
+        in_specs=[spec(pltpu.SMEM)] + [spec(pltpu.VMEM)] * 5,
+        out_specs=[spec(pltpu.VMEM), spec(pl.ANY)],
+        out_shape=[
+            jax.ShapeDtypeStruct((2 * NSEQ, NSEQ), jnp.int32),
+            jax.ShapeDtypeStruct((NSEQ, 4, BLK, HD), jnp.bfloat16),
+        ],
+        scratch_shapes=[
+            pltpu.SMEM((2 * NSEQ, NSEQ), jnp.int32),
+            pltpu.SemaphoreType.DMA,
+            pltpu.SemaphoreType.DMA,
+        ],
+        cost_estimate=pl.CostEstimate(flops=10_000_000, bytes_accessed=4 << 20, transcendentals=0),
+    )(where, rows, upto8, k, v, far)
+
+
+def prep_kernel(where_ref, rows_ref, upto_ref, upto8_ref, blocks_ref, *refs):
+    table_ref, mask_ref, named_ref, prefix_ref, wanted_ref = refs
+    me = where_ref[0]
+    nid = NSEQ * 8
+    bf = jnp.bfloat16
+    named, wanted = names(rows_ref)
     named_ref[...] = named
-    pick = flag(iota((NSEQ, nid), 0) == (iota((NSEQ, nid), 1) >> 3))
-    wanted = flag(dot(pick.astype(bf), named.astype(bf), NN) > 0.5)
     prefix = dot(wanted.astype(bf), upto_ref[...], NN)
     prefix8 = dot(wanted.astype(bf), upto8_ref[...], NN)
-    gid, gw = iota((nid, NSEQ), 0), iota((nid, NSEQ), 1)
-    same = (gid >> 3) == gw
-    ones = flag(same).astype(bf)
-    inner = jnp.where(same, (gid & 7).astype(jnp.float32), 0.0).astype(bf)
-    places = []
+    ones = flag(owners()[0]).astype(bf)
+    table_ref[0 : 2 * NSEQ, :] = blocks_ref[...]
     for r in range(2):
         picked = jnp.where(prefix8 == float(r + 1), wanted, 0.0)
-        has = dot(picked.astype(bf), ones, NN)
-        block = dot(picked.astype(bf), inner, NN)
-        table_ref[r * NSEQ : (r + 1) * NSEQ, :] = jnp.where(has > 0.5, block, -1.0).astype(jnp.int32)
-        places.append((picked, has))
-    to_smem = pltpu.make_async_copy(table_ref.at[pl.ds(0, 2 * NSEQ), :], table, table_sem)
-    to_smem.start()
-    for r, (picked, has) in enumerate(places):
         place = dot((picked * (prefix - 1.0)).astype(bf), ones, NN)
         spare = iota((NSEQ, NSEQ), 1) + POOL + NSEQ * r
-        table_ref[(2 + r) * NSEQ : (3 + r) * NSEQ, :] = jnp.where(has > 0.5, place.astype(jnp.int32), spare)
+        has = blocks_ref[r * NSEQ : (r + 1) * NSEQ, :] >= 0
+        table_ref[(2 + r) * NSEQ : (3 + r) * NSEQ, :] = jnp.where(has, place.astype(jnp.int32), spare)
     prefix_ref[...] = jnp.where(wanted > 0.5, prefix - 1.0, -1.0)
     wanted_ref[...] = wanted
-    to_smem.wait()
-
-    def step(u, _):
-        first = u >= me
-        reader = jnp.where(first, u, NSEQ - 1 - u)
-        writer = jnp.where(first, me, NSEQ - 1 - me)
-        for r in range(2):
-            rows = tile(jnp.maximum(table[r * NSEQ + reader, writer], 0))
-
-            @pl.when(first)
-            def _():
-                for kind, ref in ((0, k_ref), (1, v_ref)):
-                    pltpu.make_async_copy(ref.at[rows, pl.ds(0, HD)], send_ref.at[u, kind * 2 + r], sem).start()
-
-            @pl.when(jnp.logical_not(first))
-            def _():
-                for kind in range(2):
-                    pltpu.make_async_copy(far_ref.at[kind, rows, :], send_ref.at[u, kind * 2 + r], sem).start()
-
-        return 0
-
-    lax.fori_loop(0, NSEQ, step, 0, unroll=4)
     spread = flag(iota((8, SEG), 0) == (iota((8, SEG), 1) >> 6))
     ids8, row8 = iota((8, nid), 1), iota((8, nid), 0)
     for h in range(2):
@@ -113,35 +146,26 @@
         held = jnp.where(iota((1, nid), 1) < seg * 8 + 8, wanted_ref[pl.ds(seg, 1), :], 0.0)
         count = jnp.sum(held, axis=1, keepdims=True)
         table_ref[COUNT_ROW + h : COUNT_ROW + h + 1, :] = jnp.broadcast_to(count, (1, NSEQ)).astype(jnp.int32)
-    pltpu.make_async_copy(send_ref, send_ref, sem).wait()
-
-
-def select(where, rows, k, v, far):
-    spec = lambda space: pl.BlockSpec(memory_space=space)
+
+
+def prep(where, rows, upto, upto8, blocks):
     nid = NSEQ * 8
-    row, col = iota((nid, nid), 0), iota((nid, nid), 1)
-    upto = (row <= col).astype(jnp.bfloat16)
-    upto8 = ((row <= col) & ((row >> 3) == (col >> 3))).astype(jnp.bfloat16)
     return pl.pallas_call(
-        select_kernel,
-        name="select",
-        in_specs=[spec(pltpu.SMEM)] + [spec(pltpu.VMEM)] * 6,
-        out_specs=[spec(pltpu.VMEM)] * 2 + [spec(pl.ANY)],
+        prep_kernel,
+        name="prep",
+        in_specs=[pl.BlockSpec(memory_space=pltpu.SMEM)] + [pl.BlockSpec(memory_space=pltpu.VMEM)] * 4,
+        out_specs=[pl.BlockSpec(memory_space=pltpu.VMEM)] * 2,
         out_shape=[
             jax.ShapeDtypeStruct((TABLE_ROWS, NSEQ), jnp.int32),
             jax.ShapeDtypeStruct((2, POOL, SEG), jnp.float32),
-            jax.ShapeDtypeStruct((NSEQ, 4, BLK, HD), jnp.bfloat16),
         ],
         scratch_shapes=[
-            pltpu.SMEM((2 * NSEQ, NSEQ), jnp.int32),
             pltpu.VMEM((nid, nid), jnp.float32),
             pltpu.VMEM((NSEQ, nid), jnp.float32),
             pltpu.VMEM((NSEQ, nid), jnp.float32),
-            pltpu.SemaphoreType.DMA,
-            pltpu.SemaphoreType.DMA,
         ],
-        cost_estimate=pl.CostEstimate(flops=10_000_000, bytes_accessed=4 << 20, transcendentals=0),
-    )(where, rows, upto, upto8, k, v, far)
+        cost_estimate=pl.CostEstimate(flops=10_000_000, bytes_accessed=1 << 20, transcendentals=0),
+    )(where, rows, upto, upto8, blocks)
 
 
 def attend_kernel(where_ref, table_ref, bias_ref, *refs):
@@ -416,7 +440,12 @@
     copies = jnp.broadcast_to(retrieved, (devices, *retrieved.shape))
     lists = lax.all_to_all(copies, ("seq", "head"), split_axis=0, concat_axis=0, tiled=True)
     far_q = mirror(queries[:, HD:], grad_out[:, HD:])
-    table, mask, send = select(where, lists.reshape(devices, 16), keys, values, far_kv)
+    rows = lists.reshape(devices, 16)
+    row, col = iota((devices, devices), 0), iota((devices, devices), 1)
+    upto = (row <= col).astype(jnp.bfloat16)
+    upto8 = ((row <= col) & ((row >> 3) == (col >> 3))).astype(jnp.bfloat16)
+    blocks, send = select(where, rows, upto8, keys, values, far_kv)
+    table, mask = prep(where, rows, upto, upto8, blocks)
     got = exchange(send)
     att, gq, dkl, dvl, far_att, far_gq, far_dkl, far_dvl, back = attend(
         where, table, mem_bias, queries, grad_out, keys, values, far_kv, far_q, mask, got

time: 146 us -> 146 us (level)
  waiting for transfers between devices: 65.4 us -> 62 us
  Pallas kernels: 26 us -> 29.2 us
    ppermute x3, waiting for transfers between devices: 28.9 us -> 25.5 us  [mirror(): return lax.ppermute(jnp.stack([first, second]), 'seq', pairs)]
    pallas_call x0 -> x1, Pallas kernels: none -> 3.38 us  [prep(): pl.pallas_call(prep_kernel, name='prep', in_specs=[pl.BlockSpec(memory_sp...]
  transfers between devices with their start and end apart: 7 -> 7, of which waited for: 5 -> 5; matrix products, arithmetic and copies ran while one was open for 3% -> 3% of each run, Pallas kernels for 2% -> 4%
where the time goes in v4:
time: 146 us; the launch traced here: 145 us
  waiting for transfers between devices  62 us (42%)
  starting transfers between devices  44.3 us (30%)
  Pallas kernels  29.2 us (20%)
  local copies, waits for them, and re-layouts  4.62 us (3%)
  other arithmetic  4.5 us (3%)
    ppermute x3, waiting for transfers between devices, mirror(): return lax.ppermute(jnp.stack([first, second]), 'seq', pairs)  25.5 us
    all_to_all x2, waiting for transfers between devices, exchange(): return lax.all_to_all(value, 'seq', split_axis=0, concat_axis=0, tiled=True)  22.8 us
    pallas_call x1, Pallas kernels, attend(): pl.pallas_call(attend_kernel, name='attend', in_specs=[spec(sm)] * 3 + [s...  17.1 us
    all_to_all x1, starting transfers between devices, layer(): lax.all_to_all(copies, ('seq', 'head'), split_axis=0, concat_axis=0, tile...  15.6 us
    ppermute x3, starting transfers between devices, mirror(): return lax.ppermute(jnp.stack([first, second]), 'seq', pairs)  15.3 us
    all_to_all x2, starting transfers between devices, exchange(): return lax.all_to_all(value, 'seq', split_axis=0, concat_axis=0, tiled=True)  11 us
    ppermute x1, waiting for transfers between devices, layer(): far = lax.ppermute(far, 'seq', [(i, NSEQ - 1 - i) for i in range(NSEQ)])  7.64 us
    all_to_all x1, waiting for transfers between devices, layer(): lax.all_to_all(copies, ('seq', 'head'), split_axis=0, concat_axis=0, tile...  6.04 us
  transfers between devices with their start and end apart: 7, of which 5 were waited for; matrix products, arithmetic and copies ran while one was open for 3% of the time, Pallas kernels for 4%

profile of v4, /device:TPU:1, one launch (start us, length us, event | category | flops | bytes accessed | tf_op | source)
XLA Modules:
  0.0 145.4 jit_solution(1881755596532674813)
XLA Ops:
  0.6 1.4 broadcast_in_dim.3
  2.0 15.6 %all-to-all-start = ((s32[256,1,16]{2,1,0:T(1,128)}), s32[256,1,16]{2,1,0:T(1,128)S(1)}, u32[]{:S(2)}, u32[]{:S(2)}) async-start(s32[256,1,16]{2,1,0:T(1,128)} %broadcast_in_dim.3), calls=%async_computation | async-start | bytes 262144 | tf_op jit(solution)/shard_map/all_to_all | solution.py:441
  17.7 1.0 slice_bitcast_fusion.6
  18.7 5.1 %collective-permute-start = (bf16[2,512,128]{2,1,0:T(8,128)(2,1)S(1)}, bf16[2,512,128]{2,1,0:T(8,128)(2,1)S(1)}, u32[]{:S(2)}, u32[]{:S(2)}) collective-permute-start(bf16[2,512,128]{2,1,0:T(8,128)(2,1)S(1)} %pad_maximum_fusion), channel_id=1, source_target_pairs={{0,248},{8,240},{16,232},{24,224},{32,216},{40,208},{48,200},{56,1... | collective-permute-start | bytes 786440 | tf_op jit(solution)/shard_map/ppermute | solution.py:429
  23.8 0.8 fusion.1
  24.6 6.0 %all-to-all-done = s32[256,1,16]{2,1,0:T(1,128)S(1)} async-done(((s32[256,1,16]{2,1,0:T(1,128)}), s32[256,1,16]{2,1,0:T(1,128)S(1)}, u32[]{:S(2)}, u32[]{:S(2)}) %all-to-all-start) | async-done | bytes 16416 | tf_op jit(solution)/shard_map/all_to_all | solution.py:441
  30.6 0.2 collective-permute-done.far_ref.refs_4_
  30.9 0.4 copy-done.6
  31.3 0.3 copy-done.7
  31.6 5.6 %select.1 = (s32[64,32]{1,0:T(8,128)}, bf16[32,4,64,128]{3,2,1,0:T(8,128)(2,1)}) custom-call(s32[1]{0:T(128)} %bitcast.where_ref, s32[256,16]{1,0:T(8,128)} %bitcast.21, bf16[256,256]{1,0:T(8,128)(2,1)} %get-tuple-element.43.upto8_ref, bf16[512,256]{1,0:T(8,128)(2,1)} %refs_2_.1, bf16[512,256]{1,0:T(8,128)(2,1)} %refs_3_.1, bf16[2,512,128]{2,1,0:T(8,128)(2,1)} %copy-done.7), custom_call_target="tpu_custom_call" | custom-call | flops 10000000 | bytes 4194304 | tf_op jit(solution)/shard_map/select/pallas_call | solution.py:101
  37.1 0.0 copy-start.12
  37.2 0.0 copy-start.13
  37.2 6.8 %all-to-all-start.1 = ((bf16[32,4,64,128]{3,2,1,0:T(8,128)(2,1)}), bf16[32,4,64,128]{3,2,1,0:T(8,128)(2,1)S(1)}, u32[]{:S(2)}, u32[]{:S(2)}) async-start(bf16[32,4,64,128]{3,2,1,0:T(8,128)(2,1)} %get-tuple-element.23), calls=%async_computation.1 | async-start | bytes 4194304 | tf_op jit(solution)/shard_map/all_to_all | solution.py:433
  44.0 5.1 %collective-permute-start.1 = (bf16[2,512,128]{2,1,0:T(8,128)(2,1)S(1)}, bf16[2,512,128]{2,1,0:T(8,128)(2,1)S(1)}, u32[]{:S(2)}, u32[]{:S(2)}) collective-permute-start(bf16[2,512,128]{2,1,0:T(8,128)(2,1)S(1)} %pad_maximum_fusion.1), channel_id=1, source_target_pairs={{0,248},{8,240},{16,232},{24,224},{32,216},{40,208},{48,200},{56,1... | collective-permute-start | bytes 786440 | tf_op jit(solution)/shard_map/ppermute | solution.py:429
  49.2 3.4 %prep.1 = (s32[136,32]{1,0:T(8,128)}, f32[2,32,512]{2,1,0:T(8,128)}) custom-call(s32[1]{0:T(128)} %bitcast.where_ref, s32[256,16]{1,0:T(8,128)} %bitcast.22, bf16[256,256]{1,0:T(8,128)(2,1)} %get-tuple-element.42.upto_ref, bf16[256,256]{1,0:T(8,128)(2,1)} %get-tuple-element.43.upto8_ref, s32[64,32]{1,0:T(8,128)} %get-tuple-element.20.blocks_ref), custom_call_target="tpu_custom_call" | custom-call | flops 10000000 | bytes 1048576 | tf_op jit(solution)/shard_map/prep/pallas_call | solution.py:153
  52.5 25.3 %collective-permute-done.1.refs_5_ = bf16[2,512,128]{2,1,0:T(8,128)(2,1)S(1)} collective-permute-done((bf16[2,512,128]{2,1,0:T(8,128)(2,1)S(1)}, bf16[2,512,128]{2,1,0:T(8,128)(2,1)S(1)}, u32[]{:S(2)}, u32[]{:S(2)}) %collective-permute-start.1) | collective-permute-done | bytes 262176 | tf_op jit(solution)/shard_map/ppermute | solution.py:429
  77.9 0.7 copy-done.14
  78.6 0.7 copy-done.5
  79.3 17.1 %attend.1 = (bf16[512,128]{1,0:T(8,128)(2,1)}, bf16[512,128]{1,0:T(8,128)(2,1)}, f32[512,128]{1,0:T(8,128)}, f32[512,128]{1,0:T(8,128)}, bf16[512,128]{1,0:T(8,1...) custom-call(s32[1]{0:T(128)} %bitcast.where_ref, ...), custom_call_target="tpu_custom_call" | custom-call | flops 16000000000 | bytes 8388608 | tf_op jit(solution)/shard_map/attend/pallas_call | solution.py:347
  96.4 0.0 copy-start
  96.5 0.0 copy-start.1
  96.5 4.2 %all-to-all-start.2 = ((bf16[32,4,64,128]{3,2,1,0:T(8,128)(2,1)}), bf16[32,4,64,128]{3,2,1,0:T(8,128)(2,1)S(1)}, u32[]{:S(2)}, u32[]{:S(2)}) async-start(bf16[32,4,64,128]{3,2,1,0:T(8,128)(2,1)} %get-tuple-element.32), calls=%async_computation.2 | async-start | bytes 4194304 | tf_op jit(solution)/shard_map/all_to_all | solution.py:433
  100.7 0.7 pad_maximum_fusion.2
  101.5 5.0 %collective-permute-start.2 = (bf16[2,512,128]{2,1,0:T(8,128)(2,1)}, bf16[2,512,128]{2,1,0:T(8,128)(2,1)S(1)}, u32[]{:S(2)}, u32[]{:S(2)}) collective-permute-start(bf16[2,512,128]{2,1,0:T(8,128)(2,1)} %pad_maximum_fusion.2), channel_id=1, source_target_pairs={{0,248},{8,240},{16,232},{24,224},{32,216},{40,208},{48,200},{56,1... | collective-permute-start | bytes 786440 | tf_op jit(solution)/shard_map/ppermute | solution.py:429
  106.5 22.8 %all-to-all-done.2.refs_4_ = bf16[32,4,64,128]{3,2,1,0:T(8,128)(2,1)S(1)} async-done(((bf16[32,4,64,128]{3,2,1,0:T(8,128)(2,1)}), bf16[32,4,64,128]{3,2,1,0:T(8,128)(2,1)S(1)}, u32[]{:S(2)}, u32[]{:S(2)}) %all-to-all-start.2) | async-done | bytes 2097184 | tf_op jit(solution)/shard_map/all_to_all | solution.py:433
  129.3 3.1 %settle.1 = (bf16[512,128]{1,0:T(8,128)(2,1)S(1)}, bf16[512,128]{1,0:T(8,128)(2,1)S(1)}, bf16[2,512,128]{2,1,0:T(8,128)(2,1)S(1)}) custom-call(s32[1]{0:T(128)} %bitcast.where_ref, s32[136,32]{1,0:T(8,128)S(1)} %copy-done.4, f32[512,128]{1,0:T(8,128)S(1)} %copy-done, f32[512,128]{1,0:T(8,128)S(1)} %copy-done.1, f32[512,128]{1,0:T(8,128)S(1)} %copy-done.2, ...), custom_call_target="tpu_custom_call" | custom-call | flops 2000000 | bytes 3145728 | tf_op jit(solution)/shard_map/settle/pallas_call | solution.py:410
  132.4 2.3 %collective-permute-start.3 = (bf16[2,512,128]{2,1,0:T(8,128)(2,1)S(1)}, bf16[2,512,128]{2,1,0:T(8,128)(2,1)S(1)}, u32[]{:S(2)}, u32[]{:S(2)}) collective-permute-start(bf16[2,512,128]{2,1,0:T(8,128)(2,1)S(1)} %get-tuple-element.34), channel_id=1, source_target_pairs={{0,248},{8,240},{16,232},{24,224},{32,216},{40,208},{48,200},{56,1... | collective-permute-start | bytes 786440 | tf_op jit(solution)/shard_map/ppermute | solution.py:458
  134.8 0.7 pad_maximum_fusion.4
  135.5 0.7 pad_maximum_fusion.3
  136.3 7.6 %collective-permute-done.3 = bf16[2,512,128]{2,1,0:T(8,128)(2,1)S(1)} collective-permute-done((bf16[2,512,128]{2,1,0:T(8,128)(2,1)S(1)}, bf16[2,512,128]{2,1,0:T(8,128)(2,1)S(1)}, u32[]{:S(2)}, u32[]{:S(2)}) %collective-permute-start.3) | collective-permute-done | bytes 262176 | tf_op jit(solution)/shard_map/ppermute | solution.py:458
  143.9 0.7 pad_maximum_fusion.6
  144.7 0.7 pad_maximum_fusion.5
  (30 shorter events, 0.2 us)
Async XLA Ops:
  2.0 28.6 %all-to-all-start = ((s32[256,1,16]{2,1,0:T(1,128)}), s32[256,1,16]{2,1,0:T(1,128)S(1)}, u32[]{:S(2)}, u32[]{:S(2)}) async-start(s32[256,1,16]{2,1,0:T(1,128)} %broadcast_in_dim.3), calls=%async_computation | async-start | bytes 262144 | tf_op jit(solution)/shard_map/all_to_all | solution.py:441
  18.7 12.2 %collective-permute-start = (bf16[2,512,128]{2,1,0:T(8,128)(2,1)S(1)}, bf16[2,512,128]{2,1,0:T(8,128)(2,1)S(1)}, u32[]{:S(2)}, u32[]{:S(2)}) collective-permute-start(bf16[2,512,128]{2,1,0:T(8,128)(2,1)S(1)} %pad_maximum_fusion), channel_id=1, source_target_pairs={{0,248},{8,240},{16,232},{24,224},{32,216},{40,208},{48,200},{56,1... | collective-permute-start | bytes 786440 | tf_op jit(solution)/shard_map/ppermute | solution.py:429
  30.6 0.7 copy-start.6
  30.9 0.7 copy-start.7
  37.1 6.8 %copy-start.12 = (bf16[512,256]{1,0:T(8,128)(2,1)S(1)}, bf16[512,256]{1,0:T(8,128)(2,1)}, u32[]{:S(2)}) copy-start(bf16[512,256]{1,0:T(8,128)(2,1)} %refs_0_.1) | copy-start | bytes 786436
  37.2 6.8 %copy-start.13 = (bf16[512,256]{1,0:T(8,128)(2,1)S(1)}, bf16[512,256]{1,0:T(8,128)(2,1)}, u32[]{:S(2)}) copy-start(bf16[512,256]{1,0:T(8,128)(2,1)} %refs_1_.1) | copy-start | bytes 786436
  37.2 40.7 %all-to-all-start.1 = ((bf16[32,4,64,128]{3,2,1,0:T(8,128)(2,1)}), bf16[32,4,64,128]{3,2,1,0:T(8,128)(2,1)S(1)}, u32[]{:S(2)}, u32[]{:S(2)}) async-start(bf16[32,4,64,128]{3,2,1,0:T(8,128)(2,1)} %get-tuple-element.23), calls=%async_computation.1 | async-start | bytes 4194304 | tf_op jit(solution)/shard_map/all_to_all | solution.py:433
  44.0 33.8 %collective-permute-start.1 = (bf16[2,512,128]{2,1,0:T(8,128)(2,1)S(1)}, bf16[2,512,128]{2,1,0:T(8,128)(2,1)S(1)}, u32[]{:S(2)}, u32[]{:S(2)}) collective-permute-start(bf16[2,512,128]{2,1,0:T(8,128)(2,1)S(1)} %pad_maximum_fusion.1), channel_id=1, source_target_pairs={{0,248},{8,240},{16,232},{24,224},{32,216},{40,208},{48,200},{56,1... | collective-permute-start | bytes 786440 | tf_op jit(solution)/shard_map/ppermute | solution.py:429
  77.9 0.7 copy-start.14
  77.9 1.4 copy-start.5
  96.4 4.3 %copy-start.10 = (bf16[512,128]{1,0:T(8,128)(2,1)S(1)}, bf16[512,128]{1,0:T(8,128)(2,1)}, u32[]{:S(2)}) copy-start(bf16[512,128]{1,0:T(8,128)(2,1)} %get-tuple-element.25) | copy-start | bytes 393220
  96.4 4.3 %copy-start.11 = (bf16[512,128]{1,0:T(8,128)(2,1)S(1)}, bf16[512,128]{1,0:T(8,128)(2,1)}, u32[]{:S(2)}) copy-start(bf16[512,128]{1,0:T(8,128)(2,1)} %get-tuple-element.26) | copy-start | bytes 393220
  96.4 32.8 %copy-start = (f32[512,128]{1,0:T(8,128)S(1)}, f32[512,128]{1,0:T(8,128)}, u32[]{:S(2)}) copy-start(f32[512,128]{1,0:T(8,128)} %get-tuple-element.28.refs_0_) | copy-start | bytes 786436
  96.5 32.8 %copy-start.1 = (f32[512,128]{1,0:T(8,128)S(1)}, f32[512,128]{1,0:T(8,128)}, u32[]{:S(2)}) copy-start(f32[512,128]{1,0:T(8,128)} %get-tuple-element.29.refs_1_) | copy-start | bytes 786436
  96.5 32.8 %copy-start.2 = (f32[512,128]{1,0:T(8,128)S(1)}, f32[512,128]{1,0:T(8,128)}, u32[]{:S(2)}) copy-start(f32[512,128]{1,0:T(8,128)} %get-tuple-element.30.refs_2_) | copy-start | bytes 786436
  96.5 32.8 %copy-start.3 = (f32[512,128]{1,0:T(8,128)S(1)}, f32[512,128]{1,0:T(8,128)}, u32[]{:S(2)}) copy-start(f32[512,128]{1,0:T(8,128)} %get-tuple-element.31.refs_3_) | copy-start | bytes 786436
  96.5 32.8 %copy-start.4 = (s32[136,32]{1,0:T(8,128)S(1)}, s32[136,32]{1,0:T(8,128)}, u32[]{:S(2)}) copy-start(s32[136,32]{1,0:T(8,128)} %get-tuple-element.21.table_ref) | copy-start | bytes 52228
  96.5 32.8 %all-to-all-start.2 = ((bf16[32,4,64,128]{3,2,1,0:T(8,128)(2,1)}), bf16[32,4,64,128]{3,2,1,0:T(8,128)(2,1)S(1)}, u32[]{:S(2)}, u32[]{:S(2)}) async-start(bf16[32,4,64,128]{3,2,1,0:T(8,128)(2,1)} %get-tuple-element.32), calls=%async_computation.2 | async-start | bytes 4194304 | tf_op jit(solution)/shard_map/all_to_all | solution.py:433
  101.5 33.3 %collective-permute-start.2 = (bf16[2,512,128]{2,1,0:T(8,128)(2,1)}, bf16[2,512,128]{2,1,0:T(8,128)(2,1)S(1)}, u32[]{:S(2)}, u32[]{:S(2)}) collective-permute-start(bf16[2,512,128]{2,1,0:T(8,128)(2,1)} %pad_maximum_fusion.2), channel_id=1, source_target_pairs={{0,248},{8,240},{16,232},{24,224},{32,216},{40,208},{48,200},{56,1... | collective-permute-start | bytes 786440 | tf_op jit(solution)/shard_map/ppermute | solution.py:429
  129.3 5.5 %copy-start.9 = (bf16[512,128]{1,0:T(8,128)(2,1)S(1)}, bf16[512,128]{1,0:T(8,128)(2,1)}, u32[]{:S(2)}) copy-start(bf16[512,128]{1,0:T(8,128)(2,1)} %get-tuple-element.27) | copy-start | bytes 393220
  129.3 6.2 %copy-start.8 = (bf16[512,128]{1,0:T(8,128)(2,1)S(1)}, bf16[512,128]{1,0:T(8,128)(2,1)}, u32[]{:S(2)}) copy-start(bf16[512,128]{1,0:T(8,128)(2,1)} %get-tuple-element.24) | copy-start | bytes 393220
  132.4 11.5 %collective-permute-start.3 = (bf16[2,512,128]{2,1,0:T(8,128)(2,1)S(1)}, bf16[2,512,128]{2,1,0:T(8,128)(2,1)S(1)}, u32[]{:S(2)}, u32[]{:S(2)}) collective-permute-start(bf16[2,512,128]{2,1,0:T(8,128)(2,1)S(1)} %get-tuple-element.34), channel_id=1, source_target_pairs={{0,248},{8,240},{16,232},{24,224},{32,216},{40,208},{48,200},{56,1... | collective-permute-start | bytes 786440 | tf_op jit(solution)/shard_map/ppermute | solution.py:458

commit v5 on v4

--- a/solution.py
+++ b/solution.py
@@ -168,57 +168,50 @@
     )(where, rows, upto, upto8, blocks)
 
 
-def attend_kernel(where_ref, table_ref, bias_ref, *refs):
-    q_ref, do_ref, k_ref, v_ref, far_kv_ref, far_q_ref, mask_ref, got_ref = refs[:8]
-    outs, back_ref = refs[8:16], refs[16]
-    kt, vt, s_ref, dp_ref, add_ref, dka, dva, dkb, dvb, sems, out_sem = refs[17:]
+def attend_kernel(h, where_ref, table_ref, bias_ref, q_ref, do_ref, k_ref, v_ref, mask_ref, got_ref, *refs):
+    refs = refs[1 - h :]
+    (att_ref, gq_ref, dkl_ref, dvl_ref), back_ref = refs[:4], refs[4]
+    kt, vt, s_ref, dp_ref, add_ref, dka, dva, dkb, dvb, sems, out_sem = refs[5:]
     me = where_ref[0]
     keys = POOL * BLK
     tiles = (kt, vt)
-    segs = (me, NSEQ - 1 - me)
+    seg = me if h == 0 else NSEQ - 1 - me
+    first, last = (0, me) if h == 0 else (me + 1, NSEQ)
 
     def fetch(u, _):
-        first = u < me
-        h = jnp.where(first, 0, 1)
-        seg = jnp.where(first, segs[0], segs[1])
-        writer = jnp.where(first, u, NSEQ - 1 - u)
-
-        @pl.when(u != me)
-        def _():
-            for r in range(2):
-                at = tile(h * TILES + table_ref[(2 + r) * NSEQ + seg, writer])
-                for kind in range(2):
-                    pltpu.make_async_copy(
-                        got_ref.at[u, kind * 2 + r], tiles[kind].at[at, :], sems.at[kind]
-                    ).start()
-
-        return 0
-
-    lax.fori_loop(0, NSEQ, fetch, 0, unroll=4)
-    heads = []
-    for h in range(2):
-        if h == 0:
-            lanes = slice(0, HD)
-            q, do, k, v = (r.at[:, lanes] for r in (q_ref, do_ref, k_ref, v_ref))
-        else:
-            q, do, k, v = far_q_ref.at[0], far_q_ref.at[1], far_kv_ref.at[0], far_kv_ref.at[1]
-        heads.append((q, do, k, v))
-        held = table_ref[COUNT_ROW + h, 0]
+        writer = u if h == 0 else NSEQ - 1 - u
         for r in range(2):
-            rows = tile(jnp.maximum(table_ref[r * NSEQ + segs[h], segs[h]], 0))
-            at = tile(h * TILES + table_ref[(2 + r) * NSEQ + segs[h], segs[h]])
-            kt[at, :] = k[rows, :]
-            vt[at, :] = v[rows, :]
-
-        def clear(i, _):
-            at = tile(h * TILES + i)
-            kt[at, :] = jnp.zeros((BLK, HD), jnp.bfloat16)
-            vt[at, :] = jnp.zeros((BLK, HD), jnp.bfloat16)
-            return 0
-
-        lax.fori_loop(held, (held + SPC - 1) // SPC * SPC, clear, 0)
-        for i in range(POOL // SPC):
-            add_ref[h, i] = jnp.where(mask_ref[h, i * SPC : (i + 1) * SPC, :] > 0.5, bias_ref[h] * LOG2E, -1e30)
+            at = tile(table_ref[(2 + r) * NSEQ + seg, writer])
+            for kind in range(2):
+                pltpu.make_async_copy(got_ref.at[u, kind * 2 + r], tiles[kind].at[at, :], sems.at[kind]).start()
+        return 0
+
+    def fetched(u, _):
+        for kind in range(2):
+            two = tiles[kind].at[pl.ds(0, 2 * BLK), :]
+            pltpu.make_async_copy(two, two, sems.at[kind]).wait()
+        return 0
+
+    lax.fori_loop(first, last, fetch, 0)
+    if h == 0:
+        q, do, k, v = (r.at[:, pl.ds(0, HD)] for r in (q_ref, do_ref, k_ref, v_ref))
+    else:
+        q, do, k, v = (r.at[0] for r in (q_ref, do_ref, k_ref, v_ref))
+    held = table_ref[COUNT_ROW + h, 0]
+    for r in range(2):
+        rows = tile(jnp.maximum(table_ref[r * NSEQ + seg, seg], 0))
+        at = tile(table_ref[(2 + r) * NSEQ + seg, seg])
+        kt[at, :] = k[rows, :]
+        vt[at, :] = v[rows, :]
+
+    def clear(i, _):
+        kt[tile(i), :] = jnp.zeros((BLK, HD), jnp.bfloat16)
+        vt[tile(i), :] = jnp.zeros((BLK, HD), jnp.bfloat16)
+        return 0
+
+    lax.fori_loop(held, (held + SPC - 1) // SPC * SPC, clear, 0)
+    for i in range(POOL // SPC):
+        add_ref[i] = jnp.where(mask_ref[h, i * SPC : (i + 1) * SPC, :] > 0.5, bias_ref[h] * LOG2E, -1e30)
 
     def fold(value, op):
         return op(value.reshape(KC // 8, 8, value.shape[1]), axis=0)
@@ -228,143 +221,145 @@
         late = op(total[:, lo:], value)
         return late if lo == 0 else jnp.concatenate([total[:, :lo], late], axis=1)
 
-    for h in range(2):
-        q, do, k, v = heads[h]
-        att_ref, gq_ref, dkl_ref, dvl_ref = outs[h * 4 : h * 4 + 4]
-        steps = (table_ref[COUNT_ROW + h, 0] + SPC - 1) // SPC
-        qc, doc = q[...], do[...]
-
-        def chunk(i):
-            return pl.ds(pl.multiple_of(i * KC, KC), KC)
-
-        def held_chunk(i):
-            return pl.ds(pl.multiple_of(h * TILES * BLK + i * KC, KC), KC)
-
-        def mem_score(i, top):
-            score = dot(kt[held_chunk(i), :], qc, NT) * (SCALE * LOG2E)
-            add = add_ref[h, i]
-            score = (score.reshape(SPC, BLK, QT) + add[:, None, :]).reshape(KC, QT)
-            s_ref[chunk(i), :] = score
-            return jnp.maximum(top, fold(score, jnp.max))
-
-        top = jnp.full((8, QT), -1e30, jnp.float32)
-        for n in range(SEG // KC):
-            lo = n * KC
-            score = dot(k[lo : lo + KC, :], qc[lo:], NT) * (SCALE * LOG2E)
-            score = jnp.where(iota(score.shape, 0) <= iota(score.shape, 1), score, -1e30)
-            s_ref[keys + lo : keys + lo + KC, lo:] = score
-            top = merge(top, fold(score, jnp.max), jnp.maximum)
-        if h == 0:
-            for kind in range(2):
-                most = tiles[kind].at[pl.ds(0, 2 * (NSEQ - 1) * BLK), :]
-                pltpu.make_async_copy(most, most, sems.at[kind]).wait()
-        top = lax.fori_loop(0, steps, mem_score, top)
-        top = jnp.max(top, axis=0, keepdims=True)
-
-        def weigh(i, mass):
-            e = jnp.exp2(s_ref[chunk(i), :] - top)
-            s_ref[chunk(i), :] = e
-            return mass + fold(e, jnp.sum)
-
-        mass = lax.fori_loop(0, steps, weigh, jnp.zeros((8, QT), jnp.float32))
-        for lo in range(0, SEG, KC):
-            at = slice(keys + lo, keys + lo + KC)
-            e = jnp.exp2(s_ref[at, lo:] - top[:, lo:])
-            s_ref[at, lo:] = e
-            mass = merge(mass, fold(e, jnp.sum), jnp.add)
-        inv = 1.0 / jnp.sum(mass, axis=0, keepdims=True)
-
-        def forward(at, vc, carry, lo=0):
-            out, delta = carry
-            p = s_ref[at, lo:] * inv[:, lo:]
-            s_ref[at, lo:] = p
-            w = p.astype(jnp.bfloat16)
-            out = merge(out, dot(vc, w, TN), jnp.add)
-            dp = dot(vc, doc[lo:], NT)
-            dp_ref[at, lo:] = dp
-            return dot(w, doc[lo:], NN), (out, merge(delta, fold(p * dp, jnp.sum), jnp.add))
-
-        def backward(at, kc, dq, lo=0):
-            ds = (s_ref[at, lo:] * (dp_ref[at, lo:] - delta[:, lo:]) * SCALE).astype(jnp.bfloat16)
-            return dot(ds, qc[lo:], NN), merge(dq, dot(kc, ds, TN), jnp.add)
-
-        def mem_forward(i, carry):
-            dva[chunk(i), :], carry = forward(chunk(i), vt[held_chunk(i), :], carry)
-            return carry
-
-        def mem_backward(i, dq):
-            dka[chunk(i), :], dq = backward(chunk(i), kt[held_chunk(i), :], dq)
-            return dq
-
-        carry = (jnp.zeros((HD, QT), jnp.float32), jnp.zeros((8, QT), jnp.float32))
-        carry = lax.fori_loop(0, steps, mem_forward, carry)
-        for n in range(SEG // KC):
-            rows = slice(n * KC, (n + 1) * KC)
-            at = slice(keys + n * KC, keys + (n + 1) * KC)
-            dvl_ref[rows, :], carry = forward(at, v[rows, :], carry, n * KC)
+    steps = (held + SPC - 1) // SPC
+    qc, doc = q[...], do[...]
+
+    def chunk(i):
+        return pl.ds(pl.multiple_of(i * KC, KC), KC)
+
+    def mem_score(i, top):
+        score = dot(kt[chunk(i), :], qc, NT) * (SCALE * LOG2E)
+        add = add_ref[i]
+        score = (score.reshape(SPC, BLK, QT) + add[:, None, :]).reshape(KC, QT)
+        s_ref[chunk(i), :] = score
+        return jnp.maximum(top, fold(score, jnp.max))
+
+    top = jnp.full((8, QT), -1e30, jnp.float32)
+    for n in range(SEG // KC):
+        lo = n * KC
+        score = dot(k[lo : lo + KC, :], qc[lo:], NT) * (SCALE * LOG2E)
+        score = jnp.where(iota(score.shape, 0) <= iota(score.shape, 1), score, -1e30)
+        s_ref[keys + lo : keys + lo + KC, lo:] = score
+        top = merge(top, fold(score, jnp.max), jnp.maximum)
+    lax.fori_loop(first, last, fetched, 0)
+    top = lax.fori_loop(0, steps, mem_score, top)
+    top = jnp.max(top, axis=0, keepdims=True)
+
+    def weigh(i, mass):
+        e = jnp.exp2(s_ref[chunk(i), :] - top)
+        s_ref[chunk(i), :] = e
+        return mass + fold(e, jnp.sum)
+
+    mass = lax.fori_loop(0, steps, weigh, jnp.zeros((8, QT), jnp.float32))
+    for lo in range(0, SEG, KC):
+        at = slice(keys + lo, keys + lo + KC)
+        e = jnp.exp2(s_ref[at, lo:] - top[:, lo:])
+        s_ref[at, lo:] = e
+        mass = merge(mass, fold(e, jnp.sum), jnp.add)
+    inv = 1.0 / jnp.sum(mass, axis=0, keepdims=True)
+
+    def forward(at, vc, carry, lo=0):
         out, delta = carry
-        delta = jnp.sum(delta, axis=0, keepdims=True)
-        att_ref[...] = out.T.astype(jnp.bfloat16)
-        dq = lax.fori_loop(0, steps, mem_backward, jnp.zeros((HD, QT), jnp.float32))
-        for n in range(SEG // KC):
-            rows = slice(n * KC, (n + 1) * KC)
-            at = slice(keys + n * KC, keys + (n + 1) * KC)
-            dkl_ref[rows, :], dq = backward(at, k[rows, :], dq, n * KC)
-        gq_ref[...] = dq.T.astype(jnp.bfloat16)
-
-        def pack(i, _):
-            dkb[h, chunk(i), :] = dka[chunk(i), :].astype(jnp.bfloat16)
-            dvb[h, chunk(i), :] = dva[chunk(i), :].astype(jnp.bfloat16)
-            return 0
-
-        lax.fori_loop(0, steps, pack, 0)
+        p = s_ref[at, lo:] * inv[:, lo:]
+        s_ref[at, lo:] = p
+        w = p.astype(jnp.bfloat16)
+        out = merge(out, dot(vc, w, TN), jnp.add)
+        dp = dot(vc, doc[lo:], NT)
+        dp_ref[at, lo:] = dp
+        return dot(w, doc[lo:], NN), (out, merge(delta, fold(p * dp, jnp.sum), jnp.add))
+
+    def backward(at, kc, dq, lo=0):
+        ds = (s_ref[at, lo:] * (dp_ref[at, lo:] - delta[:, lo:]) * SCALE).astype(jnp.bfloat16)
+        return dot(ds, qc[lo:], NN), merge(dq, dot(kc, ds, TN), jnp.add)
+
+    def mem_forward(i, carry):
+        dva[chunk(i), :], carry = forward(chunk(i), vt[chunk(i), :], carry)
+        return carry
+
+    def mem_backward(i, dq):
+        dka[chunk(i), :], dq = backward(chunk(i), kt[chunk(i), :], dq)
+        return dq
+
+    carry = (jnp.zeros((HD, QT), jnp.float32), jnp.zeros((8, QT), jnp.float32))
+    carry = lax.fori_loop(0, steps, mem_forward, carry)
+    for n in range(SEG // KC):
+        rows = slice(n * KC, (n + 1) * KC)
+        at = slice(keys + n * KC, keys + (n + 1) * KC)
+        dvl_ref[rows, :], carry = forward(at, v[rows, :], carry, n * KC)
+    out, delta = carry
+    delta = jnp.sum(delta, axis=0, keepdims=True)
+    att_ref[...] = out.T.astype(jnp.bfloat16)
+    dq = lax.fori_loop(0, steps, mem_backward, jnp.zeros((HD, QT), jnp.float32))
+    for n in range(SEG // KC):
+        rows = slice(n * KC, (n + 1) * KC)
+        at = slice(keys + n * KC, keys + (n + 1) * KC)
+        dkl_ref[rows, :], dq = backward(at, k[rows, :], dq, n * KC)
+    gq_ref[...] = dq.T.astype(jnp.bfloat16)
+
+    def pack(i, _):
+        dkb[chunk(i), :] = dka[chunk(i), :].astype(jnp.bfloat16)
+        dvb[chunk(i), :] = dva[chunk(i), :].astype(jnp.bfloat16)
+        return 0
+
+    lax.fori_loop(0, steps, pack, 0)
+    for r in range(2):
+        block = table_ref[r * NSEQ + seg, seg]
+
+        @pl.when(block >= 0)
+        def _():
+            rows, at = tile(block), tile(table_ref[(2 + r) * NSEQ + seg, seg])
+            dkl_ref[rows, :] += dkb[at, :].astype(jnp.float32)
+            dvl_ref[rows, :] += dvb[at, :].astype(jnp.float32)
+
+    def put(u, _):
+        writer = u if h == 0 else NSEQ - 1 - u
         for r in range(2):
-            block = table_ref[r * NSEQ + segs[h], segs[h]]
-
-            @pl.when(block >= 0)
-            def _():
-                rows, at = tile(block), tile(table_ref[(2 + r) * NSEQ + segs[h], segs[h]])
-                dkl_ref[rows, :] += dkb[h, at, :].astype(jnp.float32)
-                dvl_ref[rows, :] += dvb[h, at, :].astype(jnp.float32)
-
-        def put(u, _):
-            writer = u if h == 0 else NSEQ - 1 - u
-            for r in range(2):
-                at = tile(jnp.minimum(table_ref[(2 + r) * NSEQ + segs[h], writer], POOL - 1))
-                for kind, ref in ((0, dkb), (1, dvb)):
-                    pltpu.make_async_copy(ref.at[h, at, :], back_ref.at[u, kind * 2 + r], out_sem).start()
-            return 0
-
-        lax.fori_loop(*((0, me + 1) if h == 0 else (me + 1, NSEQ)), put, 0)
-    pltpu.make_async_copy(back_ref, back_ref, out_sem).wait()
-
-
-def attend(where, table, bias, q, do, k, v, far_kv, far_q, mask, got):
+            at = tile(jnp.minimum(table_ref[(2 + r) * NSEQ + seg, writer], POOL - 1))
+            for kind, ref in ((0, dkb), (1, dvb)):
+                pltpu.make_async_copy(ref.at[at, :], back_ref.at[u, kind * 2 + r], out_sem).start()
+        return 0
+
+    def sent(u, _):
+        pltpu.make_async_copy(back_ref.at[0], back_ref.at[0], out_sem).wait()
+        return 0
+
+    ends = (0, me + 1) if h == 0 else (me + 1, NSEQ)
+    lax.fori_loop(*ends, put, 0)
+    lax.fori_loop(*ends, sent, 0)
+
+
+def attend(h, where, table, bias, q, do, k, v, mask, got, back=()):
     bf, f32, vm, hbm, sm = jnp.bfloat16, jnp.float32, pltpu.VMEM, pl.ANY, pltpu.SMEM
     spec = lambda space: pl.BlockSpec(memory_space=space)
     keys = POOL * BLK
-    each = [jax.ShapeDtypeStruct((SEG, HD), d) for d in (bf, bf, f32, f32)]
+    if h == 0:
+        ins = [spec(vm)] * 4
+    else:
+        half = lambda i: pl.BlockSpec((1, SEG, HD), lambda _: (i, 0, 0))
+        ins = [half(0), half(1), half(0), half(1)]
     return pl.pallas_call(
-        attend_kernel,
-        name="attend",
-        in_specs=[spec(sm)] * 3 + [spec(vm)] * 7 + [spec(hbm)],
-        out_specs=[spec(vm)] * 8 + [spec(hbm)],
-        out_shape=each * 2 + [jax.ShapeDtypeStruct((NSEQ, 4, BLK, HD), bf)],
+        lambda *refs: attend_kernel(h, *refs),
+        grid=(1,) if h else (),
+        in_specs=[spec(sm)] * 3 + ins + [spec(vm), spec(hbm)] + [spec(hbm)] * len(back),
+        out_specs=[spec(vm)] * 4 + [spec(hbm)],
+        out_shape=[jax.ShapeDtypeStruct((SEG, HD), d) for d in (bf, bf, f32, f32)]
+        + [jax.ShapeDtypeStruct((NSEQ, 4, BLK, HD), bf)],
         scratch_shapes=[
-            pltpu.VMEM((2 * TILES * BLK, HD), bf),
-            pltpu.VMEM((2 * TILES * BLK, HD), bf),
+            pltpu.VMEM((TILES * BLK, HD), bf),
+            pltpu.VMEM((TILES * BLK, HD), bf),
             pltpu.VMEM((keys + SEG, QT), f32),
             pltpu.VMEM((keys + SEG, QT), f32),
-            pltpu.VMEM((2, POOL // SPC, SPC, SEG), f32),
+            pltpu.VMEM((POOL // SPC, SPC, SEG), f32),
             pltpu.VMEM((keys, HD), f32),
             pltpu.VMEM((keys, HD), f32),
-            pltpu.VMEM((2, keys, HD), bf),
-            pltpu.VMEM((2, keys, HD), bf),
+            pltpu.VMEM((keys, HD), bf),
+            pltpu.VMEM((keys, HD), bf),
             pltpu.SemaphoreType.DMA((2,)),
             pltpu.SemaphoreType.DMA,
         ],
-        cost_estimate=pl.CostEstimate(flops=16_000_000_000, bytes_accessed=8 << 20, transcendentals=1_500_000),
-    )(where, table, bias, q, do, k, v, far_kv, far_q, mask, got)
+        input_output_aliases={9: 4} if back else {},
+        cost_estimate=pl.CostEstimate(flops=8_000_000_000, bytes_accessed=4 << 20, transcendentals=750_000),
+    )(where, table, bias, q, do, k, v, mask, got, *back)
 
 
 def settle_kernel(where_ref, table_ref, *refs):
@@ -447,8 +442,11 @@
     blocks, send = select(where, rows, upto8, keys, values, far_kv)
     table, mask = prep(where, rows, upto, upto8, blocks)
     got = exchange(send)
-    att, gq, dkl, dvl, far_att, far_gq, far_dkl, far_dvl, back = attend(
-        where, table, mem_bias, queries, grad_out, keys, values, far_kv, far_q, mask, got
+    far_att, far_gq, far_dkl, far_dvl, back = attend(
+        1, where, table, mem_bias, far_q, far_q, far_kv, far_kv, mask, got
+    )
+    att, gq, dkl, dvl, back = attend(
+        0, where, table, mem_bias, queries, grad_out, keys, values, mask, got, (back,)
     )
     home = mirror(far_att, far_gq)
     attended = jnp.concatenate([att, home[0]], axis=1)

time: 146 us -> 150 us (1.027)
  Pallas kernels: 29.2 us -> 32.7 us
    pallas_call x1 -> x2, Pallas kernels: 17.1 us -> 20.7 us  [attend(): pl.pallas_call(lambda *refs: attend_kernel(h, *refs), grid=(1,) if h else...]
where the time goes in v5:
time: 150 us; the launch traced here: 149 us
  waiting for transfers between devices  62 us (41%)
  starting transfers between devices  44.6 us (30%)
  Pallas kernels  32.7 us (22%)
  local copies, waits for them, and re-layouts  4.62 us (3%)
  other arithmetic  4.5 us (3%)
    ppermute x3, waiting for transfers between devices, mirror(): return lax.ppermute(jnp.stack([first, second]), 'seq', pairs)  25.5 us
    all_to_all x2, waiting for transfers between devices, exchange(): return lax.all_to_all(value, 'seq', split_axis=0, concat_axis=0, tiled=True)  22.8 us
    pallas_call x2, Pallas kernels, attend(): pl.pallas_call(lambda *refs: attend_kernel(h, *refs), grid=(1,) if h else...  20.7 us
    all_to_all x1, starting transfers between devices, layer(): lax.all_to_all(copies, ('seq', 'head'), split_axis=0, concat_axis=0, tile...  15.6 us
    ppermute x3, starting transfers between devices, mirror(): return lax.ppermute(jnp.stack([first, second]), 'seq', pairs)  15.3 us
    all_to_all x2, starting transfers between devices, exchange(): return lax.all_to_all(value, 'seq', split_axis=0, concat_axis=0, tiled=True)  11.3 us
    ppermute x1, waiting for transfers between devices, layer(): far = lax.ppermute(far, 'seq', [(i, NSEQ - 1 - i) for i in range(NSEQ)])  7.64 us
    all_to_all x1, waiting for transfers between devices, layer(): lax.all_to_all(copies, ('seq', 'head'), split_axis=0, concat_axis=0, tile...  6.04 us
  transfers between devices with their start and end apart: 7, of which 5 were waited for; matrix products, arithmetic and copies ran while one was open for 3% of the time, Pallas kernels for 4%

profile of v5, /device:TPU:1, one launch (start us, length us, event | category | flops | bytes accessed | tf_op | source)
XLA Modules:
  0.0 149.2 jit_solution(1269977702625381451)
XLA Ops:
  0.6 1.4 broadcast_in_dim.3
  2.0 15.6 %all-to-all-start = ((s32[256,1,16]{2,1,0:T(1,128)}), s32[256,1,16]{2,1,0:T(1,128)S(1)}, u32[]{:S(2)}, u32[]{:S(2)}) async-start(s32[256,1,16]{2,1,0:T(1,128)} %broadcast_in_dim.3), calls=%async_computation | async-start | bytes 262144 | tf_op jit(solution)/shard_map/all_to_all | solution.py:436
  17.7 1.0 slice_bitcast_fusion.6
  18.7 5.1 %collective-permute-start = (bf16[2,512,128]{2,1,0:T(8,128)(2,1)S(1)}, bf16[2,512,128]{2,1,0:T(8,128)(2,1)S(1)}, u32[]{:S(2)}, u32[]{:S(2)}) collective-permute-start(bf16[2,512,128]{2,1,0:T(8,128)(2,1)S(1)} %pad_maximum_fusion), channel_id=1, source_target_pairs={{0,248},{8,240},{16,232},{24,224},{32,216},{40,208},{48,200},{56,1... | collective-permute-start | bytes 786440 | tf_op jit(solution)/shard_map/ppermute | solution.py:424
  23.8 0.8 fusion.1
  24.6 6.0 %all-to-all-done = s32[256,1,16]{2,1,0:T(1,128)S(1)} async-done(((s32[256,1,16]{2,1,0:T(1,128)}), s32[256,1,16]{2,1,0:T(1,128)S(1)}, u32[]{:S(2)}, u32[]{:S(2)}) %all-to-all-start) | async-done | bytes 16416 | tf_op jit(solution)/shard_map/all_to_all | solution.py:436
  30.6 0.2 collective-permute-done.far_ref.refs_5_.refs_6_
  30.9 0.4 copy-done.6
  31.3 0.3 copy-done.7
  31.6 5.6 %select.1 = (s32[64,32]{1,0:T(8,128)}, bf16[32,4,64,128]{3,2,1,0:T(8,128)(2,1)}) custom-call(s32[1]{0:T(128)} %bitcast.where_ref.refs_0_, s32[256,16]{1,0:T(8,128)} %bitcast.21, bf16[256,256]{1,0:T(8,128)(2,1)} %get-tuple-element.45.upto8_ref, bf16[512,256]{1,0:T(8,128)(2,1)} %refs_5_.1, bf16[512,256]{1,0:T(8,128)(2,1)} %refs_6_.1, ...), custom_call_target="tpu_custom_call" | custom-call | flops 10000000 | bytes 4194304 | tf_op jit(solution)/shard_map/select/pallas_call | solution.py:101
  37.1 0.0 copy-start.12
  37.2 0.0 copy-start.13
  37.2 6.8 %all-to-all-start.1 = ((bf16[32,4,64,128]{3,2,1,0:T(8,128)(2,1)}), bf16[32,4,64,128]{3,2,1,0:T(8,128)(2,1)S(1)}, u32[]{:S(2)}, u32[]{:S(2)}) async-start(bf16[32,4,64,128]{3,2,1,0:T(8,128)(2,1)} %get-tuple-element.24), calls=%async_computation.1 | async-start | bytes 4194304 | tf_op jit(solution)/shard_map/all_to_all | solution.py:428
  44.1 5.1 %collective-permute-start.1 = (bf16[2,512,128]{2,1,0:T(8,128)(2,1)S(1)}, bf16[2,512,128]{2,1,0:T(8,128)(2,1)S(1)}, u32[]{:S(2)}, u32[]{:S(2)}) collective-permute-start(bf16[2,512,128]{2,1,0:T(8,128)(2,1)S(1)} %pad_maximum_fusion.1), channel_id=1, source_target_pairs={{0,248},{8,240},{16,232},{24,224},{32,216},{40,208},{48,200},{56,1... | collective-permute-start | bytes 786440 | tf_op jit(solution)/shard_map/ppermute | solution.py:424
  49.2 3.4 %prep.1 = (s32[136,32]{1,0:T(8,128)}, f32[2,32,512]{2,1,0:T(8,128)}) custom-call(s32[1]{0:T(128)} %bitcast.where_ref.refs_0_, s32[256,16]{1,0:T(8,128)} %bitcast.22, bf16[256,256]{1,0:T(8,128)(2,1)} %get-tuple-element.44.upto_ref, bf16[256,256]{1,0:T(8,128)(2,1)} %get-tuple-element.45.upto8_ref, s32[64,32]{1,0:T(8,128)} %get-tuple-element.21.blocks_ref), custom_call_target="tpu_custom_call" | custom-call | flops 10000000 | bytes 1048576 | tf_op jit(solution)/shard_map/prep/pallas_call | solution.py:153
  52.6 25.3 %collective-permute-done.1.refs_3_.refs_4_ = bf16[2,512,128]{2,1,0:T(8,128)(2,1)S(1)} collective-permute-done((bf16[2,512,128]{2,1,0:T(8,128)(2,1)S(1)}, bf16[2,512,128]{2,1,0:T(8,128)(2,1)S(1)}, u32[]{:S(2)}, u32[]{:S(2)}) %collective-permute-start.1) | collective-permute-done | bytes 262176 | tf_op jit(solution)/shard_map/ppermute | solution.py:424
  77.9 0.7 copy-done.14
  78.6 0.7 copy-done.5
  79.3 14.4 %shard_map.96 = (bf16[512,128]{1,0:T(8,128)(2,1)}, bf16[512,128]{1,0:T(8,128)(2,1)}, f32[512,128]{1,0:T(8,128)}, f32[512,128]{1,0:T(8,128)}, bf16[32,4,64,128]{3,2,1,0:T(8,128)(2,1)}) custom-call(s32[1]{0:T(128)} %bitcast.where_ref.refs_0_, s32[136,32]{1,0:T(8,128)} %get-tuple-element.22.refs_1_.table_ref, f32[2]{0:T(128)} %refs_2_.3, ...), custom_call_target="tpu_custom_call" | custom-call | flops 8000000000 | bytes 4194304 | tf_op jit(solution)/shard_map/pallas_call | solution.py:340
  93.7 6.3 %shard_map.97 = (bf16[512,128]{1,0:T(8,128)(2,1)}, bf16[512,128]{1,0:T(8,128)(2,1)}, f32[512,128]{1,0:T(8,128)}, f32[512,128]{1,0:T(8,128)}, bf16[32,4,64,128]{3,2,1,0:T(8,128)(2,1)}) custom-call(s32[1]{0:T(128)} %bitcast.where_ref.refs_0_, s32[136,32]{1,0:T(8,128)} %get-tuple-element.22.refs_1_.table_ref, ...), custom_call_target="tpu_custom_call", output_to_operand_aliasing={{4}: (9, {})} | custom-call | flops 8000000000 | bytes 4194304 | tf_op jit(solution)/shard_map/pallas_call | solution.py:340
  100.0 0.0 copy-start.2
  100.1 4.5 %all-to-all-start.2 = ((bf16[32,4,64,128]{3,2,1,0:T(8,128)(2,1)}), bf16[32,4,64,128]{3,2,1,0:T(8,128)(2,1)S(1)}, u32[]{:S(2)}, u32[]{:S(2)}) async-start(bf16[32,4,64,128]{3,2,1,0:T(8,128)(2,1)} %get-tuple-element.34), calls=%async_computation.2 | async-start | bytes 4194304 | tf_op jit(solution)/shard_map/all_to_all | solution.py:428
  104.6 0.7 pad_maximum_fusion.2
  105.3 5.0 %collective-permute-start.2 = (bf16[2,512,128]{2,1,0:T(8,128)(2,1)}, bf16[2,512,128]{2,1,0:T(8,128)(2,1)S(1)}, u32[]{:S(2)}, u32[]{:S(2)}) collective-permute-start(bf16[2,512,128]{2,1,0:T(8,128)(2,1)} %pad_maximum_fusion.2), channel_id=1, source_target_pairs={{0,248},{8,240},{16,232},{24,224},{32,216},{40,208},{48,200},{56,1... | collective-permute-start | bytes 786440 | tf_op jit(solution)/shard_map/ppermute | solution.py:424
  110.3 22.8 %all-to-all-done.2.refs_4_ = bf16[32,4,64,128]{3,2,1,0:T(8,128)(2,1)S(1)} async-done(((bf16[32,4,64,128]{3,2,1,0:T(8,128)(2,1)}), bf16[32,4,64,128]{3,2,1,0:T(8,128)(2,1)S(1)}, u32[]{:S(2)}, u32[]{:S(2)}) %all-to-all-start.2) | async-done | bytes 2097184 | tf_op jit(solution)/shard_map/all_to_all | solution.py:428
  133.2 3.1 %settle.1 = (bf16[512,128]{1,0:T(8,128)(2,1)S(1)}, bf16[512,128]{1,0:T(8,128)(2,1)S(1)}, bf16[2,512,128]{2,1,0:T(8,128)(2,1)S(1)}) custom-call(s32[1]{0:T(128)} %bitcast.where_ref.refs_0_, s32[136,32]{1,0:T(8,128)S(1)} %copy-done.4, f32[512,128]{1,0:T(8,128)S(1)} %copy-done.2, f32[512,128]{1,0:T(8,128)S(1)} %copy-done.3, f32[512,128]{1,0:T(8,128)S(1)} %copy-done, ...), custom_call_target="tpu_custom_call" | custom-call | flops 2000000 | bytes 3145728 | tf_op jit(solution)/shard_map/settle/pallas_call | solution.py:405
  136.2 2.3 %collective-permute-start.3 = (bf16[2,512,128]{2,1,0:T(8,128)(2,1)S(1)}, bf16[2,512,128]{2,1,0:T(8,128)(2,1)S(1)}, u32[]{:S(2)}, u32[]{:S(2)}) collective-permute-start(bf16[2,512,128]{2,1,0:T(8,128)(2,1)S(1)} %get-tuple-element.36), channel_id=1, source_target_pairs={{0,248},{8,240},{16,232},{24,224},{32,216},{40,208},{48,200},{56,1... | collective-permute-start | bytes 786440 | tf_op jit(solution)/shard_map/ppermute | solution.py:456
  138.6 0.7 pad_maximum_fusion.4
  139.4 0.7 pad_maximum_fusion.3
  140.1 7.6 %collective-permute-done.3 = bf16[2,512,128]{2,1,0:T(8,128)(2,1)S(1)} collective-permute-done((bf16[2,512,128]{2,1,0:T(8,128)(2,1)S(1)}, bf16[2,512,128]{2,1,0:T(8,128)(2,1)S(1)}, u32[]{:S(2)}, u32[]{:S(2)}) %collective-permute-start.3) | collective-permute-done | bytes 262176 | tf_op jit(solution)/shard_map/ppermute | solution.py:456
  147.8 0.7 pad_maximum_fusion.6
  148.5 0.7 pad_maximum_fusion.5
  (31 shorter events, 0.2 us)
Async XLA Ops:
  2.0 28.6 %all-to-all-start = ((s32[256,1,16]{2,1,0:T(1,128)}), s32[256,1,16]{2,1,0:T(1,128)S(1)}, u32[]{:S(2)}, u32[]{:S(2)}) async-start(s32[256,1,16]{2,1,0:T(1,128)} %broadcast_in_dim.3), calls=%async_computation | async-start | bytes 262144 | tf_op jit(solution)/shard_map/all_to_all | solution.py:436
  18.7 12.2 %collective-permute-start = (bf16[2,512,128]{2,1,0:T(8,128)(2,1)S(1)}, bf16[2,512,128]{2,1,0:T(8,128)(2,1)S(1)}, u32[]{:S(2)}, u32[]{:S(2)}) collective-permute-start(bf16[2,512,128]{2,1,0:T(8,128)(2,1)S(1)} %pad_maximum_fusion), channel_id=1, source_target_pairs={{0,248},{8,240},{16,232},{24,224},{32,216},{40,208},{48,200},{56,1... | collective-permute-start | bytes 786440 | tf_op jit(solution)/shard_map/ppermute | solution.py:424
  30.6 0.7 copy-start.6
  30.9 0.7 copy-start.7
  37.1 6.8 %copy-start.12 = (bf16[512,256]{1,0:T(8,128)(2,1)S(1)}, bf16[512,256]{1,0:T(8,128)(2,1)}, u32[]{:S(2)}) copy-start(bf16[512,256]{1,0:T(8,128)(2,1)} %refs_4_.1) | copy-start | bytes 786436
  37.2 6.8 %copy-start.13 = (bf16[512,256]{1,0:T(8,128)(2,1)S(1)}, bf16[512,256]{1,0:T(8,128)(2,1)}, u32[]{:S(2)}) copy-start(bf16[512,256]{1,0:T(8,128)(2,1)} %refs_3_.1) | copy-start | bytes 786436
  37.2 40.7 %all-to-all-start.1 = ((bf16[32,4,64,128]{3,2,1,0:T(8,128)(2,1)}), bf16[32,4,64,128]{3,2,1,0:T(8,128)(2,1)S(1)}, u32[]{:S(2)}, u32[]{:S(2)}) async-start(bf16[32,4,64,128]{3,2,1,0:T(8,128)(2,1)} %get-tuple-element.24), calls=%async_computation.1 | async-start | bytes 4194304 | tf_op jit(solution)/shard_map/all_to_all | solution.py:428
  44.1 33.8 %collective-permute-start.1 = (bf16[2,512,128]{2,1,0:T(8,128)(2,1)S(1)}, bf16[2,512,128]{2,1,0:T(8,128)(2,1)S(1)}, u32[]{:S(2)}, u32[]{:S(2)}) collective-permute-start(bf16[2,512,128]{2,1,0:T(8,128)(2,1)S(1)} %pad_maximum_fusion.1), channel_id=1, source_target_pairs={{0,248},{8,240},{16,232},{24,224},{32,216},{40,208},{48,200},{56,1... | collective-permute-start | bytes 786440 | tf_op jit(solution)/shard_map/ppermute | solution.py:424
  77.9 0.7 copy-start.14
  77.9 1.4 copy-start.5
  100.0 4.6 %copy-start.10 = (bf16[512,128]{1,0:T(8,128)(2,1)S(1)}, bf16[512,128]{1,0:T(8,128)(2,1)}, u32[]{:S(2)}) copy-start(bf16[512,128]{1,0:T(8,128)(2,1)} %get-tuple-element.27) | copy-start | bytes 393220
  100.0 4.6 %copy-start.11 = (bf16[512,128]{1,0:T(8,128)(2,1)S(1)}, bf16[512,128]{1,0:T(8,128)(2,1)}, u32[]{:S(2)}) copy-start(bf16[512,128]{1,0:T(8,128)(2,1)} %get-tuple-element.28) | copy-start | bytes 393220
  100.0 33.1 %copy-start = (f32[512,128]{1,0:T(8,128)S(1)}, f32[512,128]{1,0:T(8,128)}, u32[]{:S(2)}) copy-start(f32[512,128]{1,0:T(8,128)} %get-tuple-element.32.refs_2_) | copy-start | bytes 786436
  100.0 33.1 %copy-start.1 = (f32[512,128]{1,0:T(8,128)S(1)}, f32[512,128]{1,0:T(8,128)}, u32[]{:S(2)}) copy-start(f32[512,128]{1,0:T(8,128)} %get-tuple-element.33.refs_3_) | copy-start | bytes 786436
  100.0 33.1 %copy-start.2 = (f32[512,128]{1,0:T(8,128)S(1)}, f32[512,128]{1,0:T(8,128)}, u32[]{:S(2)}) copy-start(f32[512,128]{1,0:T(8,128)} %get-tuple-element.30.refs_0_) | copy-start | bytes 786436
  100.1 33.1 %copy-start.3 = (f32[512,128]{1,0:T(8,128)S(1)}, f32[512,128]{1,0:T(8,128)}, u32[]{:S(2)}) copy-start(f32[512,128]{1,0:T(8,128)} %get-tuple-element.31.refs_1_) | copy-start | bytes 786436
  100.1 33.1 %copy-start.4 = (s32[136,32]{1,0:T(8,128)S(1)}, s32[136,32]{1,0:T(8,128)}, u32[]{:S(2)}) copy-start(s32[136,32]{1,0:T(8,128)} %get-tuple-element.22.refs_1_.table_ref) | copy-start | bytes 52228
  100.1 33.0 %all-to-all-start.2 = ((bf16[32,4,64,128]{3,2,1,0:T(8,128)(2,1)}), bf16[32,4,64,128]{3,2,1,0:T(8,128)(2,1)S(1)}, u32[]{:S(2)}, u32[]{:S(2)}) async-start(bf16[32,4,64,128]{3,2,1,0:T(8,128)(2,1)} %get-tuple-element.34), calls=%async_computation.2 | async-start | bytes 4194304 | tf_op jit(solution)/shard_map/all_to_all | solution.py:428
  105.3 33.3 %collective-permute-start.2 = (bf16[2,512,128]{2,1,0:T(8,128)(2,1)}, bf16[2,512,128]{2,1,0:T(8,128)(2,1)S(1)}, u32[]{:S(2)}, u32[]{:S(2)}) collective-permute-start(bf16[2,512,128]{2,1,0:T(8,128)(2,1)} %pad_maximum_fusion.2), channel_id=1, source_target_pairs={{0,248},{8,240},{16,232},{24,224},{32,216},{40,208},{48,200},{56,1... | collective-permute-start | bytes 786440 | tf_op jit(solution)/shard_map/ppermute | solution.py:424
  133.1 5.5 %copy-start.9 = (bf16[512,128]{1,0:T(8,128)(2,1)S(1)}, bf16[512,128]{1,0:T(8,128)(2,1)}, u32[]{:S(2)}) copy-start(bf16[512,128]{1,0:T(8,128)(2,1)} %get-tuple-element.29) | copy-start | bytes 393220
  133.1 6.2 %copy-start.8 = (bf16[512,128]{1,0:T(8,128)(2,1)S(1)}, bf16[512,128]{1,0:T(8,128)(2,1)}, u32[]{:S(2)}) copy-start(bf16[512,128]{1,0:T(8,128)(2,1)} %get-tuple-element.26) | copy-start | bytes 393220
  136.2 11.5 %collective-permute-start.3 = (bf16[2,512,128]{2,1,0:T(8,128)(2,1)S(1)}, bf16[2,512,128]{2,1,0:T(8,128)(2,1)S(1)}, u32[]{:S(2)}, u32[]{:S(2)}) collective-permute-start(bf16[2,512,128]{2,1,0:T(8,128)(2,1)S(1)} %get-tuple-element.36), channel_id=1, source_target_pairs={{0,248},{8,240},{16,232},{24,224},{32,216},{40,208},{48,200},{56,1... | collective-permute-start | bytes 786440 | tf_op jit(solution)/shard_map/ppermute | solution.py:456

commit v6 on v4

--- a/solution.py
+++ b/solution.py
@@ -11,6 +11,7 @@
 BLK = 64
 NSEQ = 32
 HD = 128
+FEAT = 256
 SEG = 512
 POOL = 32
 LOG2E = 1.4426950408889634
@@ -369,7 +370,7 @@
 
 def settle_kernel(where_ref, table_ref, *refs):
     locals_, back_ref = refs[:4], refs[4]
-    gk_ref, gv_ref, far_ref, acc = refs[5:]
+    gk_ref, gv_ref, fark_ref, farv_ref, acc = refs[5:]
     me = where_ref[0]
     part = pl.program_id(0)
     count = NSEQ // PARTS
@@ -399,9 +400,10 @@
 
     @pl.when(part == PARTS - 1)
     def _():
-        gk_ref[...] = acc[0].astype(jnp.bfloat16)
-        gv_ref[...] = acc[1].astype(jnp.bfloat16)
-        far_ref[...] = acc[2:4].astype(jnp.bfloat16)
+        gk_ref[:, :HD] = acc[0].astype(jnp.bfloat16)
+        gv_ref[:, :HD] = acc[1].astype(jnp.bfloat16)
+        fark_ref[...] = acc[2].astype(jnp.bfloat16)
+        farv_ref[...] = acc[3].astype(jnp.bfloat16)
 
 
 def settle(where, table, parts, back):
@@ -415,10 +417,10 @@
             grid=(PARTS,),
             in_specs=[whole(SEG, HD)] * 4
             + [pl.BlockSpec((NSEQ // PARTS, 4, BLK, HD), lambda i, *_: (i, 0, 0, 0))],
-            out_specs=[whole(SEG, HD)] * 2 + [whole(2, SEG, HD)],
+            out_specs=[whole(SEG, FEAT)] * 2 + [whole(SEG, HD)] * 2,
             scratch_shapes=[pltpu.VMEM((4, SEG, HD), f32)],
         ),
-        out_shape=[jax.ShapeDtypeStruct((SEG, HD), bf)] * 2 + [jax.ShapeDtypeStruct((2, SEG, HD), bf)],
+        out_shape=[jax.ShapeDtypeStruct((SEG, FEAT), bf)] * 2 + [jax.ShapeDtypeStruct((SEG, HD), bf)] * 2,
         compiler_params=pltpu.CompilerParams(vmem_limit_bytes=VMEM_SETTLE),
         cost_estimate=pl.CostEstimate(flops=2_000_000, bytes_accessed=3 << 20, transcendentals=0),
     )(where, table, *parts, back)
@@ -454,10 +456,11 @@
     attended = jnp.concatenate([att, home[0]], axis=1)
     grad_queries = jnp.concatenate([gq, home[1]], axis=1)
     back = exchange(back)
-    gk, gv, far = settle(where, table, (dkl, dvl, far_dkl, far_dvl), back)
-    far = lax.ppermute(far, "seq", [(i, NSEQ - 1 - i) for i in range(NSEQ)])
-    grad_keys = jnp.concatenate([gk, far[0]], axis=1)
-    grad_values = jnp.concatenate([gv, far[1]], axis=1)
+    gk, gv, far_gk, far_gv = settle(where, table, (dkl, dvl, far_dkl, far_dvl), back)
+    pairs = [(i, NSEQ - 1 - i) for i in range(NSEQ)]
+    far_gk, far_gv = (lax.ppermute(far, "seq", pairs) for far in (far_gk, far_gv))
+    grad_keys = lax.dynamic_update_slice(gk, far_gk, (0, HD))
+    grad_values = lax.dynamic_update_slice(gv, far_gv, (0, HD))
     return attended, grad_queries, grad_keys, grad_values
 
 

time: 146 us -> 151 us (1.034)
  starting transfers between devices: 44.3 us -> 47.1 us
  waiting for transfers between devices: 62 us -> 64.5 us
  other arithmetic: 4.5 us -> 2.31 us
    ppermute x3, waiting for transfers between devices: 25.5 us -> 54.2 us  [mirror(): return lax.ppermute(jnp.stack([first, second]), 'seq', pairs)]
    all_to_all x2, waiting for transfers between devices: 22.8 us -> 0.01 us  [exchange(): return lax.all_to_all(value, 'seq', split_axis=0, concat_axis=0, tiled=True)]
    ppermute x1 -> x2, waiting for transfers between devices: 7.64 us -> 4.2 us  [layer(): lax.ppermute(far, 'seq', pairs)]
    ppermute x1 -> x2, starting transfers between devices: 2.34 us -> 5.07 us  [layer(): lax.ppermute(far, 'seq', pairs)]
  transfers between devices with their start and end apart: 7 -> 8, of which waited for: 5 -> 6; matrix products, arithmetic and copies ran while one was open for 3% -> 3% of each run, Pallas kernels for 4% -> 2%
where the time goes in v6:
time: 151 us
  waiting for transfers between devices  64.5 us (43%)
  starting transfers between devices  47.1 us (31%)
  Pallas kernels  30 us (20%)
  local copies, waits for them, and re-layouts  5.93 us (4%)
  other arithmetic  2.31 us (2%)
    ppermute x3, waiting for transfers between devices, mirror(): return lax.ppermute(jnp.stack([first, second]), 'seq', pairs)  54.2 us
    pallas_call x1, Pallas kernels, attend(): pl.pallas_call(attend_kernel, name='attend', in_specs=[spec(sm)] * 3 + [s...  17.1 us
    all_to_all x1, starting transfers between devices, layer(): lax.all_to_all(copies, ('seq', 'head'), split_axis=0, concat_axis=0, tile...  15.6 us
    ppermute x3, starting transfers between devices, mirror(): return lax.ppermute(jnp.stack([first, second]), 'seq', pairs)  15.4 us
    all_to_all x2, starting transfers between devices, exchange(): return lax.all_to_all(value, 'seq', split_axis=0, concat_axis=0, tiled=True)  11 us
    all_to_all x1, waiting for transfers between devices, layer(): lax.all_to_all(copies, ('seq', 'head'), split_axis=0, concat_axis=0, tile...  6.04 us
    pallas_call x1, Pallas kernels, select(): pl.pallas_call(select_kernel, name='select', in_specs=[spec(pltpu.SMEM)]...  5.58 us
    ppermute x2, starting transfers between devices, layer(): lax.ppermute(far, 'seq', pairs)  5.07 us
  transfers between devices with their start and end apart: 8, of which 6 were waited for; matrix products, arithmetic and copies ran while one was open for 3% of the time, Pallas kernels for 2%

profile of v6, /device:TPU:1, one launch (start us, length us, event | category | flops | bytes accessed | tf_op | source)
XLA Modules:
  0.0 150.7 jit_solution(16769797398572027969)
XLA Ops:
  0.6 1.4 broadcast_in_dim.3
  2.0 15.6 %all-to-all-start = ((s32[256,1,16]{2,1,0:T(1,128)}), s32[256,1,16]{2,1,0:T(1,128)S(1)}, u32[]{:S(2)}, u32[]{:S(2)}) async-start(s32[256,1,16]{2,1,0:T(1,128)} %broadcast_in_dim.3), calls=%async_computation | async-start | bytes 262144 | tf_op jit(solution)/shard_map/all_to_all | solution.py:443
  17.7 1.0 slice_bitcast_fusion.4
  18.7 5.1 %collective-permute-start = (bf16[2,512,128]{2,1,0:T(8,128)(2,1)S(1)}, bf16[2,512,128]{2,1,0:T(8,128)(2,1)S(1)}, u32[]{:S(2)}, u32[]{:S(2)}) collective-permute-start(bf16[2,512,128]{2,1,0:T(8,128)(2,1)S(1)} %pad_maximum_fusion), channel_id=1, source_target_pairs={{0,248},{8,240},{16,232},{24,224},{32,216},{40,208},{48,200},{56,1... | collective-permute-start | bytes 786440 | tf_op jit(solution)/shard_map/ppermute | solution.py:431
  23.8 0.8 fusion.1
  24.6 6.0 %all-to-all-done = s32[256,1,16]{2,1,0:T(1,128)S(1)} async-done(((s32[256,1,16]{2,1,0:T(1,128)}), s32[256,1,16]{2,1,0:T(1,128)S(1)}, u32[]{:S(2)}, u32[]{:S(2)}) %all-to-all-start) | async-done | bytes 16416 | tf_op jit(solution)/shard_map/all_to_all | solution.py:443
  30.6 0.2 collective-permute-done.far_ref.refs_4_
  30.9 0.4 copy-done.6
  31.3 0.3 copy-done.7
  31.6 5.6 %select.1 = (s32[64,32]{1,0:T(8,128)}, bf16[32,4,64,128]{3,2,1,0:T(8,128)(2,1)}) custom-call(s32[1]{0:T(128)} %bitcast.where_ref, s32[256,16]{1,0:T(8,128)} %bitcast.17, bf16[256,256]{1,0:T(8,128)(2,1)} %get-tuple-element.43.upto8_ref, bf16[512,256]{1,0:T(8,128)(2,1)} %refs_2_.1, bf16[512,256]{1,0:T(8,128)(2,1)} %refs_3_.1, bf16[2,512,128]{2,1,0:T(8,128)(2,1)} %copy-done.7), custom_call_target="tpu_custom_call" | custom-call | flops 10000000 | bytes 4194304 | tf_op jit(solution)/shard_map/select/pallas_call | solution.py:102
  37.1 0.0 copy-start.12
  37.2 6.8 %all-to-all-start.1 = ((bf16[32,4,64,128]{3,2,1,0:T(8,128)(2,1)}), bf16[32,4,64,128]{3,2,1,0:T(8,128)(2,1)S(1)}, u32[]{:S(2)}, u32[]{:S(2)}) async-start(bf16[32,4,64,128]{3,2,1,0:T(8,128)(2,1)} %get-tuple-element.24), calls=%async_computation.1 | async-start | bytes 4194304 | tf_op jit(solution)/shard_map/all_to_all | solution.py:435
  44.0 5.1 %collective-permute-start.1 = (bf16[2,512,128]{2,1,0:T(8,128)(2,1)S(1)}, bf16[2,512,128]{2,1,0:T(8,128)(2,1)S(1)}, u32[]{:S(2)}, u32[]{:S(2)}) collective-permute-start(bf16[2,512,128]{2,1,0:T(8,128)(2,1)S(1)} %pad_maximum_fusion.1), channel_id=1, source_target_pairs={{0,248},{8,240},{16,232},{24,224},{32,216},{40,208},{48,200},{56,1... | collective-permute-start | bytes 786440 | tf_op jit(solution)/shard_map/ppermute | solution.py:431
  49.2 3.4 %prep.1 = (s32[136,32]{1,0:T(8,128)}, f32[2,32,512]{2,1,0:T(8,128)}) custom-call(s32[1]{0:T(128)} %bitcast.where_ref, s32[256,16]{1,0:T(8,128)} %bitcast.18, bf16[256,256]{1,0:T(8,128)(2,1)} %get-tuple-element.42.upto_ref, bf16[256,256]{1,0:T(8,128)(2,1)} %get-tuple-element.43.upto8_ref, s32[64,32]{1,0:T(8,128)} %get-tuple-element.21.blocks_ref), custom_call_target="tpu_custom_call" | custom-call | flops 10000000 | bytes 1048576 | tf_op jit(solution)/shard_map/prep/pallas_call | solution.py:154
  52.5 25.3 %collective-permute-done.1.refs_5_ = bf16[2,512,128]{2,1,0:T(8,128)(2,1)S(1)} collective-permute-done((bf16[2,512,128]{2,1,0:T(8,128)(2,1)S(1)}, bf16[2,512,128]{2,1,0:T(8,128)(2,1)S(1)}, u32[]{:S(2)}, u32[]{:S(2)}) %collective-permute-start.1) | collective-permute-done | bytes 262176 | tf_op jit(solution)/shard_map/ppermute | solution.py:431
  77.9 0.7 copy-done.14
  78.6 0.7 copy-done.5
  79.3 17.1 %attend.1 = (bf16[512,128]{1,0:T(8,128)(2,1)}, bf16[512,128]{1,0:T(8,128)(2,1)}, f32[512,128]{1,0:T(8,128)}, f32[512,128]{1,0:T(8,128)}, bf16[512,128]{1,0:T(8,1...) custom-call(s32[1]{0:T(128)} %bitcast.where_ref, ...), custom_call_target="tpu_custom_call" | custom-call | flops 16000000000 | bytes 8388608 | tf_op jit(solution)/shard_map/attend/pallas_call | solution.py:348
  96.4 0.0 copy-start
  96.5 0.0 copy-start.1
  96.5 4.2 %all-to-all-start.2 = ((bf16[32,4,64,128]{3,2,1,0:T(8,128)(2,1)}), bf16[32,4,64,128]{3,2,1,0:T(8,128)(2,1)S(1)}, u32[]{:S(2)}, u32[]{:S(2)}) async-start(bf16[32,4,64,128]{3,2,1,0:T(8,128)(2,1)} %get-tuple-element.33), calls=%async_computation.2 | async-start | bytes 4194304 | tf_op jit(solution)/shard_map/all_to_all | solution.py:435
  100.8 5.1 %collective-permute-start.2 = (bf16[2,512,128]{2,1,0:T(8,128)(2,1)S(1)}, bf16[2,512,128]{2,1,0:T(8,128)(2,1)S(1)}, u32[]{:S(2)}, u32[]{:S(2)}) collective-permute-start(bf16[2,512,128]{2,1,0:T(8,128)(2,1)S(1)} %pad_maximum_fusion.2), channel_id=1, source_target_pairs={{0,248},{8,240},{16,232},{24,224},{32,216},{40,208},{48,200},{56,1... | collective-permute-start | bytes 786440 | tf_op jit(solution)/shard_map/ppermute | solution.py:431
  105.9 28.7 %collective-permute-done.2 = bf16[2,512,128]{2,1,0:T(8,128)(2,1)S(1)} collective-permute-done((bf16[2,512,128]{2,1,0:T(8,128)(2,1)S(1)}, bf16[2,512,128]{2,1,0:T(8,128)(2,1)S(1)}, u32[]{:S(2)}, u32[]{:S(2)}) %collective-permute-start.2) | collective-permute-done | bytes 262176 | tf_op jit(solution)/shard_map/ppermute | solution.py:431
  134.7 3.9 %settle.1 = (bf16[512,256]{1,0:T(8,128)(2,1)}, bf16[512,256]{1,0:T(8,128)(2,1)}, bf16[512,128]{1,0:T(8,128)(2,1)S(1)}, bf16[512,128]{1,0:T(8,128)(2,1)S(1)}) custom-call(s32[1]{0:T(128)} %bitcast.where_ref, s32[136,32]{1,0:T(8,128)S(1)} %copy-done.4, f32[512,128]{1,0:T(8,128)S(1)} %copy-done, f32[512,128]{1,0:T(8,128)S(1)} %copy-done.1, ...), custom_call_target="tpu_custom_call" | custom-call | flops 2000000 | bytes 3145728 | tf_op jit(solution)/shard_map/settle/pallas_call | solution.py:412
  138.6 1.9 %collective-permute-start.3 = (bf16[512,128]{1,0:T(8,128)(2,1)S(1)}, bf16[512,128]{1,0:T(8,128)(2,1)S(1)}, u32[]{:S(2)}, u32[]{:S(2)}) collective-permute-start(bf16[512,128]{1,0:T(8,128)(2,1)S(1)} %get-tuple-element.35), channel_id=1, source_target_pairs={{0,248},{8,240},{16,232},{24,224},{32,216},{40,208},{48,200},{56,1... | collective-permute-start | bytes 393224 | tf_op jit(solution)/shard_map/ppermute | solution.py:461
  140.5 0.7 pad_maximum_fusion.4
  141.2 3.2 %collective-permute-start.4 = (bf16[512,128]{1,0:T(8,128)(2,1)S(1)}, bf16[512,128]{1,0:T(8,128)(2,1)S(1)}, u32[]{:S(2)}, u32[]{:S(2)}) collective-permute-start(bf16[512,128]{1,0:T(8,128)(2,1)S(1)} %get-tuple-element.37), channel_id=1, source_target_pairs={{0,248},{8,240},{16,232},{24,224},{32,216},{40,208},{48,200},{56,1... | collective-permute-start | bytes 393224 | tf_op jit(solution)/shard_map/ppermute | solution.py:461
  144.4 0.7 pad_maximum_fusion.3
  145.2 2.7 %collective-permute-done.3 = bf16[512,128]{1,0:T(8,128)(2,1)S(1)} collective-permute-done((bf16[512,128]{1,0:T(8,128)(2,1)S(1)}, bf16[512,128]{1,0:T(8,128)(2,1)S(1)}, u32[]{:S(2)}, u32[]{:S(2)}) %collective-permute-start.3) | collective-permute-done | bytes 131104 | tf_op jit(solution)/shard_map/ppermute | solution.py:461
  147.9 0.7 constant_dynamic-update-slice_fusion.1
  148.6 1.5 collective-permute-done.4
  150.0 0.7 constant_dynamic-update-slice_fusion
  (31 shorter events, 0.2 us)
Async XLA Ops:
  2.0 28.6 %all-to-all-start = ((s32[256,1,16]{2,1,0:T(1,128)}), s32[256,1,16]{2,1,0:T(1,128)S(1)}, u32[]{:S(2)}, u32[]{:S(2)}) async-start(s32[256,1,16]{2,1,0:T(1,128)} %broadcast_in_dim.3), calls=%async_computation | async-start | bytes 262144 | tf_op jit(solution)/shard_map/all_to_all | solution.py:443
  18.7 12.2 %collective-permute-start = (bf16[2,512,128]{2,1,0:T(8,128)(2,1)S(1)}, bf16[2,512,128]{2,1,0:T(8,128)(2,1)S(1)}, u32[]{:S(2)}, u32[]{:S(2)}) collective-permute-start(bf16[2,512,128]{2,1,0:T(8,128)(2,1)S(1)} %pad_maximum_fusion), channel_id=1, source_target_pairs={{0,248},{8,240},{16,232},{24,224},{32,216},{40,208},{48,200},{56,1... | collective-permute-start | bytes 786440 | tf_op jit(solution)/shard_map/ppermute | solution.py:431
  30.6 0.7 copy-start.6
  30.9 0.7 copy-start.7
  37.1 6.8 %copy-start.12 = (bf16[512,256]{1,0:T(8,128)(2,1)S(1)}, bf16[512,256]{1,0:T(8,128)(2,1)}, u32[]{:S(2)}) copy-start(bf16[512,256]{1,0:T(8,128)(2,1)} %refs_0_.1) | copy-start | bytes 786436
  37.2 6.8 %copy-start.13 = (bf16[512,256]{1,0:T(8,128)(2,1)S(1)}, bf16[512,256]{1,0:T(8,128)(2,1)}, u32[]{:S(2)}) copy-start(bf16[512,256]{1,0:T(8,128)(2,1)} %refs_1_.1) | copy-start | bytes 786436
  37.2 40.7 %all-to-all-start.1 = ((bf16[32,4,64,128]{3,2,1,0:T(8,128)(2,1)}), bf16[32,4,64,128]{3,2,1,0:T(8,128)(2,1)S(1)}, u32[]{:S(2)}, u32[]{:S(2)}) async-start(bf16[32,4,64,128]{3,2,1,0:T(8,128)(2,1)} %get-tuple-element.24), calls=%async_computation.1 | async-start | bytes 4194304 | tf_op jit(solution)/shard_map/all_to_all | solution.py:435
  44.0 33.8 %collective-permute-start.1 = (bf16[2,512,128]{2,1,0:T(8,128)(2,1)S(1)}, bf16[2,512,128]{2,1,0:T(8,128)(2,1)S(1)}, u32[]{:S(2)}, u32[]{:S(2)}) collective-permute-start(bf16[2,512,128]{2,1,0:T(8,128)(2,1)S(1)} %pad_maximum_fusion.1), channel_id=1, source_target_pairs={{0,248},{8,240},{16,232},{24,224},{32,216},{40,208},{48,200},{56,1... | collective-permute-start | bytes 786440 | tf_op jit(solution)/shard_map/ppermute | solution.py:431
  77.9 0.7 copy-start.14
  77.9 1.4 copy-start.5
  96.4 4.3 %copy-start.10 = (bf16[512,128]{1,0:T(8,128)(2,1)S(1)}, bf16[512,128]{1,0:T(8,128)(2,1)}, u32[]{:S(2)}) copy-start(bf16[512,128]{1,0:T(8,128)(2,1)} %get-tuple-element.26) | copy-start | bytes 393220
  96.4 4.3 %copy-start.11 = (bf16[512,128]{1,0:T(8,128)(2,1)S(1)}, bf16[512,128]{1,0:T(8,128)(2,1)}, u32[]{:S(2)}) copy-start(bf16[512,128]{1,0:T(8,128)(2,1)} %get-tuple-element.27) | copy-start | bytes 393220
  96.4 38.2 %copy-start = (f32[512,128]{1,0:T(8,128)S(1)}, f32[512,128]{1,0:T(8,128)}, u32[]{:S(2)}) copy-start(f32[512,128]{1,0:T(8,128)} %get-tuple-element.29.refs_0_) | copy-start | bytes 786436
  96.5 38.2 %copy-start.1 = (f32[512,128]{1,0:T(8,128)S(1)}, f32[512,128]{1,0:T(8,128)}, u32[]{:S(2)}) copy-start(f32[512,128]{1,0:T(8,128)} %get-tuple-element.30.refs_1_) | copy-start | bytes 786436
  96.5 38.2 %copy-start.2 = (f32[512,128]{1,0:T(8,128)S(1)}, f32[512,128]{1,0:T(8,128)}, u32[]{:S(2)}) copy-start(f32[512,128]{1,0:T(8,128)} %get-tuple-element.31.refs_2_) | copy-start | bytes 786436
  96.5 38.2 %copy-start.3 = (f32[512,128]{1,0:T(8,128)S(1)}, f32[512,128]{1,0:T(8,128)}, u32[]{:S(2)}) copy-start(f32[512,128]{1,0:T(8,128)} %get-tuple-element.32.refs_3_) | copy-start | bytes 786436
  96.5 38.2 %copy-start.4 = (s32[136,32]{1,0:T(8,128)S(1)}, s32[136,32]{1,0:T(8,128)}, u32[]{:S(2)}) copy-start(s32[136,32]{1,0:T(8,128)} %get-tuple-element.22.table_ref) | copy-start | bytes 52228
  96.5 38.1 %all-to-all-start.2 = ((bf16[32,4,64,128]{3,2,1,0:T(8,128)(2,1)}), bf16[32,4,64,128]{3,2,1,0:T(8,128)(2,1)S(1)}, u32[]{:S(2)}, u32[]{:S(2)}) async-start(bf16[32,4,64,128]{3,2,1,0:T(8,128)(2,1)} %get-tuple-element.33), calls=%async_computation.2 | async-start | bytes 4194304 | tf_op jit(solution)/shard_map/all_to_all | solution.py:435
  100.8 33.8 %collective-permute-start.2 = (bf16[2,512,128]{2,1,0:T(8,128)(2,1)S(1)}, bf16[2,512,128]{2,1,0:T(8,128)(2,1)S(1)}, u32[]{:S(2)}, u32[]{:S(2)}) collective-permute-start(bf16[2,512,128]{2,1,0:T(8,128)(2,1)S(1)} %pad_maximum_fusion.2), channel_id=1, source_target_pairs={{0,248},{8,240},{16,232},{24,224},{32,216},{40,208},{48,200},{56,1... | collective-permute-start | bytes 786440 | tf_op jit(solution)/shard_map/ppermute | solution.py:431
  134.7 5.8 %copy-start.9 = (bf16[512,128]{1,0:T(8,128)(2,1)S(1)}, bf16[512,128]{1,0:T(8,128)(2,1)}, u32[]{:S(2)}) copy-start(bf16[512,128]{1,0:T(8,128)(2,1)} %get-tuple-element.28) | copy-start | bytes 393220
  134.7 9.8 %copy-start.8 = (bf16[512,128]{1,0:T(8,128)(2,1)S(1)}, bf16[512,128]{1,0:T(8,128)(2,1)}, u32[]{:S(2)}) copy-start(bf16[512,128]{1,0:T(8,128)(2,1)} %get-tuple-element.25) | copy-start | bytes 393220
  138.6 9.3 %collective-permute-start.3 = (bf16[512,128]{1,0:T(8,128)(2,1)S(1)}, bf16[512,128]{1,0:T(8,128)(2,1)S(1)}, u32[]{:S(2)}, u32[]{:S(2)}) collective-permute-start(bf16[512,128]{1,0:T(8,128)(2,1)S(1)} %get-tuple-element.35), channel_id=1, source_target_pairs={{0,248},{8,240},{16,232},{24,224},{32,216},{40,208},{48,200},{56,1... | collective-permute-start | bytes 393224 | tf_op jit(solution)/shard_map/ppermute | solution.py:461
  141.2 8.8 %collective-permute-start.4 = (bf16[512,128]{1,0:T(8,128)(2,1)S(1)}, bf16[512,128]{1,0:T(8,128)(2,1)S(1)}, u32[]{:S(2)}, u32[]{:S(2)}) collective-permute-start(bf16[512,128]{1,0:T(8,128)(2,1)S(1)} %get-tuple-element.37), channel_id=1, source_target_pairs={{0,248},{8,240},{16,232},{24,224},{32,216},{40,208},{48,200},{56,1... | collective-permute-start | bytes 393224 | tf_op jit(solution)/shard_map/ppermute | solution.py:461
